TPU v7x, 256 devices: a whole 4x4x8 slice. The times are simulated.
256 devices in a mesh: samp: 16 (over x, y), ind: 16 (over z, core).
Axes of the slice: x: 4, y: 4, z: 8, core: 2. Of those that a mesh axis runs over, the one named last changes fastest.
Arguments:
- points: bfloat16 [32768, 64], P('samp'), may hold values from -6 to 6
- centers: bfloat16 [65536, 64], P('ind'), may hold values from -6 to 6
- coeffs: bfloat16 [65536, 128], P('ind'), may hold values from -0.6 to 0.6
- targets: bfloat16 [32768, 128], P('samp'), may hold values from 0 to 1
- diag_inv: float32 [128, 512, 512], P('ind'), may hold values from -3 to 15
- low_left: bfloat16 [128, 512, 64], P('ind'), may hold values from -0.0014648438 to 0.0014648438
- low_right: bfloat16 [128, 512, 64], P('ind'), may hold values from -0.25 to 0.25
- decay_rates: float32 [128, 64], P('ind'), may hold values from 0.05 to 64
- block_ranks: int32 [128], P('ind'), may hold values from 16 to 64
Outputs:
- direction: float32 [65536, 128], P('ind')
All inputs are finite; a program needn't handle non-finite values.
Results may differ from a plain program's by a relative error of at most 0.0003.
Values may be sent and summed in bfloat16 or wider, within the bound.
No kernel may reach another device: no remote copies, remote signals or barrier semaphores. Data moves between devices by JAX's collectives and lax.ppermute only.
A program may use at most 128 MiB of HBM per device.

v0:
```python
import math

import jax
import jax.numpy as jnp
from jax import lax
from jax.sharding import Mesh
from jax.sharding import PartitionSpec as P

D = 64
B = 512
R = 64
NB = 128
IND = ("ind_0", "ind_1")


highest = lax.Precision.HIGHEST
ridge_weight = 0.1


def split_up(array, dim, count):
    before, after = (array.shape[:dim], array.shape[dim + 1 :])
    return jnp.moveaxis(array.reshape(*before, count, -1, *after), dim, 0)


def summed_on_arrival(array, axis, dim):
    pieces = split_up(array, dim, lax.axis_size(axis))
    arrived = lax.all_to_all(pieces, axis, split_axis=0, concat_axis=0, tiled=True)
    return arrived.sum(axis=0)


def gather_axes(array, axes, dim):
    whole = array
    for number in range(len(axes) - 1, -1, -1):
        whole = lax.all_gather(whole, axes[number], axis=dim, tiled=True)
    return whole


def sent_to_all(array, axis):
    copies = jnp.broadcast_to(array, (lax.axis_size(axis), *array.shape))
    return lax.all_to_all(copies, axis, split_axis=0, concat_axis=0, tiled=True)


def collected_together(array, axis):
    leaves = jax.tree.leaves(array)
    sequence = sorted(range(len(leaves)), key=lambda k: -leaves[k].size)
    width = (1, *leaves[sequence[0]].shape)[-1]
    lines = [
        jnp.pad(leaves[k].reshape(-1), (0, -leaves[k].size % width)).reshape(-1, width)
        for k in sequence
    ]
    both, at, found = (sent_to_all(jnp.concatenate(lines), axis), 0, {})
    for k, line in zip(sequence, lines):
        piece = both[:, at : at + len(line)].reshape(len(both), -1)
        found[k] = piece[:, : leaves[k].size].reshape(-1, *leaves[k].shape)
        at += len(line)
    numbers = iter(range(len(leaves)))
    return jax.tree.map(lambda _: found[next(numbers)], array)


def combined_pairwise(pieces, combine):
    while len(jax.tree.leaves(pieces)[0]) > 1:
        pieces = jax.vmap(combine)(
            *(jax.tree.map(lambda part: part[side::2], pieces) for side in (0, 1))
        )
    return jax.tree.map(lambda part: part[0], pieces)


def entering_2(array, axis, combine, identity):
    count, mine = (lax.axis_size(axis), lax.axis_index(axis))
    passed = jnp.arange(count) < mine

    def kept(part, zero, own):
        part = jnp.where(
            passed.reshape(-1, *(1 for _ in own.shape)),
            part.astype(own.dtype),
            jnp.asarray(zero, own.dtype),
        )
        return part

    pieces = collected_together(
        jax.tree.map(lambda part, kind: part.astype(kind), array, (jnp.bfloat16, jnp.bfloat16)),
        axis,
    )
    return combined_pairwise(jax.tree.map(kept, pieces, identity, array), combine)


def in_order(pieces, dim):
    pieces = jnp.moveaxis(pieces, 0, dim)
    lengths = pieces.shape
    return pieces.reshape(*lengths[:dim], lengths[dim] * lengths[dim + 1], *lengths[dim + 2 :])


def collect(array, axis, dim):
    pieces = sent_to_all(array, axis)
    return in_order(pieces, dim)


def kernel_tile(points, point_sq, center_block):
    center_sq = jnp.sum(jnp.square(center_block.astype(jnp.float32)), axis=1)
    cross_term = lax.dot_general(
        points, center_block, (((1,), (1,)), ((), ())), preferred_element_type=jnp.float32
    )
    distance = point_sq[:, None] + center_sq[None, :] - 2.0 * cross_term
    return jnp.exp(-(1.0 / D) * distance).astype(jnp.bfloat16)


def solve_step(state, inputs):
    inv_block, left_block, right_block, decay_block, grad_block = inputs
    rhs_block = grad_block - jnp.dot(left_block, state, precision=highest)
    solved = jnp.dot(inv_block, rhs_block, precision=highest)
    state = decay_block[:, None] * state + jnp.dot(right_block.T, solved, precision=highest)
    return (state, solved)


def summarize(carried, inputs):
    transfer, offset = carried
    inv_block, left_block, right_block, decay_block, grad_block = inputs
    projected = jnp.dot(right_block.T, inv_block, precision=highest)
    step_map = jnp.diag(decay_block) - jnp.dot(projected, left_block, precision=highest)
    transfer = jnp.dot(step_map, transfer, precision=highest)
    offset = jnp.dot(step_map, offset, precision=highest) + jnp.dot(
        projected, grad_block, precision=highest
    )
    return ((transfer, offset), None)


def compose(earlier, latter):
    return (
        jnp.dot(latter[0], earlier[0], precision=highest),
        jnp.dot(latter[0], earlier[1], precision=highest) + latter[1],
    )


def body(points, centers, coeffs, targets, diag_inv, low_left, low_right, decay_rates, block_ranks):
    sample_rows = points.shape[0]
    inducing_rows = centers.shape[0]
    label_count = coeffs.shape[1]
    block_width = 2 * B
    block_count = inducing_rows // block_width
    center_blocks = centers.reshape(block_count, block_width, D)
    coeff_blocks = coeffs.reshape(block_count, block_width, label_count)
    point_sq = jnp.sum(jnp.square(points.astype(jnp.float32)), axis=1)

    def predict_step(running, paired):
        kernel_part = kernel_tile(points, point_sq, paired[0])
        running = running + jnp.dot(kernel_part, paired[1], preferred_element_type=jnp.float32)
        return (running, kernel_part)

    partial_value, stored = lax.scan(
        predict_step,
        jnp.zeros((sample_rows, label_count), jnp.float32),
        (center_blocks, coeff_blocks),
    )
    pred_part = summed_on_arrival(partial_value, IND, 0)
    share_rows = pred_part.shape[0]
    own_targets = lax.dynamic_slice_in_dim(targets, lax.axis_index(IND) * share_rows, share_rows, 0)
    resid_part = (jax.nn.sigmoid(pred_part) - own_targets.astype(jnp.float32)).astype(jnp.bfloat16)
    residual = gather_axes(resid_part, IND, 0)

    def gradient_piece(kernel_part):
        return lax.dot_general(
            kernel_part, residual, (((0,), (0,)), ((), ())), preferred_element_type=jnp.float32
        )

    pieces = lax.map(gradient_piece, stored).reshape(inducing_rows, label_count)
    scaling = 1.0 / math.sqrt(sample_rows * lax.axis_size("samp"))
    summed = summed_on_arrival(pieces, "samp", 1)
    part_cols = summed.shape[1]
    own_coeffs = lax.dynamic_slice_in_dim(coeffs, lax.axis_index("samp") * part_cols, part_cols, 1)
    gradient = summed * scaling + ridge_weight * own_coeffs.astype(jnp.float32)
    local_blocks = inducing_rows // B
    rank_mask = (jnp.arange(R)[None, :] < block_ranks[:, None]).astype(jnp.float32)
    left_masked = low_left.astype(jnp.float32) * rank_mask[:, None, :]
    right_masked = low_right.astype(jnp.float32) * rank_mask[:, None, :]
    decays = jnp.exp(-decay_rates / NB)
    grad_blocks = gradient.reshape(local_blocks, B, part_cols)
    inputs = (diag_inv, left_masked, right_masked, decays, grad_blocks)
    identity_map = jnp.eye(R, dtype=jnp.float32)
    empty_state = jnp.zeros((R, part_cols), jnp.float32)
    (transfer, offset), _ = lax.scan(summarize, (identity_map, empty_state), inputs)
    before = entering_2((transfer, offset), IND, compose, (identity_map, empty_state))
    entering = before[1]
    _, solved = lax.scan(solve_step, entering, inputs)
    direction = solved.reshape(inducing_rows, part_cols)
    direction = collect(direction, "samp", 1)
    return direction


def solution(mesh):
    finer = Mesh(mesh.devices.reshape(mesh.shape["samp"], 8, 2), ("samp", "ind_0", "ind_1"))
    placed = (
        P("samp", None),
        P(IND, None),
        P(IND, None),
        P("samp", None),
        P(IND, None, None),
        P(IND, None, None),
        P(IND, None, None),
        P(IND, None),
        P(IND),
    )
    return jax.shard_map(body, mesh=finer, in_specs=placed, out_specs=P(IND, None), check_vma=False)
```

profile of v0, /device:TPU:1, one launch (start us, length us, event | category | flops | bytes accessed | tf_op | source)
XLA Modules:
  0.0 294.5 jit_solution(416423194468268933)
XLA Ops:
  0.0 1.5 copy.39
  2.6 41.1 %while.50 = (s32[]{:T(128)}, f32[2048,128]{1,0:T(8,128)}, bf16[4,2048,1024]{1,2,0:T(8,128)(2,1)}, f32[2048]{0:T(1024)S(1)}, bf16[4,1024,64]{2,1,0:T(8,128)(2,1)S...) while((s32[]{:T(128)}, f32[2048,128]{1,0:T(8,128)}, ...), condition=%wide.region_3.4_spmd.clone, body=%wide.region_1.3_spmd.clone.sunk | while | flops 816512000 | bytes 15615595 | solution.py:149
  2.8 5.4 %bitcast_dynamic-update-slice_fusion.5 = (bf16[4,2048,1024]{1,2,0:T(8,128)(2,1)}, bf16[2048,1024]{0,1:T(8,128)(2,1)}) fusion(bf16[4,2048,1024]{1,2,0:T(8,128)(2,1)} %get-tuple-element.468, s32[]{:T(128)} %get-tuple-element.466, bf16[2048,64]{0,1:T(8,128)(2,1)} %get-tuple-element.480, bf16[4,1024,64]{2,1,0:T(8,128)(2,1)S(1)} %get-tuple-element.479, ...), kind=kOutput, calls=%fused_computation.24.clone.1 | convolution fusion | flops 278921216 | bytes 8926208 | tf_op jit(solution)/shard_map/while/body/eval_jaxpr/dot_general | solution.py:100
  8.2 4.5 %convolution_add_fusion.10 = f32[2048,128]{1,0:T(8,128)} fusion(bf16[2048,1024]{0,1:T(8,128)(2,1)} %get-tuple-element.447, f32[2048,128]{1,0:T(8,128)} %get-tuple-element.467, pred[]{:T(512)S(6)} %compare.6, bf16[4,1024,128]{2,1,0:T(8,128)(2,1)} %get-tuple-element.481, s32[]{:T(128)} %get-tuple-element.466), kind=kOutput, calls=%fused_computation.25.clone.1 | convolution fusion | flops 537395200 | bytes 6554113 | tf_op jit(solution)/shard_map/while/body/eval_jaxpr/dot_general | solution.py:146
  12.9 5.3 %bitcast_dynamic-update-slice_fusion.5 = (bf16[4,2048,1024]{1,2,0:T(8,128)(2,1)}, bf16[2048,1024]{0,1:T(8,128)(2,1)}) fusion(bf16[4,2048,1024]{1,2,0:T(8,128)(2,1)} %get-tuple-element.468, s32[]{:T(128)} %get-tuple-element.466, bf16[2048,64]{0,1:T(8,128)(2,1)} %get-tuple-element.480, bf16[4,1024,64]{2,1,0:T(8,128)(2,1)S(1)} %get-tuple-element.479, ...), kind=kOutput, calls=%fused_computation.24.clone.1 | convolution fusion | flops 278921216 | bytes 8926208 | tf_op jit(solution)/shard_map/while/body/eval_jaxpr/dot_general | solution.py:100
  18.2 4.8 %convolution_add_fusion.10 = f32[2048,128]{1,0:T(8,128)} fusion(bf16[2048,1024]{0,1:T(8,128)(2,1)} %get-tuple-element.447, f32[2048,128]{1,0:T(8,128)} %get-tuple-element.467, pred[]{:T(512)S(6)} %compare.6, bf16[4,1024,128]{2,1,0:T(8,128)(2,1)} %get-tuple-element.481, s32[]{:T(128)} %get-tuple-element.466), kind=kOutput, calls=%fused_computation.25.clone.1 | convolution fusion | flops 537395200 | bytes 6554113 | tf_op jit(solution)/shard_map/while/body/eval_jaxpr/dot_general | solution.py:146
  23.2 5.3 %bitcast_dynamic-update-slice_fusion.5 = (bf16[4,2048,1024]{1,2,0:T(8,128)(2,1)}, bf16[2048,1024]{0,1:T(8,128)(2,1)}) fusion(bf16[4,2048,1024]{1,2,0:T(8,128)(2,1)} %get-tuple-element.468, s32[]{:T(128)} %get-tuple-element.466, bf16[2048,64]{0,1:T(8,128)(2,1)} %get-tuple-element.480, bf16[4,1024,64]{2,1,0:T(8,128)(2,1)S(1)} %get-tuple-element.479, ...), kind=kOutput, calls=%fused_computation.24.clone.1 | convolution fusion | flops 278921216 | bytes 8926208 | tf_op jit(solution)/shard_map/while/body/eval_jaxpr/dot_general | solution.py:100
  28.5 4.8 %convolution_add_fusion.10 = f32[2048,128]{1,0:T(8,128)} fusion(bf16[2048,1024]{0,1:T(8,128)(2,1)} %get-tuple-element.447, f32[2048,128]{1,0:T(8,128)} %get-tuple-element.467, pred[]{:T(512)S(6)} %compare.6, bf16[4,1024,128]{2,1,0:T(8,128)(2,1)} %get-tuple-element.481, s32[]{:T(128)} %get-tuple-element.466), kind=kOutput, calls=%fused_computation.25.clone.1 | convolution fusion | flops 537395200 | bytes 6554113 | tf_op jit(solution)/shard_map/while/body/eval_jaxpr/dot_general | solution.py:146
  33.6 5.3 %bitcast_dynamic-update-slice_fusion.5 = (bf16[4,2048,1024]{1,2,0:T(8,128)(2,1)}, bf16[2048,1024]{0,1:T(8,128)(2,1)}) fusion(bf16[4,2048,1024]{1,2,0:T(8,128)(2,1)} %get-tuple-element.468, s32[]{:T(128)} %get-tuple-element.466, bf16[2048,64]{0,1:T(8,128)(2,1)} %get-tuple-element.480, bf16[4,1024,64]{2,1,0:T(8,128)(2,1)S(1)} %get-tuple-element.479, ...), kind=kOutput, calls=%fused_computation.24.clone.1 | convolution fusion | flops 278921216 | bytes 8926208 | tf_op jit(solution)/shard_map/while/body/eval_jaxpr/dot_general | solution.py:100
  38.8 4.8 %convolution_add_fusion.10 = f32[2048,128]{1,0:T(8,128)} fusion(bf16[2048,1024]{0,1:T(8,128)(2,1)} %get-tuple-element.447, f32[2048,128]{1,0:T(8,128)} %get-tuple-element.467, pred[]{:T(512)S(6)} %compare.6, bf16[4,1024,128]{2,1,0:T(8,128)(2,1)} %get-tuple-element.481, s32[]{:T(128)} %get-tuple-element.466), kind=kOutput, calls=%fused_computation.25.clone.1 | convolution fusion | flops 537395200 | bytes 6554113 | tf_op jit(solution)/shard_map/while/body/eval_jaxpr/dot_general | solution.py:146
  43.7 10.0 %all-to-all-start = ((f32[16,128,128]{2,1,0:T(8,128)}), f32[16,128,128]{2,1,0:T(8,128)S(1)}, u32[]{:S(2)}, u32[]{:S(2)}) async-start(f32[16,128,128]{2,1,0:T(8,128)} %bitcast.10), calls=%async_computation | async-start | bytes 2097152 | tf_op jit(solution)/shard_map/all_to_all | solution.py:27
  53.6 28.0 %all-to-all-done = f32[16,128,128]{2,1,0:T(8,128)S(1)} async-done(((f32[16,128,128]{2,1,0:T(8,128)}), f32[16,128,128]{2,1,0:T(8,128)S(1)}, u32[]{:S(2)}, u32[]{:S(2)}) %all-to-all-start) | async-done | bytes 1048608 | tf_op jit(solution)/shard_map/all_to_all | solution.py:27
  82.5 1.9 all_gather.6
  84.3 21.8 %all_gather.7 = bf16[2048,128]{1,0:T(8,128)(2,1)} all-gather(bf16[256,128]{1,0:T(8,128)(2,1)S(1)} %all_gather.6), channel_id=1, replica_groups=mesh['samp'=16,'ind_0'=8,'ind_1'=2] {'ind_0'}, dimensions={0}, use_global_device_ids=true | all-gather | bytes 589824 | tf_op jit(solution)/shard_map/all_gather | solution.py:34
  106.1 32.5 %while.48 = (s32[]{:T(128)}, f32[4,1024,128]{1,0,2:T(4,128)S(1)}, bf16[4,2048,1024]{1,2,0:T(8,128)(2,1)}, bf16[2048,128]{1,0:T(8,128)(2,1)}, s32[]{:T(128)}, /*index=5*/s32[]{:T(128)}) while((s32[]{:T(128)}, f32[4,1024,128]{1,0,2:T(4,128)S(1)}, bf16[4,2048,1024]{1,2,0:T(8,128)(2,1)}, bf16[2048,128]{1,0:T(8,128)(2,1)}, s32[]{:T(128)}, ...), condition=%wide.region_6.7_spmd, body=%wide.region_5.6_spmd.sunk | while | flops 536870912 | bytes 7340617 | solution.py:165
  106.1 3.5 %fusion.104 = f32[1,1024,128]{2,1,0:T(8,128)S(1)} fusion(bf16[2048,128]{1,0:T(8,128)(2,1)} %get-tuple-element.499, bf16[4,2048,1024]{1,2,0:T(8,128)(2,1)} %get-tuple-element.498, s32[]{:T(128)} %get-tuple-element.490), kind=kOutput, calls=%fused_computation.3.clone.1 | convolution fusion | flops 536870912 | bytes 5243392 | tf_op jit(solution)/shard_map/while/body/eval_jaxpr/dot_general | solution.py:161
  110.1 4.1 %dynamic_update_slice.18 = f32[4,1024,128]{1,0,2:T(4,128)S(1)} dynamic-update-slice(f32[4,1024,128]{1,0,2:T(4,128)S(1)} %get-tuple-element.491, f32[1,1024,128]{1,0,2:T(1,128)S(1)} %copy.60, s32[]{:T(128)} %get-tuple-element.490, s32[]{:T(128)} %constant.58.clone.1..sunk, s32[]{:T(128)} %constant.58.clone.1..sunk) | dynamic-update-slice | bytes 1048580 | tf_op jit(solution)/shard_map/while/body/jit(dynamic_update_index_in_dim)/dynamic_update_slice | solution.py:165
  114.2 3.6 %fusion.104 = f32[1,1024,128]{2,1,0:T(8,128)S(1)} fusion(bf16[2048,128]{1,0:T(8,128)(2,1)} %get-tuple-element.499, bf16[4,2048,1024]{1,2,0:T(8,128)(2,1)} %get-tuple-element.498, s32[]{:T(128)} %get-tuple-element.490), kind=kOutput, calls=%fused_computation.3.clone.1 | convolution fusion | flops 536870912 | bytes 5243392 | tf_op jit(solution)/shard_map/while/body/eval_jaxpr/dot_general | solution.py:161
  118.2 4.1 %dynamic_update_slice.18 = f32[4,1024,128]{1,0,2:T(4,128)S(1)} dynamic-update-slice(f32[4,1024,128]{1,0,2:T(4,128)S(1)} %get-tuple-element.491, f32[1,1024,128]{1,0,2:T(1,128)S(1)} %copy.60, s32[]{:T(128)} %get-tuple-element.490, s32[]{:T(128)} %constant.58.clone.1..sunk, s32[]{:T(128)} %constant.58.clone.1..sunk) | dynamic-update-slice | bytes 1048580 | tf_op jit(solution)/shard_map/while/body/jit(dynamic_update_index_in_dim)/dynamic_update_slice | solution.py:165
  122.4 3.6 %fusion.104 = f32[1,1024,128]{2,1,0:T(8,128)S(1)} fusion(bf16[2048,128]{1,0:T(8,128)(2,1)} %get-tuple-element.499, bf16[4,2048,1024]{1,2,0:T(8,128)(2,1)} %get-tuple-element.498, s32[]{:T(128)} %get-tuple-element.490), kind=kOutput, calls=%fused_computation.3.clone.1 | convolution fusion | flops 536870912 | bytes 5243392 | tf_op jit(solution)/shard_map/while/body/eval_jaxpr/dot_general | solution.py:161
  126.4 4.1 %dynamic_update_slice.18 = f32[4,1024,128]{1,0,2:T(4,128)S(1)} dynamic-update-slice(f32[4,1024,128]{1,0,2:T(4,128)S(1)} %get-tuple-element.491, f32[1,1024,128]{1,0,2:T(1,128)S(1)} %copy.60, s32[]{:T(128)} %get-tuple-element.490, s32[]{:T(128)} %constant.58.clone.1..sunk, s32[]{:T(128)} %constant.58.clone.1..sunk) | dynamic-update-slice | bytes 1048580 | tf_op jit(solution)/shard_map/while/body/jit(dynamic_update_index_in_dim)/dynamic_update_slice | solution.py:165
  130.5 3.6 %fusion.104 = f32[1,1024,128]{2,1,0:T(8,128)S(1)} fusion(bf16[2048,128]{1,0:T(8,128)(2,1)} %get-tuple-element.499, bf16[4,2048,1024]{1,2,0:T(8,128)(2,1)} %get-tuple-element.498, s32[]{:T(128)} %get-tuple-element.490), kind=kOutput, calls=%fused_computation.3.clone.1 | convolution fusion | flops 536870912 | bytes 5243392 | tf_op jit(solution)/shard_map/while/body/eval_jaxpr/dot_general | solution.py:161
  134.5 4.1 %dynamic_update_slice.18 = f32[4,1024,128]{1,0,2:T(4,128)S(1)} dynamic-update-slice(f32[4,1024,128]{1,0,2:T(4,128)S(1)} %get-tuple-element.491, f32[1,1024,128]{1,0,2:T(1,128)S(1)} %copy.60, s32[]{:T(128)} %get-tuple-element.490, s32[]{:T(128)} %constant.58.clone.1..sunk, s32[]{:T(128)} %constant.58.clone.1..sunk) | dynamic-update-slice | bytes 1048580 | tf_op jit(solution)/shard_map/while/body/jit(dynamic_update_index_in_dim)/dynamic_update_slice | solution.py:165
  138.7 2.5 reshape_reshape.4
  141.1 6.8 %all-to-all-start.1 = ((f32[16,4096,8]{1,2,0:T(8,128)}), f32[16,4096,8]{1,2,0:T(8,128)}, u32[]{:S(2)}, u32[]{:S(2)}) async-start(f32[16,4096,8]{1,2,0:T(8,128)} %bitcast.11), calls=%async_computation.1 | async-start | bytes 4194304 | tf_op jit(solution)/shard_map/all_to_all | solution.py:27
  148.7 1.5 copy.37
  150.2 2.4 copy.38
  152.7 3.0 %convert_multiply_fusion = (f32[8,512,64]{2,1,0:T(8,128)}, f32[8,512,64]{2,1,0:T(8,128)S(1)}) fusion(bf16[8,512,64]{2,1,0:T(8,128)(2,1)} %copy.38, f32[8,64]{1,0:T(8,128)S(1)} %fusion.62, bf16[8,512,64]{2,1,0:T(8,128)(2,1)S(1)} %copy.37), kind=kLoop, calls=%fused_computation.55 | loop fusion | flops 1048576 | bytes 3147776 | tf_op jit(solution)/shard_map/mul | solution.py:173
  155.7 15.2 %all-to-all-done.1 = f32[16,4096,8]{1,2,0:T(8,128)} async-done(((f32[16,4096,8]{1,2,0:T(8,128)}), f32[16,4096,8]{1,2,0:T(8,128)}, u32[]{:S(2)}, u32[]{:S(2)}) %all-to-all-start.1) | async-done | bytes 2097184 | tf_op jit(solution)/shard_map/all_to_all | solution.py:27
  170.8 1.7 reduce_sum.38
  172.6 30.3 %while.51 = (s32[]{:T(128)}, f32[64,64]{1,0:T(8,128)S(1)}, f32[64,8]{0,1:T(8,128)S(1)}, f32[8,64]{1,0:T(8,128)S(1)}, f32[8,512,64]{2,1,0:T(8,128)S(1)}, /*index=...) while((s32[]{:T(128)}, f32[64,64]{1,0:T(8,128)S(1)}, ...), condition=%wide.region_9.10_spmd.clone, body=%wide.region_8.9_spmd.clone.sunk | while | flops 233190400 | bytes 2109815 | solution.py:180
  172.6 1.9 fusion.124
  174.5 1.2 convolution_subtract_fusion.5
  176.4 1.9 fusion.124
  180.2 1.9 fusion.124
  182.1 1.2 convolution_subtract_fusion.5
  183.9 1.9 fusion.124
  187.7 1.9 fusion.124
  189.7 1.2 convolution_subtract_fusion.5
  191.5 1.9 fusion.124
  195.3 1.9 fusion.124
  197.3 1.2 convolution_subtract_fusion.5
  199.1 1.9 fusion.124
  203.9 10.1 %all-to-all-start.2 = ((bf16[16,72,64]{1,2,0:T(8,128)(2,1)}), bf16[16,72,64]{1,2,0:T(8,128)(2,1)S(1)}, u32[]{:S(2)}, u32[]{:S(2)}) async-start(bf16[16,72,64]{1,2,0:T(8,128)(2,1)} %broadcast_in_dim.89), calls=%async_computation.2 | async-start | bytes 524288 | tf_op jit(solution)/shard_map/all_to_all | solution.py:40
  214.1 11.8 %all-to-all-done.2 = bf16[16,72,64]{1,2,0:T(8,128)(2,1)S(1)} async-done(((bf16[16,72,64]{1,2,0:T(8,128)(2,1)}), bf16[16,72,64]{1,2,0:T(8,128)(2,1)S(1)}, u32[]{:S(2)}, u32[]{:S(2)}) %all-to-all-start.2) | async-done | bytes 147488 | tf_op jit(solution)/shard_map/all_to_all | solution.py:40
  228.9 30.4 %while.49 = (s32[]{:T(128)}, f32[64,8]{0,1:T(8,128)S(1)}, f32[8,512,8]{1,2,0:T(8,128)S(1)}, f32[8,64]{1,0:T(8,128)S(1)}, f32[8,512,64]{2,1,0:T(8,128)S(1)}, /*in...) while((s32[]{:T(128)}, f32[64,8]{0,1:T(8,128)S(1)}, ...), condition=%wide.region_11.12_spmd, body=%wide.region_10.11_spmd.sunk | while | flops 31462400 | bytes 1682533 | solution.py:183
  228.9 1.3 convolution_subtract_fusion.4
  230.2 2.2 bitcast_dynamic-update-slice_fusion.4
  232.7 1.3 convolution_subtract_fusion.4
  234.0 2.2 bitcast_dynamic-update-slice_fusion.4
  236.5 1.3 convolution_subtract_fusion.4
  237.8 2.2 bitcast_dynamic-update-slice_fusion.4
  240.3 1.3 convolution_subtract_fusion.4
  241.6 2.2 bitcast_dynamic-update-slice_fusion.4
  244.1 1.3 convolution_subtract_fusion.4
  245.4 2.2 bitcast_dynamic-update-slice_fusion.4
  247.9 1.3 convolution_subtract_fusion.4
  249.2 2.2 bitcast_dynamic-update-slice_fusion.4
  251.7 1.3 convolution_subtract_fusion.4
  253.0 2.2 bitcast_dynamic-update-slice_fusion.4
  255.5 1.3 convolution_subtract_fusion.4
  256.8 2.2 bitcast_dynamic-update-slice_fusion.4
  259.5 33.2 %all_to_all.20 = f32[16,4096,8]{1,2,0:T(8,128)S(1)} all-to-all(f32[16,4096,8]{1,2,0:T(8,128)S(1)} %broadcast_in_dim.94), channel_id=1, replica_groups=mesh['samp'=16,'ind_0'=8,'ind_1'=2] {'samp'}, dimensions={0} | all-to-all | bytes 4194304 | tf_op jit(solution)/shard_map/all_to_all | solution.py:40
  292.7 1.8 copy.49
  (112 shorter events, 20.9 us)
Async XLA Ops:
  43.7 37.9 %all-to-all-start = ((f32[16,128,128]{2,1,0:T(8,128)}), f32[16,128,128]{2,1,0:T(8,128)S(1)}, u32[]{:S(2)}, u32[]{:S(2)}) async-start(f32[16,128,128]{2,1,0:T(8,128)} %bitcast.10), calls=%async_computation | async-start | bytes 2097152 | tf_op jit(solution)/shard_map/all_to_all | solution.py:27
  138.7 9.3 %copy-start = (bf16[4,1024,128]{2,1,0:T(8,128)(2,1)S(1)}, bf16[4,1024,128]{2,1,0:T(8,128)(2,1)}, u32[]{:S(2)}) copy-start(bf16[4,1024,128]{2,1,0:T(8,128)(2,1)} %get-tuple-element.562) | copy-start | bytes 3145732
  141.1 29.7 %all-to-all-start.1 = ((f32[16,4096,8]{1,2,0:T(8,128)}), f32[16,4096,8]{1,2,0:T(8,128)}, u32[]{:S(2)}, u32[]{:S(2)}) async-start(f32[16,4096,8]{1,2,0:T(8,128)} %bitcast.11), calls=%async_computation.1 | async-start | bytes 4194304 | tf_op jit(solution)/shard_map/all_to_all | solution.py:27
  148.0 4.6 %copy-start.2 = (s32[8]{0:T(128)S(1)}, s32[8]{0:T(128)}, u32[]{:S(2)}) copy-start(s32[8]{0:T(128)} %param.25) | copy-start | bytes 100
  148.0 4.7 %copy-start.1 = (f32[8,64]{1,0:T(8,128)S(1)}, f32[8,64]{1,0:T(8,128)}, u32[]{:S(2)}) copy-start(f32[8,64]{1,0:T(8,128)} %param.24) | copy-start | bytes 6148
  203.9 21.9 %all-to-all-start.2 = ((bf16[16,72,64]{1,2,0:T(8,128)(2,1)}), bf16[16,72,64]{1,2,0:T(8,128)(2,1)S(1)}, u32[]{:S(2)}, u32[]{:S(2)}) async-start(bf16[16,72,64]{1,2,0:T(8,128)(2,1)} %broadcast_in_dim.89), calls=%async_computation.2 | async-start | bytes 524288 | tf_op jit(solution)/shard_map/all_to_all | solution.py:40
where the time goes:
time: 296 us; the launch traced here: 294 us
  matrix products  116 us (39%)
  blocking collectives  56.8 us (19%)
  waiting for transfers between devices  54.9 us (19%)
  local copies, waits for them, and re-layouts  30.8 us (10%)
  starting transfers between devices  26.9 us (9%)
  other arithmetic  7.74 us (3%)
    all_to_all x2, waiting for transfers between devices, summed_on_arrival(): lax.all_to_all(pieces, axis, split_axis=0, concat_axis=0, tiled=True)  43.2 us
    all_to_all x1, blocking collectives, sent_to_all(): return lax.all_to_all(copies, axis, split_axis=0, concat_axis=0, tiled=True)  33.2 us
    all_gather x2, blocking collectives, gather_axes(): whole = lax.all_gather(whole, axes[number], axis=dim, tiled=True)  23.6 us
    dot_general x4, matrix products, kernel_tile(): lax.dot_general(points, center_block, (((1,), (1,)), ((), ())), preferred...  21.3 us
    dot_general x4, matrix products, predict_step(): jnp.dot(kernel_part, paired[1], preferred_element_type=jnp.float32)  18.9 us
    dynamic_update_slice x8, local copies, waits for them, and re-layouts, body(): pieces = lax.map(gradient_piece, stored).reshape(inducing_rows, label_count)  18.2 us
    dot_general x8, matrix products, solve_step(): solved = jnp.dot(inv_block, rhs_block, precision=highest)  17.8 us
    all_to_all x2, starting transfers between devices, summed_on_arrival(): lax.all_to_all(pieces, axis, split_axis=0, concat_axis=0, tiled=True)  16.8 us
  transfers between devices with their start and end apart: 3, of which 3 were waited for; matrix products, arithmetic and copies ran while one was open for 3% of the time, Pallas kernels for 0%

commit v1 on v0

v1 whole, which is shorter than its diff:
```python
import functools
import math

import jax
import jax.numpy as jnp
from jax import lax
from jax.experimental import pallas as pl
from jax.experimental.pallas import tpu as pltpu
from jax.sharding import PartitionSpec as P

D = 64
B = 512
R = 64
NB = 128
LOG2E = math.log2(math.e)

f32 = jnp.float32
bf16 = jnp.bfloat16
wire = jnp.float16
ridge_weight = 0.1
highest = lax.Precision.HIGHEST


def dot(a, b, ca, cb):
    return lax.dot_general(a, b, (((ca,), (cb,)), ((), ())), preferred_element_type=f32)


def split(a):
    high = a.astype(bf16)
    return high, (a - high.astype(f32)).astype(bf16)


def dot3(a, b, ca, cb):
    ah, al = split(a)
    bh, bl = split(b)
    return dot(ah, bh, ca, cb) + (dot(ah, bl, ca, cb) + dot(al, bh, ca, cb))


def predict_kernel(width, points_t, centers_t, coeffs, kernel_out, pred):
    x_t = points_t[...].astype(f32)
    x32 = x_t.T
    x = x32.astype(bf16)
    p = jnp.sum(x32 * x32, axis=1, keepdims=True) * (-LOG2E / D)
    total = None
    for at in range(0, centers_t.shape[1], width):
        c = centers_t[:, at : at + width]
        c32 = c.astype(f32)
        q = jnp.sum(c32 * c32, axis=0, keepdims=True) * (-LOG2E / D)
        exponent = dot(x, c, 1, 0) * (2 * LOG2E / D) + (p + q)
        k = jnp.exp2(exponent).astype(bf16)
        kernel_out[:, at : at + width] = k
        part = dot(k, coeffs[at : at + width, :], 1, 0)
        total = part if total is None else total + part
    pred[...] = total


def predict(points_t, centers_t, coeffs, rows=512, width=256):
    n, m, labels = points_t.shape[1], centers_t.shape[1], coeffs.shape[1]
    return pl.pallas_call(
        functools.partial(predict_kernel, width),
        grid=(n // rows,),
        in_specs=[
            pl.BlockSpec((D, rows), lambda i: (0, i)),
            pl.BlockSpec((D, m), lambda i: (0, 0)),
            pl.BlockSpec((m, labels), lambda i: (0, 0)),
        ],
        out_specs=[
            pl.BlockSpec((rows, m), lambda i: (i, 0)),
            pl.BlockSpec((rows, labels), lambda i: (i, 0)),
        ],
        out_shape=[
            jax.ShapeDtypeStruct((n, m), bf16),
            jax.ShapeDtypeStruct((n, labels), f32),
        ],
        compiler_params=pltpu.CompilerParams(vmem_limit_bytes=40 << 20),
        cost_estimate=pl.CostEstimate(
            flops=2 * n * m * (D + labels), bytes_accessed=2 * n * m, transcendentals=n * m
        ),
        name="predict",
    )(points_t, centers_t, coeffs)


def gradient_kernel(residual, kernel_cols, out, turned):
    @pl.when(pl.program_id(0) == 0)
    def _():
        turned[...] = residual[...].astype(f32).T.astype(bf16)

    out[...] = dot(turned[...], kernel_cols[...], 1, 0)


def gradient_t(residual, stored, cols=1024):
    n, labels = residual.shape
    m = stored.shape[1]
    return pl.pallas_call(
        gradient_kernel,
        grid=(m // cols,),
        in_specs=[
            pl.BlockSpec((n, labels), lambda i: (0, 0)),
            pl.BlockSpec((n, cols), lambda i: (0, i)),
        ],
        out_specs=pl.BlockSpec((labels, cols), lambda i: (0, i)),
        out_shape=jax.ShapeDtypeStruct((labels, m), f32),
        scratch_shapes=[pltpu.VMEM((labels, n), bf16)],
        compiler_params=pltpu.CompilerParams(vmem_limit_bytes=40 << 20),
        cost_estimate=pl.CostEstimate(
            flops=2 * n * m * labels, bytes_accessed=2 * n * m, transcendentals=0
        ),
        name="gradient",
    )(residual, stored)


def prepare_kernel(ranks, inverse, left_t, right_t, rates, proj, step, side, suffix_proj, transfer, acc):
    i = pl.program_id(0)
    k = pl.num_programs(0) - 1 - i
    eye = lax.broadcasted_iota(jnp.int32, (R, R), 0) == lax.broadcasted_iota(jnp.int32, (R, R), 1)

    @pl.when(i == 0)
    def _():
        acc[...] = eye.astype(f32)

    kept = lax.broadcasted_iota(jnp.int32, (R, B), 0) < ranks[k]
    left = jnp.where(kept, left_t[0].astype(f32), 0.0).astype(bf16)
    right = jnp.where(kept, right_t[0].astype(f32), 0.0).astype(bf16)
    high, low = split(inverse[0])
    p = dot(right, high, 1, 0) + dot(right, low, 1, 0)
    proj[...] = p
    side[...] = dot(left, high, 1, 1) + dot(left, low, 1, 1)
    ph, plow = split(p)
    decay = jnp.exp(rates[0] * (-1.0 / NB))
    a = jnp.where(eye, decay, 0.0) - (dot(ph, left, 1, 1) + dot(plow, left, 1, 1))
    step[0] = a
    suffix = acc[...]
    suffix_proj[...] = dot3(suffix, p, 1, 0)
    suffix = jnp.dot(suffix, a, precision=highest, preferred_element_type=f32)
    acc[...] = suffix
    transfer[...] = jnp.concatenate([suffix, jnp.zeros_like(suffix)], axis=1)


def prepare(block_ranks, diag_inv, left_t, right_t, rates):
    count = diag_inv.shape[0]
    back = lambda i, ranks: (count - 1 - i, 0, 0)
    wide = lambda i, ranks: (0, count - 1 - i)
    wide_shape = jax.ShapeDtypeStruct((R, count * B), f32)
    return pl.pallas_call(
        prepare_kernel,
        grid_spec=pltpu.PrefetchScalarGridSpec(
            num_scalar_prefetch=1,
            grid=(count,),
            in_specs=[
                pl.BlockSpec((1, B, B), back),
                pl.BlockSpec((1, R, B), back),
                pl.BlockSpec((1, R, B), back),
                pl.BlockSpec((1, 1, R), back),
            ],
            out_specs=[
                pl.BlockSpec((R, B), wide),
                pl.BlockSpec((1, R, R), back),
                pl.BlockSpec((R, B), wide),
                pl.BlockSpec((R, B), wide),
                pl.BlockSpec((R, 2 * R), lambda i, ranks: (0, 0)),
            ],
            scratch_shapes=[pltpu.VMEM((R, R), f32)],
        ),
        out_shape=[
            wide_shape,
            jax.ShapeDtypeStruct((count, R, R), f32),
            wide_shape,
            wide_shape,
            jax.ShapeDtypeStruct((R, 2 * R), f32),
        ],
        cost_estimate=pl.CostEstimate(
            flops=8 * count * R * B * B, bytes_accessed=6 * count * B * B, transcendentals=0
        ),
        name="prepare",
    )(block_ranks, diag_inv, left_t, right_t, rates[:, None, :])


def offset_kernel(grad, suffix_proj, out):
    found = dot3(grad[...], suffix_proj[...], 1, 1)
    out[...] = jnp.concatenate([found, jnp.zeros_like(found)], axis=1)


def offset_of(grad, suffix_proj):
    return pl.pallas_call(
        offset_kernel,
        out_shape=jax.ShapeDtypeStruct((grad.shape[0], 2 * R), f32),
        name="offset",
    )(grad, suffix_proj)


def local_kernel(grad, inverse, proj, solved, pushed):
    g = grad[...]
    gh = g.astype(bf16).astype(f32)
    gl = g - gh
    pair = jnp.concatenate([gh, gl]).astype(bf16)
    n = g.shape[0]

    def times(matrix):
        high, low = split(matrix)
        main = dot(pair, high, 1, 1)
        return (main[:n] + main[n:]) + dot(pair, low, 1, 1)[:n]

    solved[...] = times(inverse[0])
    pushed[0] = times(proj[...])


def local_solve(grad, diag_inv, proj):
    count = diag_inv.shape[0]
    labels = grad.shape[0]
    return pl.pallas_call(
        local_kernel,
        grid=(count,),
        in_specs=[
            pl.BlockSpec((labels, B), lambda i: (0, i)),
            pl.BlockSpec((1, B, B), lambda i: (i, 0, 0)),
            pl.BlockSpec((R, B), lambda i: (0, i)),
        ],
        out_specs=[
            pl.BlockSpec((labels, B), lambda i: (0, i)),
            pl.BlockSpec((1, labels, R), lambda i: (i, 0, 0)),
        ],
        out_shape=[
            jax.ShapeDtypeStruct((labels, count * B), f32),
            jax.ShapeDtypeStruct((count, labels, R), f32),
        ],
        cost_estimate=pl.CostEstimate(
            flops=6 * count * labels * B * B, bytes_accessed=4 * count * B * B, transcendentals=0
        ),
        name="local_solve",
    )(grad, diag_inv, proj)


def finish_kernel(entering, step, pushed, side, solved, out):
    state = entering[...]
    for k in range(step.shape[0]):
        cols = slice(k * B, (k + 1) * B)
        out[:, cols] = solved[:, cols] - dot3(state, side[:, cols], 1, 0)
        moved = lax.dot_general(
            state,
            step[k],
            (((1,), (1,)), ((), ())),
            precision=highest,
            preferred_element_type=f32,
        )
        state = moved + pushed[k]


def finish(entering, step, pushed, side, solved):
    return pl.pallas_call(
        finish_kernel,
        out_shape=jax.ShapeDtypeStruct(solved.shape, f32),
        name="finish",
    )(entering, step, pushed, side, solved)


def compose(earlier, latter):
    return (
        jnp.einsum("eij,ejk->eik", latter[0], earlier[0], precision=highest),
        jnp.einsum("elj,eij->eli", earlier[1], latter[0], precision=highest) + latter[1],
    )


def entering_state(transfers, offsets):
    count = transfers.shape[0]
    passed = (jnp.arange(count) < lax.axis_index("ind"))[:, None, None]
    pieces = (
        jnp.where(passed, transfers, jnp.eye(R, dtype=f32)),
        jnp.where(passed, offsets, 0.0),
    )
    while pieces[0].shape[0] > 1:
        pieces = compose(tuple(a[0::2] for a in pieces), tuple(a[1::2] for a in pieces))
    return pieces[1][0]


def sent_to_all(array, axis):
    copies = jnp.broadcast_to(array, (lax.axis_size(axis), *array.shape))
    return lax.all_to_all(copies, axis, split_axis=0, concat_axis=0, tiled=True)


def body(points, centers, coeffs, targets, diag_inv, low_left, low_right, decay_rates, block_ranks):
    n, labels = targets.shape
    m = centers.shape[0]
    ind, samp = lax.axis_size("ind"), lax.axis_size("samp")

    stored, pred = predict(points.T, centers.T, coeffs)
    arrived = lax.all_to_all(
        pred.astype(wire).reshape(ind, n // ind, labels), "ind", 0, 0, tiled=True
    )
    proj, step, side, suffix_proj, transfer = prepare(
        block_ranks,
        diag_inv,
        jnp.swapaxes(low_left, 1, 2),
        jnp.swapaxes(low_right, 1, 2),
        decay_rates,
    )
    pred_own = arrived.astype(f32).sum(axis=0)
    own_targets = lax.dynamic_slice_in_dim(targets, lax.axis_index("ind") * (n // ind), n // ind, 0)
    resid = (jax.nn.sigmoid(pred_own) - own_targets.astype(f32)).astype(bf16)
    residual = lax.all_gather(resid, "ind", axis=0, tiled=True)
    transfers = sent_to_all(transfer, "ind")[:, :, :R]

    partial = gradient_t(residual, stored)
    own = labels // samp
    arrived = lax.all_to_all(partial.astype(wire).reshape(samp, own, m), "samp", 0, 0, tiled=True)
    own_coeffs = lax.dynamic_slice_in_dim(coeffs, lax.axis_index("samp") * own, own, 1).T
    scaling = 1.0 / math.sqrt(n * samp)
    grad = arrived.astype(f32).sum(axis=0) * scaling + ridge_weight * own_coeffs.astype(f32)

    offsets = sent_to_all(offset_of(grad, suffix_proj), "ind")[:, :, :R]
    solved, pushed = local_solve(grad, diag_inv, proj)
    entering = entering_state(transfers, offsets)
    direction = finish(entering, step, pushed, side, solved)
    return sent_to_all(direction, "samp").reshape(labels, m).T


def solution(mesh):
    placed = (
        P("samp", None),
        P("ind", None),
        P("ind", None),
        P("samp", None),
        P("ind", None, None),
        P("ind", None, None),
        P("ind", None, None),
        P("ind", None),
        P("ind"),
    )
    return jax.shard_map(
        body, mesh=mesh, in_specs=placed, out_specs=P("ind", None), check_vma=False
    )
```

time: 296 us -> 170 us (0.57)
  matrix products: 116 us -> 2.6 us
  Pallas kernels: 0 us -> 45.6 us
  waiting for transfers between devices: 54.9 us -> 19.6 us
  local copies, waits for them, and re-layouts: 30.8 us -> 10.6 us
    dot_general x82 -> x6, matrix products: 116 us -> 2.45 us  [the longest x4 1.82 us: compose(): jnp.einsum('elj,eij->eli', earlier[1], latter[0], precision=highest)]
    pallas_call x0 -> x6, Pallas kernels: none -> 45.6 us  [the longest x1 12.5 us: predict(): pl.pallas_call(functools.partial(predict_kernel, width), grid=(n // rows,...]
    all_to_all x2, waiting for transfers between devices: 43.2 us -> 19.6 us  [the longest x1 13.5 us: body(): lax.all_to_all(partial.astype(wire).reshape(samp, own, m), 'samp', 0, 0,...]
    dynamic_update_slice x8 -> x0, local copies, waits for them, and re-layouts: 18.2 us -> none  [body(): pieces = lax.map(gradient_piece, stored).reshape(inducing_rows, label_count)]
    all_to_all x1 -> x2, waiting for transfers between devices: 11.8 us -> 0.01 us  [sent_to_all(): return lax.all_to_all(copies, axis, split_axis=0, concat_axis=0, tiled=True)]
    reduce_sum x7 -> x2, other arithmetic: 3.63 us -> 0.22 us  [the longest x1 0.14 us: body(): arrived.astype(f32).sum(axis=0) * scaling]
    all_to_all x1, blocking collectives: 33.2 us -> 30.1 us  [sent_to_all(): return lax.all_to_all(copies, axis, split_axis=0, concat_axis=0, tiled=True)]
    broadcast_in_dim x2 -> x3, local copies, waits for them, and re-layouts: 0.96 us -> 4.02 us  [sent_to_all(): copies = jnp.broadcast_to(array, (lax.axis_size(axis), *array.shape))]
  transfers between devices with their start and end apart: 3 -> 4, of which waited for: 3 -> 2; matrix products, arithmetic and copies ran while one was open for 3% -> 3% of each run, Pallas kernels for 0% -> 16%
where the time goes in v1:
time: 170 us; the launch traced here: 168 us
  blocking collectives  56 us (33%)
  Pallas kernels  45.6 us (27%)
  starting transfers between devices  28.8 us (17%)
  waiting for transfers between devices  19.6 us (12%)
  local copies, waits for them, and re-layouts  10.6 us (6%)
  other arithmetic  4.9 us (3%)
  matrix products  2.6 us (2%)
    all_to_all x1, blocking collectives, sent_to_all(): return lax.all_to_all(copies, axis, split_axis=0, concat_axis=0, tiled=True)  30.1 us
    all_gather x1, blocking collectives, body(): residual = lax.all_gather(resid, 'ind', axis=0, tiled=True)  26 us
    all_to_all x1, waiting for transfers between devices, body(): lax.all_to_all(partial.astype(wire).reshape(samp, own, m), 'samp', 0, 0,...  13.5 us
    pallas_call x1, Pallas kernels, predict(): pl.pallas_call(functools.partial(predict_kernel, width), grid=(n // rows,...  12.5 us
    all_to_all x2, starting transfers between devices, sent_to_all(): return lax.all_to_all(copies, axis, split_axis=0, concat_axis=0, tiled=True)  12.1 us
    pallas_call x1, Pallas kernels, prepare(): pl.pallas_call(prepare_kernel, grid_spec=pltpu.PrefetchScalarGridSpec(num...  11.1 us
    all_to_all x1, starting transfers between devices, body(): lax.all_to_all(pred.astype(wire).reshape(ind, n // ind, labels), 'ind', 0...  9.96 us
    pallas_call x1, Pallas kernels, local_solve(): pl.pallas_call(local_kernel, grid=(count,), in_specs=[pl.BlockSpec((label...  8.1 us
  transfers between devices with their start and end apart: 4, of which 2 were waited for; matrix products, arithmetic and copies ran while one was open for 3% of the time, Pallas kernels for 16%

profile of v1, /device:TPU:1, one launch (start us, length us, event | category | flops | bytes accessed | tf_op | source)
XLA Modules:
  0.0 168.2 jit_solution(4343322443436006821)
XLA Ops:
  0.0 0.0 copy-start
  0.0 1.2 copy-done
  1.2 0.0 copy-start.2
  1.2 1.0 copy-done.2
  2.3 0.0 copy-start.3
  2.3 0.9 copy-done.3
  3.2 12.5 %predict.1 = (bf16[2048,4096]{1,0:T(8,128)(2,1)}, f32[2048,128]{1,0:T(8,128)S(1)}) custom-call(bf16[64,2048]{1,0:T(8,128)(2,1)S(1)} %bitcast.28, bf16[64,4096]{1,0:T(8,128)(2,1)S(1)} %bitcast.27, bf16[4096,128]{1,0:T(8,128)(2,1)S(1)} %copy-done), custom_call_target="tpu_custom_call" | custom-call | flops 3221225472 | bytes 16777216 | tf_op jit(solution)/shard_map/predict/pallas_call | solution.py:59
  15.7 0.9 convert_element_type.25
  16.6 10.0 %all-to-all-start = ((f16[16,128,128]{2,1,0:T(8,128)(2,1)}), f16[16,128,128]{2,1,0:T(8,128)(2,1)S(1)}, u32[]{:S(2)}, u32[]{:S(2)}) async-start(f16[16,128,128]{2,1,0:T(8,128)(2,1)} %bitcast.2), calls=%async_computation | async-start | bytes 1048576 | tf_op jit(solution)/shard_map/all_to_all | solution.py:286
  26.5 11.1 %prepare.1 = (f32[64,4096]{1,0:T(8,128)}, f32[8,64,64]{2,1,0:T(8,128)}, f32[64,4096]{1,0:T(8,128)}, f32[64,4096]{1,0:T(8,128)}, f32[64,128]{1,0:T(8,128)}) custom-call(s32[8]{0:T(128)} %ranks.1, f32[8,512,512]{2,1,0:T(8,128)} %inverse.3, bf16[8,64,512]{2,1,0:T(8,128)(2,1)} %bitcast.30, bf16[8,64,512]{2,1,0:T(8,128)(2,1)} %bitcast.31, f32[8,1,64]{2,1,0:T(1,128)} %bitcast.32), custom_call_target="tpu_custom_call" | custom-call | flops 1073741824 | bytes 12582912 | tf_op jit(solution)/shard_map/prepare/pallas_call | solution.py:144
  37.7 6.1 %all-to-all-done = f16[16,128,128]{2,1,0:T(8,128)(2,1)S(1)} async-done(((f16[16,128,128]{2,1,0:T(8,128)(2,1)}), f16[16,128,128]{2,1,0:T(8,128)(2,1)S(1)}, u32[]{:S(2)}, u32[]{:S(2)}) %all-to-all-start) | async-done | bytes 524320 | tf_op jit(solution)/shard_map/all_to_all | solution.py:286
  43.7 1.6 broadcast_in_dim.42
  45.3 3.5 %all-to-all-start.3 = ((f32[16,64,128]{2,1,0:T(8,128)}), f32[16,64,128]{2,1,0:T(8,128)S(1)}, u32[]{:S(2)}, u32[]{:S(2)}) async-start(f32[16,64,128]{2,1,0:T(8,128)} %broadcast_in_dim.42), calls=%async_computation.3 | async-start | bytes 1048576 | tf_op jit(solution)/shard_map/all_to_all | solution.py:277
  48.8 0.1 convert_reduce_fusion.1
  48.9 0.8 subtract_convert_fusion
  49.7 26.0 %all_gather.3.residual = bf16[2048,128]{1,0:T(8,128)(2,1)S(1)} all-gather(bf16[128,128]{1,0:T(8,128)(2,1)S(1)} %subtract_convert_fusion), channel_id=1, replica_groups=mesh['samp'=16,'ind'=16] {'ind'}, dimensions={0}, use_global_device_ids=true | all-gather | bytes 557056 | tf_op jit(solution)/shard_map/all_gather | solution.py:299
  75.7 7.6 %gradient.1 = f32[128,4096]{1,0:T(8,128)S(1)} custom-call(bf16[2048,128]{1,0:T(8,128)(2,1)S(1)} %all_gather.3.residual, bf16[2048,4096]{1,0:T(8,128)(2,1)} %get-tuple-element.15.kernel_cols), custom_call_target="tpu_custom_call" | custom-call | flops 2147483648 | bytes 16777216 | tf_op jit(solution)/shard_map/gradient/pallas_call | solution.py:94
  83.2 0.0 copy-start.1
  83.2 1.1 convert_bitcast_fusion
  84.3 0.0 all-to-all-done.3
  84.3 0.0 copy-start.4
  84.3 0.8 copy-done.4
  85.2 6.8 %all-to-all-start.1 = ((f16[16,8,4096]{2,1,0:T(8,128)(2,1)}), f16[16,8,4096]{2,1,0:T(8,128)(2,1)S(1)}, u32[]{:S(2)}, u32[]{:S(2)}) async-start(f16[16,8,4096]{2,1,0:T(8,128)(2,1)} %convert_bitcast_fusion), calls=%async_computation.1 | async-start | bytes 2097152 | tf_op jit(solution)/shard_map/all_to_all | solution.py:304
  91.9 0.0 copy-done.1
  92.0 0.4 constant_dynamic-slice_fusion
  92.3 0.3 copy.14
  92.7 1.1 slice_select_fusion
  93.8 0.4 fusion.2
  94.2 0.3 fusion.6
  94.5 13.5 %all-to-all-done.1 = f16[16,8,4096]{2,1,0:T(8,128)(2,1)S(1)} async-done(((f16[16,8,4096]{2,1,0:T(8,128)(2,1)}), f16[16,8,4096]{2,1,0:T(8,128)(2,1)S(1)}, u32[]{:S(2)}, u32[]{:S(2)}) %all-to-all-start.1) | async-done | bytes 1048608 | tf_op jit(solution)/shard_map/all_to_all | solution.py:304
  107.9 0.1 convert_reduce_fusion
  108.1 0.7 bitcast_add_fusion.grad
  108.8 2.4 %offset.1 = f32[8,128]{1,0:T(8,128)} custom-call(f32[8,4096]{1,0:T(8,128)} %bitcast_add_fusion.grad, f32[64,4096]{1,0:T(8,128)} %get-tuple-element.16.suffix_proj), custom_call_target="tpu_custom_call" | custom-call | tf_op jit(solution)/shard_map/offset/pallas_call | solution.py:184
  111.2 1.3 broadcast_in_dim.39
  112.5 8.6 %all-to-all-start.2 = ((f32[16,8,128]{2,1,0:T(8,128)}), f32[16,8,128]{2,1,0:T(8,128)S(1)}, u32[]{:S(2)}, u32[]{:S(2)}) async-start(f32[16,8,128]{2,1,0:T(8,128)} %broadcast_in_dim.39), calls=%async_computation.2 | async-start | bytes 131072 | tf_op jit(solution)/shard_map/all_to_all | solution.py:277
  121.1 0.1 convolution_bitcast_fusion
  121.2 8.1 %local_solve.1 = (f32[8,4096]{1,0:T(8,128)}, f32[8,8,64]{2,1,0:T(8,128)}) custom-call(f32[8,4096]{1,0:T(8,128)} %bitcast_add_fusion.grad, f32[8,512,512]{2,1,0:T(8,128)} %inverse.3, f32[64,4096]{1,0:T(8,128)} %get-tuple-element.19.proj), custom_call_target="tpu_custom_call" | custom-call | flops 100663296 | bytes 8388608 | tf_op jit(solution)/shard_map/local_solve/pallas_call | solution.py:210
  129.3 0.0 all-to-all-done.2
  129.3 0.1 slice_select_fusion.1
  129.4 0.5 convolution_add_fusion
  129.9 0.3 convolution_add_fusion.1
  130.3 0.2 convolution_add_fusion.2
  130.5 0.8 fusion.1.entering
  131.3 3.9 %finish.1 = f32[8,4096]{1,0:T(8,128)} custom-call(f32[8,64]{1,0:T(8,128)} %fusion.1.entering, f32[8,64,64]{2,1,0:T(8,128)} %get-tuple-element.18.step, f32[8,8,64]{2,1,0:T(8,128)} %get-tuple-element.20.pushed, f32[64,4096]{1,0:T(8,128)} %get-tuple-element.21.side, f32[8,4096]{1,0:T(8,128)} %get-tuple-element.22.solved), custom_call_target="tpu_custom_call" | custom-call | tf_op jit(solution)/shard_map/finish/pallas_call | solution.py:249
  135.2 1.1 broadcast_in_dim.44
  136.3 30.1 %all_to_all.25 = f32[16,8,4096]{2,1,0:T(8,128)S(1)} all-to-all(f32[16,8,4096]{2,1,0:T(8,128)S(1)} %broadcast_in_dim.44), channel_id=1, replica_groups=mesh['samp'=16,'ind'=16] {'samp'}, dimensions={0} | all-to-all | bytes 4194304 | tf_op jit(solution)/shard_map/all_to_all | solution.py:277
  166.4 1.8 %copy.13 = f32[4096,128]{1,0:T(8,128)} copy(f32[4096,128]{0,1:T(8,128)S(1)} %bitcast.29) | data formatting | bytes 4194304 | tf_op jit(solution)/shard_map/transpose | solution.py:313
  (2 shorter events, 0.0 us)
Async XLA Ops:
  0.0 1.2 copy-start
  1.2 1.0 copy-start.2
  2.3 0.9 copy-start.3
  16.6 27.2 %all-to-all-start = ((f16[16,128,128]{2,1,0:T(8,128)(2,1)}), f16[16,128,128]{2,1,0:T(8,128)(2,1)S(1)}, u32[]{:S(2)}, u32[]{:S(2)}) async-start(f16[16,128,128]{2,1,0:T(8,128)(2,1)} %bitcast.2), calls=%async_computation | async-start | bytes 1048576 | tf_op jit(solution)/shard_map/all_to_all | solution.py:286
  45.3 39.0 %all-to-all-start.3 = ((f32[16,64,128]{2,1,0:T(8,128)}), f32[16,64,128]{2,1,0:T(8,128)S(1)}, u32[]{:S(2)}, u32[]{:S(2)}) async-start(f32[16,64,128]{2,1,0:T(8,128)} %broadcast_in_dim.42), calls=%async_computation.3 | async-start | bytes 1048576 | tf_op jit(solution)/shard_map/all_to_all | solution.py:277
  83.2 8.7 %copy-start.1 = (bf16[4096,128]{1,0:T(8,128)(2,1)S(1)}, bf16[4096,128]{1,0:T(8,128)(2,1)}, u32[]{:S(2)}) copy-start(bf16[4096,128]{1,0:T(8,128)(2,1)} %coeffs.1) | copy-start | bytes 3145732
  84.3 0.8 copy-start.4
  85.2 22.8 %all-to-all-start.1 = ((f16[16,8,4096]{2,1,0:T(8,128)(2,1)}), f16[16,8,4096]{2,1,0:T(8,128)(2,1)S(1)}, u32[]{:S(2)}, u32[]{:S(2)}) async-start(f16[16,8,4096]{2,1,0:T(8,128)(2,1)} %convert_bitcast_fusion), calls=%async_computation.1 | async-start | bytes 2097152 | tf_op jit(solution)/shard_map/all_to_all | solution.py:304
  112.5 16.8 %all-to-all-start.2 = ((f32[16,8,128]{2,1,0:T(8,128)}), f32[16,8,128]{2,1,0:T(8,128)S(1)}, u32[]{:S(2)}, u32[]{:S(2)}) async-start(f32[16,8,128]{2,1,0:T(8,128)} %broadcast_in_dim.39), calls=%async_computation.2 | async-start | bytes 131072 | tf_op jit(solution)/shard_map/all_to_all | solution.py:277

commit v2 on v1

v2 whole, which is shorter than its diff:
```python
import functools
import math

import jax
import jax.numpy as jnp
from jax import lax
from jax.experimental import pallas as pl
from jax.experimental.pallas import tpu as pltpu
from jax.sharding import Mesh
from jax.sharding import PartitionSpec as P

D = 64
B = 512
R = 64
NB = 128
LOG2E = math.log2(math.e)

f32 = jnp.float32
bf16 = jnp.bfloat16
wire = jnp.float16
ridge_weight = 0.1
highest = lax.Precision.HIGHEST


def dot(a, b, ca, cb):
    return lax.dot_general(a, b, (((ca,), (cb,)), ((), ())), preferred_element_type=f32)


def split(a):
    high = a.astype(bf16)
    return high, (a - high.astype(f32)).astype(bf16)


def dot3(a, b, ca, cb):
    ah, al = split(a)
    bh, bl = split(b)
    return dot(ah, bh, ca, cb) + (dot(ah, bl, ca, cb) + dot(al, bh, ca, cb))


def predict_kernel(width, half, points_t, centers_t, coeffs, kernel_out, pred):
    x_t = points_t[...].astype(f32)
    x32 = x_t.T
    x = x32.astype(bf16)
    p = jnp.sum(x32 * x32, axis=1, keepdims=True) * (-LOG2E / D)
    total = None
    for at in range(0, centers_t.shape[1], width):
        c = centers_t[:, at : at + width]
        c32 = c.astype(f32)
        q = jnp.sum(c32 * c32, axis=0, keepdims=True) * (-LOG2E / D)
        exponent = dot(x, c, 1, 0) * (2 * LOG2E / D) + (p + q)
        k = jnp.exp2(exponent).astype(bf16)
        kernel_out[:, at : at + width] = k
        part = dot(k, coeffs[at : at + width, :], 1, 0)
        total = part if total is None else total + part
    pred[...] = total


def predict(half, points_t, centers_t, coeffs, rows=512, width=256):
    n, m, labels = points_t.shape[1] // 2, centers_t.shape[1], coeffs.shape[1]
    steps = n // rows
    return pl.pallas_call(
        functools.partial(predict_kernel, width),
        grid_spec=pltpu.PrefetchScalarGridSpec(
            num_scalar_prefetch=1,
            grid=(steps,),
            in_specs=[
                pl.BlockSpec((D, rows), lambda i, half: (0, half[0] * steps + i)),
                pl.BlockSpec((D, m), lambda i, half: (0, 0)),
                pl.BlockSpec((m, labels), lambda i, half: (0, 0)),
            ],
            out_specs=[
                pl.BlockSpec((rows, m), lambda i, half: (i, 0)),
                pl.BlockSpec((rows, labels), lambda i, half: (i, 0)),
            ],
        ),
        out_shape=[
            jax.ShapeDtypeStruct((n, m), bf16),
            jax.ShapeDtypeStruct((n, labels), f32),
        ],
        compiler_params=pltpu.CompilerParams(vmem_limit_bytes=60 << 20),
        cost_estimate=pl.CostEstimate(
            flops=2 * n * m * (D + labels), bytes_accessed=2 * n * m, transcendentals=n * m
        ),
        name="predict",
    )(half.reshape(1), points_t, centers_t, coeffs)


def gradient_kernel(resid_a, resid_b, rows_a, rows_b, out, turned_a, turned_b):
    @pl.when(pl.program_id(0) == 0)
    def _():
        turned_a[...] = resid_a[...].astype(f32).T.astype(bf16)
        turned_b[...] = resid_b[...].astype(f32).T.astype(bf16)

    out[...] = dot(turned_a[...], rows_a[...], 1, 0) + dot(turned_b[...], rows_b[...], 1, 0)


def gradient_t(resid_a, resid_b, stored_a, stored_b, cols=1024):
    n, labels = resid_a.shape
    m = stored_a.shape[1]
    whole = pl.BlockSpec((n, labels), lambda i: (0, 0))
    part = pl.BlockSpec((n, cols), lambda i: (0, i))
    return pl.pallas_call(
        gradient_kernel,
        grid=(m // cols,),
        in_specs=[whole, whole, part, part],
        out_specs=pl.BlockSpec((labels, cols), lambda i: (0, i)),
        out_shape=jax.ShapeDtypeStruct((labels, m), f32),
        scratch_shapes=[pltpu.VMEM((labels, n), bf16)] * 2,
        compiler_params=pltpu.CompilerParams(vmem_limit_bytes=60 << 20),
        cost_estimate=pl.CostEstimate(
            flops=4 * n * m * labels, bytes_accessed=4 * n * m, transcendentals=0
        ),
        name="gradient",
    )(resid_a, resid_b, stored_a, stored_b)


def prepare_kernel(ranks, inverse, left_t, right_t, rates, proj, step, side, suffix_proj, transfer, acc):
    i = pl.program_id(0)
    k = pl.num_programs(0) - 1 - i
    eye = lax.broadcasted_iota(jnp.int32, (R, R), 0) == lax.broadcasted_iota(jnp.int32, (R, R), 1)

    @pl.when(i == 0)
    def _():
        acc[...] = eye.astype(f32)

    kept = lax.broadcasted_iota(jnp.int32, (R, B), 0) < ranks[k]
    left = jnp.where(kept, left_t[0].astype(f32), 0.0).astype(bf16)
    right = jnp.where(kept, right_t[0].astype(f32), 0.0).astype(bf16)
    high, low = split(inverse[0])
    p = dot(right, high, 1, 0) + dot(right, low, 1, 0)
    proj[...] = p
    side[...] = dot(left, high, 1, 1) + dot(left, low, 1, 1)
    ph, plow = split(p)
    decay = jnp.exp(rates[0] * (-1.0 / NB))
    a = jnp.where(eye, decay, 0.0) - (dot(ph, left, 1, 1) + dot(plow, left, 1, 1))
    step[0] = a
    suffix = acc[...]
    suffix_proj[...] = dot3(suffix, p, 1, 0)
    suffix = jnp.dot(suffix, a, precision=highest, preferred_element_type=f32)
    acc[...] = suffix
    transfer[...] = suffix


def prepare(block_ranks, diag_inv, left_t, right_t, rates):
    count = diag_inv.shape[0]
    back = lambda i, ranks: (count - 1 - i, 0, 0)
    wide = lambda i, ranks: (0, count - 1 - i)
    wide_shape = jax.ShapeDtypeStruct((R, count * B), f32)
    return pl.pallas_call(
        prepare_kernel,
        grid_spec=pltpu.PrefetchScalarGridSpec(
            num_scalar_prefetch=1,
            grid=(count,),
            in_specs=[
                pl.BlockSpec((1, B, B), back),
                pl.BlockSpec((1, R, B), back),
                pl.BlockSpec((1, R, B), back),
                pl.BlockSpec((1, 1, R), back),
            ],
            out_specs=[
                pl.BlockSpec((R, B), wide),
                pl.BlockSpec((1, R, R), back),
                pl.BlockSpec((R, B), wide),
                pl.BlockSpec((R, B), wide),
                pl.BlockSpec((R, R), lambda i, ranks: (0, 0)),
            ],
            scratch_shapes=[pltpu.VMEM((R, R), f32)],
        ),
        out_shape=[
            wide_shape,
            jax.ShapeDtypeStruct((count, R, R), f32),
            wide_shape,
            wide_shape,
            jax.ShapeDtypeStruct((R, R), f32),
        ],
        cost_estimate=pl.CostEstimate(
            flops=8 * count * R * B * B, bytes_accessed=6 * count * B * B, transcendentals=0
        ),
        name="prepare",
    )(block_ranks, diag_inv, left_t, right_t, rates[:, None, :])


def prefix_kernel(step, side, out):
    moved = None
    for k in range(step.shape[0]):
        cols = slice(k * B, (k + 1) * B)
        if moved is None:
            out[:, cols] = side[:, cols]
            moved = step[k].T
        else:
            out[:, cols] = dot3(moved, side[:, cols], 1, 0)
            if k + 1 < step.shape[0]:
                moved = dot3(moved, step[k], 1, 1)


def prefix_side(step, side):
    return pl.pallas_call(
        prefix_kernel,
        out_shape=jax.ShapeDtypeStruct(side.shape, f32),
        cost_estimate=pl.CostEstimate(
            flops=6 * R * side.size, bytes_accessed=8 * side.size, transcendentals=0
        ),
        name="prefix",
    )(step, side)


def offset_kernel(grad, suffix_proj, transfer, out):
    found = dot3(grad[...], suffix_proj[...], 1, 1)
    high = found.astype(bf16).astype(f32)
    t = transfer[...]
    rows = jnp.concatenate(
        [
            jnp.concatenate([t[: R // 2], t[R // 2 :]], axis=1),
            jnp.concatenate([high, found - high], axis=1),
            jnp.zeros((8, 2 * R), f32),
        ]
    ).astype(bf16)
    for e in range(out.shape[0]):
        out[e] = rows


def offset_messages(grad, suffix_proj, transfer, count):
    return pl.pallas_call(
        offset_kernel,
        out_shape=jax.ShapeDtypeStruct((count, R // 2 + 16, 2 * R), bf16),
        name="offset",
    )(grad, suffix_proj, transfer)


def local_kernel(grad, inverse, proj, step, side, solved, state):
    @pl.when(pl.program_id(0) == 0)
    def _():
        state[...] = jnp.zeros_like(state)

    g = grad[...]
    gh = g.astype(bf16).astype(f32)
    pair = jnp.concatenate([gh, g - gh]).astype(bf16)
    n = g.shape[0]

    def times(matrix):
        high, low = split(matrix)
        main = dot(pair, high, 1, 1)
        return (main[:n] + main[n:]) + dot(pair, low, 1, 1)[:n]

    entered = state[...]
    solved[...] = times(inverse[0]) - dot3(entered, side[...], 1, 0)
    state[...] = dot3(entered, step[0], 1, 1) + times(proj[...])


def local_solve(grad, diag_inv, proj, step, side):
    count = diag_inv.shape[0]
    labels = grad.shape[0]
    return pl.pallas_call(
        local_kernel,
        grid=(count,),
        in_specs=[
            pl.BlockSpec((labels, B), lambda i: (0, i)),
            pl.BlockSpec((1, B, B), lambda i: (i, 0, 0)),
            pl.BlockSpec((R, B), lambda i: (0, i)),
            pl.BlockSpec((1, R, R), lambda i: (i, 0, 0)),
            pl.BlockSpec((R, B), lambda i: (0, i)),
        ],
        out_specs=pl.BlockSpec((labels, B), lambda i: (0, i)),
        out_shape=jax.ShapeDtypeStruct((labels, count * B), f32),
        scratch_shapes=[pltpu.VMEM((labels, R), f32)],
        cost_estimate=pl.CostEstimate(
            flops=6 * count * labels * B * B, bytes_accessed=4 * count * B * B, transcendentals=0
        ),
        name="local_solve",
    )(grad, diag_inv, proj, step, side)


def finish_kernel(place, messages, solved, side, out):
    mine = place[0]
    count = messages.shape[0]
    half = R // 2

    def read(e):
        got = messages[e].astype(f32)
        transfer = jnp.concatenate([got[:half, :R], got[:half, R:]]).astype(bf16)
        rows = got[half : half + 8]
        return transfer, rows[:, :R] + rows[:, R:]

    def apply(rows, transfer):
        high, low = split(rows)
        return dot(high, transfer, 1, 1) + dot(low, transfer, 1, 1)

    eye = lax.broadcasted_iota(jnp.int32, (R, R), 0) == lax.broadcasted_iota(jnp.int32, (R, R), 1)
    early = jnp.zeros((8, R), f32)
    late = jnp.concatenate([early, eye.astype(f32)])
    blank = jnp.zeros((R, R), f32)
    for e in range(count // 2):
        transfer, rows = read(e)
        early = jnp.where(e < mine, apply(early, transfer) + rows, early)
        f = e + count // 2
        transfer, rows = read(f)
        moved = apply(late, transfer) + jnp.concatenate([rows, blank])
        late = jnp.where(f < mine, moved, late)
    entering = late[:8] + dot3(early, late[8:], 1, 0)
    z = solved[...] - dot3(entering, side[...], 1, 0)
    top = jnp.max(jnp.abs(z), axis=1, keepdims=True)
    power = jnp.ceil(jnp.log2(jnp.maximum(top, 1e-30)))
    width = z.shape[1]
    out[:, :width] = z * jnp.exp2(-power)
    out[:, width:] = jnp.broadcast_to(power, (8, 2 * R))


def finish(place, messages, solved, side):
    labels, m = solved.shape
    vmem = pl.BlockSpec(memory_space=pltpu.VMEM)
    return pl.pallas_call(
        finish_kernel,
        grid_spec=pltpu.PrefetchScalarGridSpec(
            num_scalar_prefetch=1,
            grid=(),
            in_specs=[vmem, vmem, vmem],
            out_specs=vmem,
        ),
        out_shape=jax.ShapeDtypeStruct((labels, m + 2 * R), f32),
        name="finish",
    )(place.reshape(1), messages, solved, side)


def unscaled_kernel(powers, scaled, out):
    out[...] = (scaled[...] * jnp.exp2(powers[:, :1])).T


def unscaled(whole, cols=1024):
    labels = whole.shape[0]
    m = whole.shape[1] - 2 * R
    return pl.pallas_call(
        unscaled_kernel,
        grid=(m // cols,),
        in_specs=[
            pl.BlockSpec((labels, 2 * R), lambda i: (0, m // (2 * R))),
            pl.BlockSpec((labels, cols), lambda i: (0, i)),
        ],
        out_specs=pl.BlockSpec((cols, labels), lambda i: (i, 0)),
        out_shape=jax.ShapeDtypeStruct((m, labels), f32),
        name="unscaled",
    )(whole, whole)


def sent_to_all(array, axis):
    copies = jnp.broadcast_to(array, (lax.axis_size(axis), *array.shape))
    return lax.all_to_all(copies, axis, split_axis=0, concat_axis=0, tiled=True)


def to_partner(array):
    return lax.ppermute(array, "c", [(0, 1), (1, 0)])


def body(points, centers, coeffs, targets, diag_inv, low_left, low_right, decay_rates, block_ranks):
    n, labels = targets.shape
    m = centers.shape[0]
    chips, samp = lax.axis_size("z"), lax.axis_size("samp")
    chip, core = lax.axis_index("z"), lax.axis_index("c")
    place = chip * 2 + core
    share = n // (2 * chips)

    points_t, centers_t = points.T, centers.T
    stored_b, pred_b = predict(1 - core, points_t, centers_t, coeffs)
    from_partner = to_partner(pred_b)
    stored_a, pred_a = predict(core, points_t, centers_t, coeffs)
    pair_sum = (pred_a + from_partner).astype(wire).reshape(chips, share, labels)
    arrived = lax.all_to_all(pair_sum, "z", 0, 0, tiled=True)
    proj, step, side, suffix_proj, transfer = prepare(
        block_ranks,
        diag_inv,
        jnp.swapaxes(low_left, 1, 2),
        jnp.swapaxes(low_right, 1, 2),
        decay_rates,
    )
    arrived, transfer = lax.optimization_barrier((arrived, transfer))
    pred_own = arrived.astype(f32).sum(axis=0)
    first = core * (n // 2) + chip * share
    own_targets = lax.dynamic_slice_in_dim(targets, first, share, 0)
    resid = (jax.nn.sigmoid(pred_own) - own_targets.astype(f32)).astype(bf16)
    resid_a = sent_to_all(resid, "z").reshape(n // 2, labels)
    resid_b = to_partner(resid_a)

    partial = gradient_t(resid_a, resid_b, stored_a, stored_b)
    own = labels // samp
    sent = partial.astype(wire).reshape(samp, own, m)
    sent, step_late, side_late = lax.optimization_barrier((sent, step, side))
    arrived = lax.all_to_all(sent, "samp", 0, 0, tiled=True)
    side_prefix = prefix_side(step_late, side_late)
    arrived, side_prefix = lax.optimization_barrier((arrived, side_prefix))
    own_coeffs = lax.dynamic_slice_in_dim(coeffs, lax.axis_index("samp") * own, own, 1).T
    scaling = 1.0 / math.sqrt(n * samp)
    grad = arrived.astype(f32).sum(axis=0) * scaling + ridge_weight * own_coeffs.astype(f32)

    messages = offset_messages(grad, suffix_proj, transfer, 2 * chips)
    messages = lax.all_to_all(messages, ("z", "c"), 0, 0, tiled=True)
    solved = local_solve(grad, diag_inv, proj, step, side)
    direction = finish(place, messages, solved, side_prefix)
    whole = sent_to_all(direction.astype(wire), "samp").reshape(labels, m + 2 * R)
    return unscaled(whole.astype(f32))


def solution(mesh):
    finer = Mesh(mesh.devices.reshape(mesh.shape["samp"], -1, 2), ("samp", "z", "c"))
    ind = ("z", "c")
    placed = (
        P("samp", None),
        P(ind, None),
        P(ind, None),
        P("samp", None),
        P(ind, None, None),
        P(ind, None, None),
        P(ind, None, None),
        P(ind, None),
        P(ind),
    )
    return jax.shard_map(
        body, mesh=finer, in_specs=placed, out_specs=P(ind, None), check_vma=False
    )
```

time: 170 us -> 149 us (0.88)
  blocking collectives: 56 us -> 36.3 us
  Pallas kernels: 45.6 us -> 60.2 us
  local copies, waits for them, and re-layouts: 10.6 us -> 2.15 us
  waiting for transfers between devices: 19.6 us -> 15.4 us
  other arithmetic: 4.9 us -> 8.6 us
  starting transfers between devices: 28.8 us -> 25.1 us
  matrix products: 2.6 us -> 0 us
    all_gather x1 -> x0, blocking collectives: 26 us -> none  [body(): residual = lax.all_gather(resid, 'ind', axis=0, tiled=True)]
    pallas_call x4 -> x7, Pallas kernels: 26.4 us -> 40.5 us  [the longest x2 17.4 us: predict(): pl.pallas_call(functools.partial(predict_kernel, width), grid_spec=pltpu....]
    all_to_all x4 -> x3, starting transfers between devices: 28.8 us -> 19.6 us  [the longest x1 6.78 us: body(): arrived = lax.all_to_all(sent, 'samp', 0, 0, tiled=True)]
    all_to_all x1 -> x2, blocking collectives: 30.1 us -> 36.3 us  [sent_to_all(): return lax.all_to_all(copies, axis, split_axis=0, concat_axis=0, tiled=True)]
    ppermute x0 -> x2, starting transfers between devices: none -> 5.43 us  [to_partner(): return lax.ppermute(array, 'c', [(0, 1), (1, 0)])]
    all_to_all x4 -> x3, waiting for transfers between devices: 19.6 us -> 14.3 us  [the longest x1 11.3 us: body(): arrived = lax.all_to_all(sent, 'samp', 0, 0, tiled=True)]
    broadcast_in_dim x3 -> x2, local copies, waits for them, and re-layouts: 4.02 us -> 0.11 us  [sent_to_all(): copies = jnp.broadcast_to(array, (lax.axis_size(axis), *array.shape))]
    convert_element_type x2 -> x3, other arithmetic: 0.88 us -> 4.19 us  [the longest x1 1.79 us: body(): (pred_a + from_partner).astype(wire).reshape(chips, share, labels)]
  transfers between devices with their start and end apart: 4 -> 5, of which waited for: 2 -> 4; matrix products, arithmetic and copies ran while one was open for 3% -> 0% of each run, Pallas kernels for 16% -> 22%
where the time goes in v2:
time: 149 us; the launch traced here: 148 us
  Pallas kernels  60.2 us (40%)
  blocking collectives  36.3 us (24%)
  starting transfers between devices  25.1 us (17%)
  waiting for transfers between devices  15.4 us (10%)
  other arithmetic  8.6 us (6%)
  local copies, waits for them, and re-layouts  2.15 us (1%)
    all_to_all x2, blocking collectives, sent_to_all(): return lax.all_to_all(copies, axis, split_axis=0, concat_axis=0, tiled=True)  36.3 us
    pallas_call x2, Pallas kernels, predict(): pl.pallas_call(functools.partial(predict_kernel, width), grid_spec=pltpu....  17.4 us
    all_to_all x1, waiting for transfers between devices, body(): arrived = lax.all_to_all(sent, 'samp', 0, 0, tiled=True)  11.3 us
    pallas_call x1, Pallas kernels, prepare(): pl.pallas_call(prepare_kernel, grid_spec=pltpu.PrefetchScalarGridSpec(num...  11.2 us
    pallas_call x1, Pallas kernels, gradient_t(): pl.pallas_call(gradient_kernel, grid=(m // cols,), in_specs=[whole, whole...  8.77 us
    pallas_call x1, Pallas kernels, local_solve(): pl.pallas_call(local_kernel, grid=(count,), in_specs=[pl.BlockSpec((label...  8.5 us
    all_to_all x1, starting transfers between devices, body(): arrived = lax.all_to_all(sent, 'samp', 0, 0, tiled=True)  6.78 us
    all_to_all x1, starting transfers between devices, body(): arrived = lax.all_to_all(pair_sum, 'z', 0, 0, tiled=True)  6.46 us
  transfers between devices with their start and end apart: 5, of which 4 were waited for; matrix products, arithmetic and copies ran while one was open for 0% of the time, Pallas kernels for 22%

profile of v2, /device:TPU:1, one launch (start us, length us, event | category | flops | bytes accessed | tf_op | source)
XLA Modules:
  0.0 147.8 jit_solution(11165585434977464554)
XLA Ops:
  0.0 8.7 %predict.3 = (bf16[1024,4096]{1,0:T(8,128)(2,1)}, f32[1024,128]{1,0:T(8,128)}) custom-call(s32[1]{0:T(128)} %bitcast.4.half, bf16[64,2048]{1,0:T(8,128)(2,1)} %bitcast.24, bf16[64,4096]{1,0:T(8,128)(2,1)} %bitcast.22, bf16[4096,128]{1,0:T(8,128)(2,1)} %coeffs.3), custom_call_target="tpu_custom_call" | custom-call | flops 1610612736 | bytes 8388608 | tf_op jit(solution)/shard_map/predict/pallas_call | solution.py:61
  8.7 3.2 %collective-permute-start = (f32[1024,128]{1,0:T(8,128)}, f32[1024,128]{1,0:T(8,128)S(1)}, u32[]{:S(2)}, u32[]{:S(2)}) collective-permute-start(f32[1024,128]{1,0:T(8,128)} %get-tuple-element.22), channel_id=1, source_target_pairs={{0,1},{1,0},{2,3},{3,2},{4,5},{5,4},{6,7},{7,6},{8,9},{9,8},{10,11... | collective-permute-start | bytes 1572872 | tf_op jit(solution)/shard_map/ppermute | solution.py:350
  11.9 8.7 %predict.2 = (bf16[1024,4096]{1,0:T(8,128)(2,1)}, f32[1024,128]{1,0:T(8,128)}) custom-call(s32[1]{0:T(128)} %bitcast.1.half, bf16[64,2048]{1,0:T(8,128)(2,1)} %bitcast.25, bf16[64,4096]{1,0:T(8,128)(2,1)} %bitcast.23, bf16[4096,128]{1,0:T(8,128)(2,1)} %coeffs.3), custom_call_target="tpu_custom_call" | custom-call | flops 1610612736 | bytes 8388608 | tf_op jit(solution)/shard_map/predict/pallas_call | solution.py:61
  20.6 0.0 collective-permute-done
  20.6 1.8 %add_convert_fusion = f16[1024,128]{1,0:T(8,128)(2,1)} fusion(f32[1024,128]{1,0:T(8,128)} %get-tuple-element.21, f32[1024,128]{1,0:T(8,128)S(1)} %collective-permute-done), kind=kLoop, calls=%fused_computation.4 | loop fusion | flops 262144 | bytes 1310720 | tf_op jit(solution)/shard_map/convert_element_type | solution.py:365
  22.4 6.5 %all-to-all-start = ((f16[8,128,128]{2,1,0:T(8,128)(2,1)}), f16[8,128,128]{2,1,0:T(8,128)(2,1)S(1)}, u32[]{:S(2)}, u32[]{:S(2)}) async-start(f16[8,128,128]{2,1,0:T(8,128)(2,1)} %bitcast.5), calls=%async_computation | async-start | bytes 524288 | tf_op jit(solution)/shard_map/all_to_all | solution.py:366
  28.9 11.2 %prepare.1 = (f32[64,4096]{1,0:T(8,128)}, f32[8,64,64]{2,1,0:T(8,128)}, f32[64,4096]{1,0:T(8,128)}, f32[64,4096]{1,0:T(8,128)}, f32[64,64]{1,0:T(8,128)}) custom-call(s32[8]{0:T(128)} %ranks.1, f32[8,512,512]{2,1,0:T(8,128)} %inverse.3, bf16[8,64,512]{2,1,0:T(8,128)(2,1)} %bitcast.19, bf16[8,64,512]{2,1,0:T(8,128)(2,1)} %bitcast.20, f32[8,1,64]{2,1,0:T(1,128)} %bitcast.21), custom_call_target="tpu_custom_call" | custom-call | flops 1073741824 | bytes 12582912 | tf_op jit(solution)/shard_map/prepare/pallas_call | solution.py:149
  40.0 1.2 all-to-all-done
  41.3 0.8 subtract_convert_fusion
  42.1 15.9 %all_to_all.25 = bf16[8,128,128]{2,1,0:T(8,128)(2,1)S(1)} all-to-all(bf16[8,128,128]{2,1,0:T(8,128)(2,1)S(1)} %broadcast_in_dim.10), channel_id=1, replica_groups=mesh['samp'=16,'z'=8,'c'=2] {'z'}, dimensions={0} | all-to-all | bytes 524288 | tf_op jit(solution)/shard_map/all_to_all | solution.py:346
  58.0 0.0 copy-start
  58.0 2.2 %collective-permute-start.1 = (bf16[1024,128]{1,0:T(8,128)(2,1)S(1)}, bf16[1024,128]{1,0:T(8,128)(2,1)S(1)}, u32[]{:S(2)}, u32[]{:S(2)}) collective-permute-start(bf16[1024,128]{1,0:T(8,128)(2,1)S(1)} %bitcast.17), channel_id=1, source_target_pairs={{0,1},{1,0},{2,3},{3,2},{4,5},{5,4},{6,7},{7,6},{8,9},{9,8},{10,11... | collective-permute-start | bytes 786440 | tf_op jit(solution)/shard_map/ppermute | solution.py:350
  60.2 1.2 collective-permute-done.1.resid_b
  61.3 0.0 copy-start.3
  61.3 0.0 copy-done
  61.3 0.7 copy-done.3
  62.0 8.8 %gradient.1 = f32[128,4096]{1,0:T(8,128)} custom-call(bf16[1024,128]{1,0:T(8,128)(2,1)} %bitcast.18, bf16[1024,128]{1,0:T(8,128)(2,1)} %copy-done.3, bf16[1024,4096]{1,0:T(8,128)(2,1)} %get-tuple-element.25.rows_a, bf16[1024,4096]{1,0:T(8,128)(2,1)} %get-tuple-element.26.rows_b), custom_call_target="tpu_custom_call" | custom-call | flops 2147483648 | bytes 16777216 | tf_op jit(solution)/shard_map/gradient/pallas_call | solution.py:102
  70.8 0.0 copy-start.1
  70.8 2.8 %convert_bitcast_fusion = f16[16,8,4096]{2,1,0:T(8,128)(2,1)} fusion(f32[128,4096]{1,0:T(8,128)} %gradient.1), kind=kLoop, calls=%fused_computation.2 | loop fusion | flops 524288 | bytes 3145728 | tf_op jit(solution)/shard_map/reshape | solution.py:384
  73.6 6.8 %all-to-all-start.2 = ((f16[16,8,4096]{2,1,0:T(8,128)(2,1)}), f16[16,8,4096]{2,1,0:T(8,128)(2,1)S(1)}, u32[]{:S(2)}, u32[]{:S(2)}) async-start(f16[16,8,4096]{2,1,0:T(8,128)(2,1)} %convert_bitcast_fusion), calls=%async_computation.2 | async-start | bytes 2097152 | tf_op jit(solution)/shard_map/all_to_all | solution.py:386
  80.4 0.0 copy-done.1
  80.4 0.4 constant_dynamic-slice_fusion
  80.7 0.3 copy.11
  81.0 3.7 %prefix.1.side = f32[64,4096]{1,0:T(8,128)} custom-call(f32[8,64,64]{2,1,0:T(8,128)} %get-tuple-element.30.step, f32[64,4096]{1,0:T(8,128)} %get-tuple-element.31.side), custom_call_target="tpu_custom_call" | custom-call | flops 100663296 | bytes 2097152 | tf_op jit(solution)/shard_map/prefix/pallas_call | solution.py:197
  84.7 11.3 %all-to-all-done.2 = f16[16,8,4096]{2,1,0:T(8,128)(2,1)S(1)} async-done(((f16[16,8,4096]{2,1,0:T(8,128)(2,1)}), f16[16,8,4096]{2,1,0:T(8,128)(2,1)S(1)}, u32[]{:S(2)}, u32[]{:S(2)}) %all-to-all-start.2) | async-done | bytes 1048608 | tf_op jit(solution)/shard_map/all_to_all | solution.py:386
  96.0 0.1 convert_reduce_fusion
  96.2 0.7 bitcast_add_fusion.grad
  96.8 2.5 %offset.1 = bf16[16,48,128]{2,1,0:T(8,128)(2,1)} custom-call(f32[8,4096]{1,0:T(8,128)} %bitcast_add_fusion.grad, f32[64,4096]{1,0:T(8,128)} %get-tuple-element.33.suffix_proj, f32[64,64]{1,0:T(8,128)} %get-tuple-element.34.transfer), custom_call_target="tpu_custom_call" | custom-call | tf_op jit(solution)/shard_map/offset/pallas_call | solution.py:223
  99.3 6.4 %all-to-all-start.3 = ((bf16[16,48,128]{2,1,0:T(8,128)(2,1)}), bf16[16,48,128]{2,1,0:T(8,128)(2,1)S(1)}, u32[]{:S(2)}, u32[]{:S(2)}) async-start(bf16[16,48,128]{2,1,0:T(8,128)(2,1)} %offset.1), calls=%async_computation.3 | async-start | bytes 393216 | tf_op jit(solution)/shard_map/all_to_all | solution.py:394
  105.7 8.5 %local_solve.1.solved = f32[8,4096]{1,0:T(8,128)} custom-call(f32[8,4096]{1,0:T(8,128)} %bitcast_add_fusion.grad, f32[8,512,512]{2,1,0:T(8,128)} %inverse.3, f32[64,4096]{1,0:T(8,128)} %get-tuple-element.35.proj, f32[8,64,64]{2,1,0:T(8,128)} %get-tuple-element.30.step, f32[64,4096]{1,0:T(8,128)} %get-tuple-element.31.side), custom_call_target="tpu_custom_call" | custom-call | flops 100663296 | bytes 8388608 | tf_op jit(solution)/shard_map/local_solve/pallas_call | solution.py:253
  114.2 1.8 %all-to-all-done.3.messages = bf16[16,48,128]{2,1,0:T(8,128)(2,1)S(1)} async-done(((bf16[16,48,128]{2,1,0:T(8,128)(2,1)}), bf16[16,48,128]{2,1,0:T(8,128)(2,1)S(1)}, u32[]{:S(2)}, u32[]{:S(2)}) %all-to-all-start.3) | async-done | bytes 196640 | tf_op jit(solution)/shard_map/all_to_all | solution.py:394
  116.0 0.0 copy-start.2
  116.0 0.7 copy-done.2
  116.7 3.9 %finish.1 = f32[8,4224]{1,0:T(8,128)} custom-call(s32[1]{0:T(128)} %bitcast.place, bf16[16,48,128]{2,1,0:T(8,128)(2,1)} %copy-done.2, f32[8,4096]{1,0:T(8,128)} %local_solve.1.solved, f32[64,4096]{1,0:T(8,128)} %prefix.1.side), custom_call_target="tpu_custom_call" | custom-call | tf_op jit(solution)/shard_map/finish/pallas_call | solution.py:311
  120.6 0.9 convert_element_type.37
  121.5 0.1 broadcast_in_dim.11
  121.6 20.5 %all_to_all.26 = f16[16,8,4224]{2,1,0:T(8,128)(2,1)S(1)} all-to-all(f16[16,8,4224]{2,1,0:T(8,128)(2,1)S(1)} %broadcast_in_dim.11), channel_id=1, replica_groups=mesh['samp'=16,'z'=8,'c'=2] {'samp'}, dimensions={0} | all-to-all | bytes 2162688 | tf_op jit(solution)/shard_map/all_to_all | solution.py:346
  142.1 1.5 %bitcast_convert_fusion.powers.scaled = f32[128,4224]{1,0:T(8,128)} fusion(f16[16,8,4224]{2,1,0:T(8,128)(2,1)S(1)} %all_to_all.26), kind=kLoop, calls=%fused_computation.1 | loop fusion | flops 540672 | bytes 3244032 | tf_op jit(solution)/shard_map/convert_element_type | solution.py:398
  143.5 4.3 %unscaled.1 = f32[4096,128]{1,0:T(8,128)} custom-call(f32[128,4224]{1,0:T(8,128)} %bitcast_convert_fusion.powers.scaled, f32[128,4224]{1,0:T(8,128)} %bitcast_convert_fusion.powers.scaled), custom_call_target="tpu_custom_call" | custom-call | tf_op jit(solution)/shard_map/unscaled/pallas_call | solution.py:331
  (2 shorter events, 0.1 us)
Async XLA Ops:
  8.7 11.9 %collective-permute-start = (f32[1024,128]{1,0:T(8,128)}, f32[1024,128]{1,0:T(8,128)S(1)}, u32[]{:S(2)}, u32[]{:S(2)}) collective-permute-start(f32[1024,128]{1,0:T(8,128)} %get-tuple-element.22), channel_id=1, source_target_pairs={{0,1},{1,0},{2,3},{3,2},{4,5},{5,4},{6,7},{7,6},{8,9},{9,8},{10,11... | collective-permute-start | bytes 1572872 | tf_op jit(solution)/shard_map/ppermute | solution.py:350
  22.4 18.8 %all-to-all-start = ((f16[8,128,128]{2,1,0:T(8,128)(2,1)}), f16[8,128,128]{2,1,0:T(8,128)(2,1)S(1)}, u32[]{:S(2)}, u32[]{:S(2)}) async-start(f16[8,128,128]{2,1,0:T(8,128)(2,1)} %bitcast.5), calls=%async_computation | async-start | bytes 524288 | tf_op jit(solution)/shard_map/all_to_all | solution.py:366
  58.0 3.4 %copy-start = (bf16[8,128,128]{2,1,0:T(8,128)(2,1)}, bf16[8,128,128]{2,1,0:T(8,128)(2,1)S(1)}, u32[]{:S(2)}) copy-start(bf16[8,128,128]{2,1,0:T(8,128)(2,1)S(1)} %all_to_all.25) | copy-start | bytes 786436
  58.0 3.4 %collective-permute-start.1 = (bf16[1024,128]{1,0:T(8,128)(2,1)S(1)}, bf16[1024,128]{1,0:T(8,128)(2,1)S(1)}, u32[]{:S(2)}, u32[]{:S(2)}) collective-permute-start(bf16[1024,128]{1,0:T(8,128)(2,1)S(1)} %bitcast.17), channel_id=1, source_target_pairs={{0,1},{1,0},{2,3},{3,2},{4,5},{5,4},{6,7},{7,6},{8,9},{9,8},{10,11... | collective-permute-start | bytes 786440 | tf_op jit(solution)/shard_map/ppermute | solution.py:350
  61.3 0.7 copy-start.3
  70.8 9.6 %copy-start.1 = (bf16[4096,128]{1,0:T(8,128)(2,1)S(1)}, bf16[4096,128]{1,0:T(8,128)(2,1)}, u32[]{:S(2)}) copy-start(bf16[4096,128]{1,0:T(8,128)(2,1)} %coeffs.3) | copy-start | bytes 3145732
  73.6 22.4 %all-to-all-start.2 = ((f16[16,8,4096]{2,1,0:T(8,128)(2,1)}), f16[16,8,4096]{2,1,0:T(8,128)(2,1)S(1)}, u32[]{:S(2)}, u32[]{:S(2)}) async-start(f16[16,8,4096]{2,1,0:T(8,128)(2,1)} %convert_bitcast_fusion), calls=%async_computation.2 | async-start | bytes 2097152 | tf_op jit(solution)/shard_map/all_to_all | solution.py:386
  99.3 16.7 %all-to-all-start.3 = ((bf16[16,48,128]{2,1,0:T(8,128)(2,1)}), bf16[16,48,128]{2,1,0:T(8,128)(2,1)S(1)}, u32[]{:S(2)}, u32[]{:S(2)}) async-start(bf16[16,48,128]{2,1,0:T(8,128)(2,1)} %offset.1), calls=%async_computation.3 | async-start | bytes 393216 | tf_op jit(solution)/shard_map/all_to_all | solution.py:394
  116.0 0.7 copy-start.2

commit v3 on v2

--- a/solution.py
+++ b/solution.py
@@ -55,7 +55,7 @@
     pred[...] = total
 
 
-def predict(half, points_t, centers_t, coeffs, rows=512, width=256):
+def predict(half, points_t, centers_t, coeffs, rows=256, width=256):
     n, m, labels = points_t.shape[1] // 2, centers_t.shape[1], coeffs.shape[1]
     steps = n // rows
     return pl.pallas_call(
@@ -106,7 +106,7 @@
         out_specs=pl.BlockSpec((labels, cols), lambda i: (0, i)),
         out_shape=jax.ShapeDtypeStruct((labels, m), f32),
         scratch_shapes=[pltpu.VMEM((labels, n), bf16)] * 2,
-        compiler_params=pltpu.CompilerParams(vmem_limit_bytes=60 << 20),
+        compiler_params=pltpu.CompilerParams(vmem_limit_bytes=56 << 20),
         cost_estimate=pl.CostEstimate(
             flops=4 * n * m * labels, bytes_accessed=4 * n * m, transcendentals=0
         ),
@@ -114,16 +114,16 @@
     )(resid_a, resid_b, stored_a, stored_b)
 
 
-def prepare_kernel(ranks, inverse, left_t, right_t, rates, proj, step, side, suffix_proj, transfer, acc):
+def prepare_kernel(last, ranks, inverse, left_t, right_t, rates, *refs):
+    proj, step, side, suffix_proj, transfer, acc = refs[-6:]
     i = pl.program_id(0)
-    k = pl.num_programs(0) - 1 - i
     eye = lax.broadcasted_iota(jnp.int32, (R, R), 0) == lax.broadcasted_iota(jnp.int32, (R, R), 1)
 
     @pl.when(i == 0)
     def _():
-        acc[...] = eye.astype(f32)
-
-    kept = lax.broadcasted_iota(jnp.int32, (R, B), 0) < ranks[k]
+        acc[...] = eye.astype(f32) if len(refs) == 6 else refs[0][...]
+
+    kept = lax.broadcasted_iota(jnp.int32, (R, B), 0) < ranks[last - i]
     left = jnp.where(kept, left_t[0].astype(f32), 0.0).astype(bf16)
     right = jnp.where(kept, right_t[0].astype(f32), 0.0).astype(bf16)
     high, low = split(inverse[0])
@@ -141,28 +141,33 @@
     transfer[...] = suffix
 
 
-def prepare(block_ranks, diag_inv, left_t, right_t, rates):
+def prepare(block_ranks, diag_inv, left_t, right_t, rates, earlier=None):
     count = diag_inv.shape[0]
-    back = lambda i, ranks: (count - 1 - i, 0, 0)
-    wide = lambda i, ranks: (0, count - 1 - i)
+    steps = count // 2
+    last = count - 1 if earlier is None else steps - 1
+    back = lambda i, ranks: (last - i, 0, 0)
+    wide = lambda i, ranks: (0, last - i)
+    square = pl.BlockSpec((R, R), lambda i, ranks: (0, 0))
     wide_shape = jax.ShapeDtypeStruct((R, count * B), f32)
-    return pl.pallas_call(
-        prepare_kernel,
+    kept = () if earlier is None else (earlier[4], *earlier[:4])
+    return pl.pallas_call(
+        functools.partial(prepare_kernel, last),
         grid_spec=pltpu.PrefetchScalarGridSpec(
             num_scalar_prefetch=1,
-            grid=(count,),
+            grid=(steps,),
             in_specs=[
                 pl.BlockSpec((1, B, B), back),
                 pl.BlockSpec((1, R, B), back),
                 pl.BlockSpec((1, R, B), back),
                 pl.BlockSpec((1, 1, R), back),
-            ],
+            ]
+            + ([square] + [pl.BlockSpec(memory_space=pl.ANY)] * 4 if kept else []),
             out_specs=[
                 pl.BlockSpec((R, B), wide),
                 pl.BlockSpec((1, R, R), back),
                 pl.BlockSpec((R, B), wide),
                 pl.BlockSpec((R, B), wide),
-                pl.BlockSpec((R, R), lambda i, ranks: (0, 0)),
+                square,
             ],
             scratch_shapes=[pltpu.VMEM((R, R), f32)],
         ),
@@ -173,11 +178,13 @@
             wide_shape,
             jax.ShapeDtypeStruct((R, R), f32),
         ],
+        input_output_aliases={6: 0, 7: 1, 8: 2, 9: 3} if kept else {},
         cost_estimate=pl.CostEstimate(
-            flops=8 * count * R * B * B, bytes_accessed=6 * count * B * B, transcendentals=0
-        ),
+            flops=8 * steps * R * B * B, bytes_accessed=6 * steps * B * B, transcendentals=0
+        ),
+        compiler_params=pltpu.CompilerParams(vmem_limit_bytes=58 << 20),
         name="prepare",
-    )(block_ranks, diag_inv, left_t, right_t, rates[:, None, :])
+    )(block_ranks, diag_inv, left_t, right_t, rates[:, None, :], *kept)
 
 
 def prefix_kernel(step, side, out):
@@ -200,6 +207,7 @@
         cost_estimate=pl.CostEstimate(
             flops=6 * R * side.size, bytes_accessed=8 * side.size, transcendentals=0
         ),
+        compiler_params=pltpu.CompilerParams(vmem_limit_bytes=40 << 20),
         name="prefix",
     )(step, side)
 
@@ -223,6 +231,7 @@
     return pl.pallas_call(
         offset_kernel,
         out_shape=jax.ShapeDtypeStruct((count, R // 2 + 16, 2 * R), bf16),
+        compiler_params=pltpu.CompilerParams(vmem_limit_bytes=40 << 20),
         name="offset",
     )(grad, suffix_proj, transfer)
 
@@ -266,6 +275,7 @@
         cost_estimate=pl.CostEstimate(
             flops=6 * count * labels * B * B, bytes_accessed=4 * count * B * B, transcendentals=0
         ),
+        compiler_params=pltpu.CompilerParams(vmem_limit_bytes=56 << 20),
         name="local_solve",
     )(grad, diag_inv, proj, step, side)
 
@@ -317,6 +327,7 @@
             out_specs=vmem,
         ),
         out_shape=jax.ShapeDtypeStruct((labels, m + 2 * R), f32),
+        compiler_params=pltpu.CompilerParams(vmem_limit_bytes=40 << 20),
         name="finish",
     )(place.reshape(1), messages, solved, side)
 
@@ -337,6 +348,7 @@
         ],
         out_specs=pl.BlockSpec((cols, labels), lambda i: (i, 0)),
         out_shape=jax.ShapeDtypeStruct((m, labels), f32),
+        compiler_params=pltpu.CompilerParams(vmem_limit_bytes=40 << 20),
         name="unscaled",
     )(whole, whole)
 
@@ -364,19 +376,24 @@
     stored_a, pred_a = predict(core, points_t, centers_t, coeffs)
     pair_sum = (pred_a + from_partner).astype(wire).reshape(chips, share, labels)
     arrived = lax.all_to_all(pair_sum, "z", 0, 0, tiled=True)
-    proj, step, side, suffix_proj, transfer = prepare(
+    factors = (
         block_ranks,
         diag_inv,
         jnp.swapaxes(low_left, 1, 2),
         jnp.swapaxes(low_right, 1, 2),
         decay_rates,
     )
-    arrived, transfer = lax.optimization_barrier((arrived, transfer))
+    halfway = prepare(*factors)
+    arrived, halfway = lax.optimization_barrier((arrived, halfway))
     pred_own = arrived.astype(f32).sum(axis=0)
     first = core * (n // 2) + chip * share
     own_targets = lax.dynamic_slice_in_dim(targets, first, share, 0)
     resid = (jax.nn.sigmoid(pred_own) - own_targets.astype(f32)).astype(bf16)
+    resid, halfway = lax.optimization_barrier((resid, halfway))
     resid_a = sent_to_all(resid, "z").reshape(n // 2, labels)
+    prepared = prepare(*factors, halfway)
+    resid_a, prepared = lax.optimization_barrier((resid_a, prepared))
+    proj, step, side, suffix_proj, transfer = prepared
     resid_b = to_partner(resid_a)
 
     partial = gradient_t(resid_a, resid_b, stored_a, stored_b)

time: 149 us -> 142 us (0.953)
  blocking collectives: 36.3 us -> 20.5 us
  waiting for transfers between devices: 15.4 us -> 27.1 us
  Pallas kernels: 60.2 us -> 55.6 us
  starting transfers between devices: 25.1 us -> 26.9 us
  other arithmetic: 8.6 us -> 6.98 us
  local copies, waits for them, and re-layouts: 2.15 us -> 3.68 us
    all_to_all x2 -> x1, blocking collectives: 36.3 us -> 20.5 us  [sent_to_all(): return lax.all_to_all(copies, axis, split_axis=0, concat_axis=0, tiled=True)]
    all_to_all x0 -> x1, waiting for transfers between devices: none -> 5.46 us  [sent_to_all(): return lax.all_to_all(copies, axis, split_axis=0, concat_axis=0, tiled=True)]
    all_to_all x1, waiting for transfers between devices: 1.2 us -> 5.72 us  [body(): arrived = lax.all_to_all(pair_sum, 'z', 0, 0, tiled=True)]
    all_to_all x0 -> x1, starting transfers between devices: none -> 3.41 us  [sent_to_all(): return lax.all_to_all(copies, axis, split_axis=0, concat_axis=0, tiled=True)]
    pallas_call x1, Pallas kernels: 3.69 us -> 1.38 us  [prefix_side(): pl.pallas_call(prefix_kernel, out_shape=jax.ShapeDtypeStruct(side.shape,...]
    pallas_call x1 -> x2, Pallas kernels: 11.2 us -> 13.3 us  [prepare(): pl.pallas_call(functools.partial(prepare_kernel, last), grid_spec=pltpu.P...]
    pallas_call x1, Pallas kernels: 3.9 us -> 1.83 us  [finish(): pl.pallas_call(finish_kernel, grid_spec=pltpu.PrefetchScalarGridSpec(num_...]
    all_to_all x1, waiting for transfers between devices: 11.3 us -> 13 us  [body(): arrived = lax.all_to_all(sent, 'samp', 0, 0, tiled=True)]
  transfers between devices with their start and end apart: 5 -> 6, of which waited for: 4 -> 5; matrix products, arithmetic and copies ran while one was open for 0% -> 0% of each run, Pallas kernels for 22% -> 23%
where the time goes in v3:
time: 142 us; the launch traced here: 141 us
  Pallas kernels  55.6 us (39%)
  waiting for transfers between devices  27.1 us (19%)
  starting transfers between devices  26.9 us (19%)
  blocking collectives  20.5 us (14%)
  other arithmetic  6.98 us (5%)
  local copies, waits for them, and re-layouts  3.68 us (3%)
    all_to_all x1, blocking collectives, sent_to_all(): return lax.all_to_all(copies, axis, split_axis=0, concat_axis=0, tiled=True)  20.5 us
    pallas_call x2, Pallas kernels, predict(): pl.pallas_call(functools.partial(predict_kernel, width), grid_spec=pltpu....  17.8 us
    pallas_call x2, Pallas kernels, prepare(): pl.pallas_call(functools.partial(prepare_kernel, last), grid_spec=pltpu.P...  13.3 us
    all_to_all x1, waiting for transfers between devices, body(): arrived = lax.all_to_all(sent, 'samp', 0, 0, tiled=True)  13 us
    pallas_call x1, Pallas kernels, gradient_t(): pl.pallas_call(gradient_kernel, grid=(m // cols,), in_specs=[whole, whole...  8.78 us
    pallas_call x1, Pallas kernels, local_solve(): pl.pallas_call(local_kernel, grid=(count,), in_specs=[pl.BlockSpec((label...  8.51 us
    all_to_all x1, starting transfers between devices, body(): arrived = lax.all_to_all(sent, 'samp', 0, 0, tiled=True)  6.79 us
    all_to_all x1, starting transfers between devices, body(): arrived = lax.all_to_all(pair_sum, 'z', 0, 0, tiled=True)  6.47 us
  transfers between devices with their start and end apart: 6, of which 5 were waited for; matrix products, arithmetic and copies ran while one was open for 0% of the time, Pallas kernels for 23%

profile of v3, /device:TPU:1, one launch (start us, length us, event | category | flops | bytes accessed | tf_op | source)
XLA Modules:
  0.0 140.9 jit_solution(13928667936290369789)
XLA Ops:
  0.0 8.9 %predict.3 = (bf16[1024,4096]{1,0:T(8,128)(2,1)}, f32[1024,128]{1,0:T(8,128)}) custom-call(s32[1]{0:T(128)} %bitcast.4.half, bf16[64,2048]{1,0:T(8,128)(2,1)} %bitcast.27, bf16[64,4096]{1,0:T(8,128)(2,1)} %bitcast.25, bf16[4096,128]{1,0:T(8,128)(2,1)} %coeffs.3), custom_call_target="tpu_custom_call" | custom-call | flops 1610612736 | bytes 8388608 | tf_op jit(solution)/shard_map/predict/pallas_call | solution.py:61
  8.9 3.2 %collective-permute-start = (f32[1024,128]{1,0:T(8,128)}, f32[1024,128]{1,0:T(8,128)S(1)}, u32[]{:S(2)}, u32[]{:S(2)}) collective-permute-start(f32[1024,128]{1,0:T(8,128)} %get-tuple-element.43), channel_id=1, source_target_pairs={{0,1},{1,0},{2,3},{3,2},{4,5},{5,4},{6,7},{7,6},{8,9},{9,8},{10,11... | collective-permute-start | bytes 1572872 | tf_op jit(solution)/shard_map/ppermute | solution.py:362
  12.1 8.9 %predict.2 = (bf16[1024,4096]{1,0:T(8,128)(2,1)}, f32[1024,128]{1,0:T(8,128)}) custom-call(s32[1]{0:T(128)} %bitcast.1.half, bf16[64,2048]{1,0:T(8,128)(2,1)} %bitcast.28, bf16[64,4096]{1,0:T(8,128)(2,1)} %bitcast.26, bf16[4096,128]{1,0:T(8,128)(2,1)} %coeffs.3), custom_call_target="tpu_custom_call" | custom-call | flops 1610612736 | bytes 8388608 | tf_op jit(solution)/shard_map/predict/pallas_call | solution.py:61
  21.0 0.0 collective-permute-done
  21.0 1.8 %add_convert_fusion = f16[1024,128]{1,0:T(8,128)(2,1)} fusion(f32[1024,128]{1,0:T(8,128)} %get-tuple-element.42, f32[1024,128]{1,0:T(8,128)S(1)} %collective-permute-done), kind=kLoop, calls=%fused_computation.4 | loop fusion | flops 262144 | bytes 1310720 | tf_op jit(solution)/shard_map/convert_element_type | solution.py:377
  22.8 6.5 %all-to-all-start = ((f16[8,128,128]{2,1,0:T(8,128)(2,1)}), f16[8,128,128]{2,1,0:T(8,128)(2,1)S(1)}, u32[]{:S(2)}, u32[]{:S(2)}) async-start(f16[8,128,128]{2,1,0:T(8,128)(2,1)} %bitcast.5), calls=%async_computation | async-start | bytes 524288 | tf_op jit(solution)/shard_map/all_to_all | solution.py:378
  29.3 6.6 %prepare.2 = (f32[64,4096]{1,0:T(8,128)}, f32[8,64,64]{2,1,0:T(8,128)}, f32[64,4096]{1,0:T(8,128)}, f32[64,4096]{1,0:T(8,128)}, f32[64,64]{1,0:T(8,128)}) custom-call(s32[8]{0:T(128)} %ranks.3, f32[8,512,512]{2,1,0:T(8,128)} %inverse.5, bf16[8,64,512]{2,1,0:T(8,128)(2,1)} %bitcast.17, bf16[8,64,512]{2,1,0:T(8,128)(2,1)} %bitcast.19, f32[8,1,64]{2,1,0:T(1,128)} %bitcast.23), custom_call_target="tpu_custom_call" | custom-call | flops 536870912 | bytes 6291456 | tf_op jit(solution)/shard_map/prepare/pallas_call | solution.py:153
  35.9 5.7 %all-to-all-done = f16[8,128,128]{2,1,0:T(8,128)(2,1)S(1)} async-done(((f16[8,128,128]{2,1,0:T(8,128)(2,1)}), f16[8,128,128]{2,1,0:T(8,128)(2,1)S(1)}, u32[]{:S(2)}, u32[]{:S(2)}) %all-to-all-start) | async-done | bytes 262176 | tf_op jit(solution)/shard_map/all_to_all | solution.py:378
  41.7 0.8 subtract_convert_fusion
  42.5 0.7 broadcast_in_dim.11
  43.2 3.4 %all-to-all-start.1 = ((bf16[8,128,128]{2,1,0:T(8,128)(2,1)}), bf16[8,128,128]{2,1,0:T(8,128)(2,1)S(1)}, u32[]{:S(2)}, u32[]{:S(2)}) async-start(bf16[8,128,128]{2,1,0:T(8,128)(2,1)} %broadcast_in_dim.11), calls=%async_computation.1 | async-start | bytes 524288 | tf_op jit(solution)/shard_map/all_to_all | solution.py:358
  46.6 6.7 %prepare.3 = (f32[64,4096]{1,0:T(8,128)}, f32[8,64,64]{2,1,0:T(8,128)}, f32[64,4096]{1,0:T(8,128)}, f32[64,4096]{1,0:T(8,128)}, f32[64,64]{1,0:T(8,128)}) custom-call(s32[8]{0:T(128)} %ranks.3, f32[8,512,512]{2,1,0:T(8,128)} %inverse.5, bf16[8,64,512]{2,1,0:T(8,128)(2,1)} %bitcast.18, ...), custom_call_target="tpu_custom_call", output_to_operand_aliasing={{0}: (6, {}), {1}: (7, {}), {2}: (8, {}), {3}: (9, {})} | custom-call | flops 536870912 | bytes 6291456 | tf_op jit(solution)/shard_map/prepare/pallas_call | solution.py:153
  53.3 5.5 %all-to-all-done.1 = bf16[8,128,128]{2,1,0:T(8,128)(2,1)S(1)} async-done(((bf16[8,128,128]{2,1,0:T(8,128)(2,1)}), bf16[8,128,128]{2,1,0:T(8,128)(2,1)S(1)}, u32[]{:S(2)}, u32[]{:S(2)}) %all-to-all-start.1) | async-done | bytes 262176 | tf_op jit(solution)/shard_map/all_to_all | solution.py:358
  58.8 0.0 copy-start.6
  58.8 0.6 collective-permute-start.1
  59.4 1.2 collective-permute-done.1.resid_b
  60.5 0.0 copy-start.8
  60.5 0.0 copy-done.6
  60.5 0.7 copy-done.8
  61.2 8.8 %gradient.1 = f32[128,4096]{1,0:T(8,128)} custom-call(bf16[1024,128]{1,0:T(8,128)(2,1)} %bitcast.22, bf16[1024,128]{1,0:T(8,128)(2,1)} %copy-done.8, bf16[1024,4096]{1,0:T(8,128)(2,1)} %get-tuple-element.67.rows_a, bf16[1024,4096]{1,0:T(8,128)(2,1)} %get-tuple-element.68.rows_b), custom_call_target="tpu_custom_call" | custom-call | flops 2147483648 | bytes 16777216 | tf_op jit(solution)/shard_map/gradient/pallas_call | solution.py:102
  70.0 0.0 copy-start.7
  70.0 2.8 %convert_bitcast_fusion = f16[16,8,4096]{2,1,0:T(8,128)(2,1)} fusion(f32[128,4096]{1,0:T(8,128)} %gradient.1), kind=kLoop, calls=%fused_computation.2 | loop fusion | flops 524288 | bytes 3145728 | tf_op jit(solution)/shard_map/reshape | solution.py:401
  72.8 6.8 %all-to-all-start.2 = ((f16[16,8,4096]{2,1,0:T(8,128)(2,1)}), f16[16,8,4096]{2,1,0:T(8,128)(2,1)}, u32[]{:S(2)}, u32[]{:S(2)}) async-start(f16[16,8,4096]{2,1,0:T(8,128)(2,1)} %convert_bitcast_fusion), calls=%async_computation.2 | async-start | bytes 2097152 | tf_op jit(solution)/shard_map/all_to_all | solution.py:403
  79.6 0.0 copy-start
  79.6 0.0 copy-start.2
  79.6 0.0 copy-done.7
  79.6 0.4 constant_dynamic-slice_fusion
  80.0 0.3 copy.15
  80.3 0.5 copy-done
  80.8 0.1 copy-done.2
  80.9 0.0 copy-start.1
  80.9 0.0 copy-start.5
  80.9 1.4 prefix.1.side
  82.3 13.0 %all-to-all-done.2 = f16[16,8,4096]{2,1,0:T(8,128)(2,1)} async-done(((f16[16,8,4096]{2,1,0:T(8,128)(2,1)}), f16[16,8,4096]{2,1,0:T(8,128)(2,1)}, u32[]{:S(2)}, u32[]{:S(2)}) %all-to-all-start.2) | async-done | bytes 1048608 | tf_op jit(solution)/shard_map/all_to_all | solution.py:403
  95.3 1.4 convert_reduce_fusion
  96.7 0.0 copy-done.1
  96.7 0.0 copy-done.5
  96.7 0.0 copy-start.3
  96.8 1.3 offset.1
  98.0 6.4 %all-to-all-start.3 = ((bf16[16,48,128]{2,1,0:T(8,128)(2,1)}), bf16[16,48,128]{2,1,0:T(8,128)(2,1)S(1)}, u32[]{:S(2)}, u32[]{:S(2)}) async-start(bf16[16,48,128]{2,1,0:T(8,128)(2,1)} %offset.1), calls=%async_computation.3 | async-start | bytes 393216 | tf_op jit(solution)/shard_map/all_to_all | solution.py:411
  104.5 0.0 copy-done.3
  104.5 8.5 %local_solve.1.solved = f32[8,4096]{1,0:T(8,128)} custom-call(f32[8,4096]{1,0:T(8,128)} %copy-done.3, f32[8,512,512]{2,1,0:T(8,128)} %inverse.5, f32[64,4096]{1,0:T(8,128)} %get-tuple-element.77.proj, f32[8,64,64]{2,1,0:T(8,128)} %get-tuple-element.72.step, f32[64,4096]{1,0:T(8,128)} %get-tuple-element.73.side), custom_call_target="tpu_custom_call" | custom-call | flops 100663296 | bytes 8388608 | tf_op jit(solution)/shard_map/local_solve/pallas_call | solution.py:262
  113.0 1.7 %all-to-all-done.3.messages = bf16[16,48,128]{2,1,0:T(8,128)(2,1)S(1)} async-done(((bf16[16,48,128]{2,1,0:T(8,128)(2,1)}), bf16[16,48,128]{2,1,0:T(8,128)(2,1)S(1)}, u32[]{:S(2)}, u32[]{:S(2)}) %all-to-all-start.3) | async-done | bytes 196640 | tf_op jit(solution)/shard_map/all_to_all | solution.py:411
  114.7 0.0 copy-start.4
  114.7 0.9 copy-done.4
  115.6 1.8 %finish.1 = f32[8,4224]{1,0:T(8,128)S(1)} custom-call(s32[1]{0:T(128)} %bitcast.place, bf16[16,48,128]{2,1,0:T(8,128)(2,1)S(1)} %all-to-all-done.3.messages, f32[8,4096]{1,0:T(8,128)S(1)} %copy-done.4, f32[64,4096]{1,0:T(8,128)S(1)} %prefix.1.side), custom_call_target="tpu_custom_call" | custom-call | tf_op jit(solution)/shard_map/finish/pallas_call | solution.py:321
  117.5 0.1 broadcast_in_dim.12
  117.6 20.5 %all_to_all.25 = f16[16,8,4224]{2,1,0:T(8,128)(2,1)S(1)} all-to-all(f16[16,8,4224]{2,1,0:T(8,128)(2,1)S(1)} %broadcast_in_dim.12), channel_id=1, replica_groups=mesh['samp'=16,'z'=8,'c'=2] {'samp'}, dimensions={0} | all-to-all | bytes 2162688 | tf_op jit(solution)/shard_map/all_to_all | solution.py:358
  138.1 0.1 bitcast_convert_fusion.powers.scaled
  138.2 2.7 %unscaled.1 = f32[4096,128]{1,0:T(8,128)} custom-call(f32[128,4224]{1,0:T(8,128)S(1)} %bitcast_convert_fusion.powers.scaled, f32[128,4224]{1,0:T(8,128)S(1)} %bitcast_convert_fusion.powers.scaled), custom_call_target="tpu_custom_call" | custom-call | tf_op jit(solution)/shard_map/unscaled/pallas_call | solution.py:342
  (3 shorter events, 0.1 us)
Async XLA Ops:
  8.9 12.1 %collective-permute-start = (f32[1024,128]{1,0:T(8,128)}, f32[1024,128]{1,0:T(8,128)S(1)}, u32[]{:S(2)}, u32[]{:S(2)}) collective-permute-start(f32[1024,128]{1,0:T(8,128)} %get-tuple-element.43), channel_id=1, source_target_pairs={{0,1},{1,0},{2,3},{3,2},{4,5},{5,4},{6,7},{7,6},{8,9},{9,8},{10,11... | collective-permute-start | bytes 1572872 | tf_op jit(solution)/shard_map/ppermute | solution.py:362
  22.8 18.8 %all-to-all-start = ((f16[8,128,128]{2,1,0:T(8,128)(2,1)}), f16[8,128,128]{2,1,0:T(8,128)(2,1)S(1)}, u32[]{:S(2)}, u32[]{:S(2)}) async-start(f16[8,128,128]{2,1,0:T(8,128)(2,1)} %bitcast.5), calls=%async_computation | async-start | bytes 524288 | tf_op jit(solution)/shard_map/all_to_all | solution.py:378
  43.2 15.6 %all-to-all-start.1 = ((bf16[8,128,128]{2,1,0:T(8,128)(2,1)}), bf16[8,128,128]{2,1,0:T(8,128)(2,1)S(1)}, u32[]{:S(2)}, u32[]{:S(2)}) async-start(bf16[8,128,128]{2,1,0:T(8,128)(2,1)} %broadcast_in_dim.11), calls=%async_computation.1 | async-start | bytes 524288 | tf_op jit(solution)/shard_map/all_to_all | solution.py:358
  58.8 1.8 %copy-start.6 = (bf16[8,128,128]{2,1,0:T(8,128)(2,1)}, bf16[8,128,128]{2,1,0:T(8,128)(2,1)S(1)}, u32[]{:S(2)}) copy-start(bf16[8,128,128]{2,1,0:T(8,128)(2,1)S(1)} %all-to-all-done.1) | copy-start | bytes 786436
  58.8 1.8 %collective-permute-start.1 = (bf16[1024,128]{1,0:T(8,128)(2,1)S(1)}, bf16[1024,128]{1,0:T(8,128)(2,1)S(1)}, u32[]{:S(2)}, u32[]{:S(2)}) collective-permute-start(bf16[1024,128]{1,0:T(8,128)(2,1)S(1)} %bitcast.21), channel_id=1, source_target_pairs={{0,1},{1,0},{2,3},{3,2},{4,5},{5,4},{6,7},{7,6},{8,9},{9,8},{10,11... | collective-permute-start | bytes 786440 | tf_op jit(solution)/shard_map/ppermute | solution.py:362
  60.5 0.7 copy-start.8
  70.0 9.6 %copy-start.7 = (bf16[4096,128]{1,0:T(8,128)(2,1)S(1)}, bf16[4096,128]{1,0:T(8,128)(2,1)}, u32[]{:S(2)}) copy-start(bf16[4096,128]{1,0:T(8,128)(2,1)} %coeffs.3) | copy-start | bytes 3145732
  72.8 22.5 %all-to-all-start.2 = ((f16[16,8,4096]{2,1,0:T(8,128)(2,1)}), f16[16,8,4096]{2,1,0:T(8,128)(2,1)}, u32[]{:S(2)}, u32[]{:S(2)}) async-start(f16[16,8,4096]{2,1,0:T(8,128)(2,1)} %convert_bitcast_fusion), calls=%async_computation.2 | async-start | bytes 2097152 | tf_op jit(solution)/shard_map/all_to_all | solution.py:403
  79.6 1.2 copy-start
  79.6 1.3 copy-start.2
  80.9 15.8 %copy-start.1 = (f32[64,4096]{1,0:T(8,128)S(1)}, f32[64,4096]{1,0:T(8,128)}, u32[]{:S(2)}) copy-start(f32[64,4096]{1,0:T(8,128)} %get-tuple-element.75.suffix_proj) | copy-start | bytes 3145732
  80.9 15.8 %copy-start.5 = (f32[64,64]{1,0:T(8,128)S(1)}, f32[64,64]{1,0:T(8,128)}, u32[]{:S(2)}) copy-start(f32[64,64]{1,0:T(8,128)} %get-tuple-element.76.transfer) | copy-start | bytes 49156
  96.7 7.7 %copy-start.3 = (f32[8,4096]{1,0:T(8,128)}, f32[8,4096]{1,0:T(8,128)S(1)}, u32[]{:S(2)}) copy-start(f32[8,4096]{1,0:T(8,128)S(1)} %bitcast_add_fusion.grad) | copy-start | bytes 393220
  98.0 16.7 %all-to-all-start.3 = ((bf16[16,48,128]{2,1,0:T(8,128)(2,1)}), bf16[16,48,128]{2,1,0:T(8,128)(2,1)S(1)}, u32[]{:S(2)}, u32[]{:S(2)}) async-start(bf16[16,48,128]{2,1,0:T(8,128)(2,1)} %offset.1), calls=%async_computation.3 | async-start | bytes 393216 | tf_op jit(solution)/shard_map/all_to_all | solution.py:411
  114.7 0.9 copy-start.4

commit v4 on v3

--- a/solution.py
+++ b/solution.py
@@ -37,76 +37,100 @@
     return dot(ah, bh, ca, cb) + (dot(ah, bl, ca, cb) + dot(al, bh, ca, cb))
 
 
-def predict_kernel(width, half, points_t, centers_t, coeffs, kernel_out, pred):
-    x_t = points_t[...].astype(f32)
-    x32 = x_t.T
-    x = x32.astype(bf16)
-    p = jnp.sum(x32 * x32, axis=1, keepdims=True) * (-LOG2E / D)
+def with_norms(columns, left):
+    half = jnp.sum(columns * columns, axis=0, keepdims=True) * -0.5
+    high = half.astype(bf16).astype(f32)
+    rest = half - high
+    middle = rest.astype(bf16).astype(f32)
+    n = columns.shape[1]
+    ones = [jnp.ones((1, n), f32)] * 3
+    parts = [high, middle, rest - middle]
+    extra = parts + ones if left else ones + parts
+    return jnp.concatenate([columns, *extra, jnp.zeros((2, n), f32)])
+
+
+def predict_kernel(width, half, points_t, centers, coeffs, stored, pred, *kept):
+    i = pl.program_id(0)
+    rows = pred.shape[0]
+    if kept:
+        centers_t, (centers, coeffs_v) = centers, kept
+
+        @pl.when(i == 0)
+        def _():
+            centers[...] = with_norms(centers_t[...].astype(f32), False).astype(bf16)
+            coeffs_v[...] = coeffs[...]
+
+    x = with_norms(points_t[...].astype(f32), True).T.astype(bf16)
+    here = pl.ds(pl.multiple_of(i * rows, rows), rows)
     total = None
-    for at in range(0, centers_t.shape[1], width):
-        c = centers_t[:, at : at + width]
-        c32 = c.astype(f32)
-        q = jnp.sum(c32 * c32, axis=0, keepdims=True) * (-LOG2E / D)
-        exponent = dot(x, c, 1, 0) * (2 * LOG2E / D) + (p + q)
-        k = jnp.exp2(exponent).astype(bf16)
-        kernel_out[:, at : at + width] = k
+    for at in range(0, centers.shape[1], width):
+        scaled = dot(x, centers[:, at : at + width], 1, 0) * (2 * LOG2E / D)
+        k = jnp.exp2(scaled).astype(bf16)
+        stored[here, at : at + width] = k
         part = dot(k, coeffs[at : at + width, :], 1, 0)
         total = part if total is None else total + part
     pred[...] = total
 
 
-def predict(half, points_t, centers_t, coeffs, rows=256, width=256):
-    n, m, labels = points_t.shape[1] // 2, centers_t.shape[1], coeffs.shape[1]
+vmem = pl.BlockSpec(memory_space=pltpu.VMEM)
+
+
+def predict(half, points_t, centers, coeffs, first, rows=512, width=256):
+    n, m, labels = points_t.shape[1] // 2, centers.shape[1], coeffs.shape[1]
     steps = n // rows
+    whole = lambda i, half: (0, 0)
+    outs = [pltpu.VMEM((n, m), bf16), jax.ShapeDtypeStruct((n, labels), f32)]
+    if first:
+        outs += [pltpu.VMEM((D + 8, m), bf16), pltpu.VMEM((m, labels), bf16)]
     return pl.pallas_call(
         functools.partial(predict_kernel, width),
         grid_spec=pltpu.PrefetchScalarGridSpec(
             num_scalar_prefetch=1,
             grid=(steps,),
-            in_specs=[
-                pl.BlockSpec((D, rows), lambda i, half: (0, half[0] * steps + i)),
-                pl.BlockSpec((D, m), lambda i, half: (0, 0)),
-                pl.BlockSpec((m, labels), lambda i, half: (0, 0)),
-            ],
-            out_specs=[
-                pl.BlockSpec((rows, m), lambda i, half: (i, 0)),
-                pl.BlockSpec((rows, labels), lambda i, half: (i, 0)),
-            ],
-        ),
-        out_shape=[
-            jax.ShapeDtypeStruct((n, m), bf16),
-            jax.ShapeDtypeStruct((n, labels), f32),
-        ],
-        compiler_params=pltpu.CompilerParams(vmem_limit_bytes=60 << 20),
+            in_specs=[pl.BlockSpec((D, rows), lambda i, half: (0, half[0] * steps + i))]
+            + (
+                [pl.BlockSpec((D, m), whole), pl.BlockSpec((m, labels), whole)]
+                if first
+                else [vmem, vmem]
+            ),
+            out_specs=[vmem, pl.BlockSpec((rows, labels), lambda i, half: (i, 0))]
+            + ([vmem, vmem] if first else []),
+        ),
+        out_shape=outs,
+        compiler_params=pltpu.CompilerParams(vmem_limit_bytes=20 << 20),
         cost_estimate=pl.CostEstimate(
             flops=2 * n * m * (D + labels), bytes_accessed=2 * n * m, transcendentals=n * m
         ),
         name="predict",
-    )(half.reshape(1), points_t, centers_t, coeffs)
+    )(half.reshape(1), points_t, centers, coeffs)
 
 
 def gradient_kernel(resid_a, resid_b, rows_a, rows_b, out, turned_a, turned_b):
-    @pl.when(pl.program_id(0) == 0)
+    i = pl.program_id(0)
+
+    @pl.when(i == 0)
     def _():
         turned_a[...] = resid_a[...].astype(f32).T.astype(bf16)
         turned_b[...] = resid_b[...].astype(f32).T.astype(bf16)
 
-    out[...] = dot(turned_a[...], rows_a[...], 1, 0) + dot(turned_b[...], rows_b[...], 1, 0)
+    cols = out.shape[1] // pl.num_programs(0)
+    here = pl.ds(pl.multiple_of(i * cols, cols), cols)
+    out[:, here] = dot(turned_a[...], rows_a[:, here], 1, 0) + dot(
+        turned_b[...], rows_b[:, here], 1, 0
+    )
 
 
 def gradient_t(resid_a, resid_b, stored_a, stored_b, cols=1024):
     n, labels = resid_a.shape
     m = stored_a.shape[1]
-    whole = pl.BlockSpec((n, labels), lambda i: (0, 0))
-    part = pl.BlockSpec((n, cols), lambda i: (0, i))
     return pl.pallas_call(
         gradient_kernel,
         grid=(m // cols,),
-        in_specs=[whole, whole, part, part],
-        out_specs=pl.BlockSpec((labels, cols), lambda i: (0, i)),
-        out_shape=jax.ShapeDtypeStruct((labels, m), f32),
+        in_specs=[vmem, vmem, vmem, vmem],
+        out_specs=vmem,
+        out_shape=pltpu.VMEM((labels, m), f32),
         scratch_shapes=[pltpu.VMEM((labels, n), bf16)] * 2,
-        compiler_params=pltpu.CompilerParams(vmem_limit_bytes=56 << 20),
+        compiler_params=pltpu.CompilerParams(vmem_limit_bytes=16 << 20),
         cost_estimate=pl.CostEstimate(
             flops=4 * n * m * labels, bytes_accessed=4 * n * m, transcendentals=0
         ),
@@ -143,8 +167,8 @@
 
 def prepare(block_ranks, diag_inv, left_t, right_t, rates, earlier=None):
     count = diag_inv.shape[0]
-    steps = count // 2
-    last = count - 1 if earlier is None else steps - 1
+    steps = count
+    last = count - 1
     back = lambda i, ranks: (last - i, 0, 0)
     wide = lambda i, ranks: (0, last - i)
     square = pl.BlockSpec((R, R), lambda i, ranks: (0, 0))
@@ -317,7 +341,6 @@
 
 def finish(place, messages, solved, side):
     labels, m = solved.shape
-    vmem = pl.BlockSpec(memory_space=pltpu.VMEM)
     return pl.pallas_call(
         finish_kernel,
         grid_spec=pltpu.PrefetchScalarGridSpec(
@@ -370,39 +393,38 @@
     place = chip * 2 + core
     share = n // (2 * chips)
 
-    points_t, centers_t = points.T, centers.T
-    stored_b, pred_b = predict(1 - core, points_t, centers_t, coeffs)
+    first = core * (n // 2) + chip * share
+    own_targets = lax.dynamic_slice_in_dim(targets, first, share, 0)
+    points, own_targets = lax.optimization_barrier((points, own_targets))
+    in_hbm = lambda array: pltpu.with_memory_space_constraint(array, pltpu.HBM)
+    diag_inv, points_t, centers_t = in_hbm(diag_inv), in_hbm(points.T), in_hbm(centers.T)
+    stored_b, pred_b, extended, coeffs_v = predict(
+        1 - core, points_t, centers_t, in_hbm(coeffs), True
+    )
     from_partner = to_partner(pred_b)
-    stored_a, pred_a = predict(core, points_t, centers_t, coeffs)
+    stored_a, pred_a = predict(core, points_t, extended, coeffs_v, False)
     pair_sum = (pred_a + from_partner).astype(wire).reshape(chips, share, labels)
     arrived = lax.all_to_all(pair_sum, "z", 0, 0, tiled=True)
-    factors = (
+    pred_own = arrived.astype(f32).sum(axis=0)
+    resid = (jax.nn.sigmoid(pred_own) - own_targets.astype(f32)).astype(bf16)
+    resid_a = sent_to_all(resid, "z").reshape(n // 2, labels)
+    resid_b = to_partner(resid_a)
+
+    partial = gradient_t(resid_a, resid_b, stored_a, stored_b)
+    own = labels // samp
+    sent = partial.astype(wire).reshape(samp, own, m)
+    sent, block_ranks = lax.optimization_barrier((sent, block_ranks))
+    arrived = lax.all_to_all(sent, "samp", 0, 0, tiled=True)
+    prepared = prepare(
         block_ranks,
         diag_inv,
         jnp.swapaxes(low_left, 1, 2),
         jnp.swapaxes(low_right, 1, 2),
         decay_rates,
     )
-    halfway = prepare(*factors)
-    arrived, halfway = lax.optimization_barrier((arrived, halfway))
-    pred_own = arrived.astype(f32).sum(axis=0)
-    first = core * (n // 2) + chip * share
-    own_targets = lax.dynamic_slice_in_dim(targets, first, share, 0)
-    resid = (jax.nn.sigmoid(pred_own) - own_targets.astype(f32)).astype(bf16)
-    resid, halfway = lax.optimization_barrier((resid, halfway))
-    resid_a = sent_to_all(resid, "z").reshape(n // 2, labels)
-    prepared = prepare(*factors, halfway)
-    resid_a, prepared = lax.optimization_barrier((resid_a, prepared))
+    side_prefix = prefix_side(prepared[1], prepared[2])
+    arrived, prepared, side_prefix = lax.optimization_barrier((arrived, prepared, side_prefix))
     proj, step, side, suffix_proj, transfer = prepared
-    resid_b = to_partner(resid_a)
-
-    partial = gradient_t(resid_a, resid_b, stored_a, stored_b)
-    own = labels // samp
-    sent = partial.astype(wire).reshape(samp, own, m)
-    sent, step_late, side_late = lax.optimization_barrier((sent, step, side))
-    arrived = lax.all_to_all(sent, "samp", 0, 0, tiled=True)
-    side_prefix = prefix_side(step_late, side_late)
-    arrived, side_prefix = lax.optimization_barrier((arrived, side_prefix))
     own_coeffs = lax.dynamic_slice_in_dim(coeffs, lax.axis_index("samp") * own, own, 1).T
     scaling = 1.0 / math.sqrt(n * samp)
     grad = arrived.astype(f32).sum(axis=0) * scaling + ridge_weight * own_coeffs.astype(f32)

time: 142 us -> 126 us (0.89)
  blocking collectives: 20.5 us -> 54.7 us
  waiting for transfers between devices: 27.1 us -> 3.2 us
  Pallas kernels: 55.6 us -> 42.5 us
  starting transfers between devices: 26.9 us -> 17.1 us
  other arithmetic: 6.98 us -> 2.77 us
    all_to_all x0 -> x1, blocking collectives: none -> 18.6 us  [body(): arrived = lax.all_to_all(pair_sum, 'z', 0, 0, tiled=True)]
    all_to_all x1 -> x2, blocking collectives: 20.5 us -> 36 us  [sent_to_all(): return lax.all_to_all(copies, axis, split_axis=0, concat_axis=0, tiled=True)]
    all_to_all x1, waiting for transfers between devices: 13 us -> 0.29 us  [body(): arrived = lax.all_to_all(sent, 'samp', 0, 0, tiled=True)]
    all_to_all x2 -> x0, waiting for transfers between devices: 11.2 us -> none  [the longest x1 5.72 us: body(): arrived = lax.all_to_all(pair_sum, 'z', 0, 0, tiled=True)]
    all_to_all x2 -> x0, starting transfers between devices: 9.88 us -> none  [the longest x1 6.47 us: body(): arrived = lax.all_to_all(pair_sum, 'z', 0, 0, tiled=True)]
    pallas_call x1, Pallas kernels: 8.78 us -> 3.15 us  [gradient_t(): pl.pallas_call(gradient_kernel, grid=(m // cols,), in_specs=[vmem, vmem,...]
    pallas_call x2, Pallas kernels: 17.8 us -> 12.6 us  [predict(): pl.pallas_call(functools.partial(predict_kernel, width), grid_spec=pltpu....]
    pallas_call x2 -> x1, Pallas kernels: 13.3 us -> 11.1 us  [prepare(): pl.pallas_call(functools.partial(prepare_kernel, last), grid_spec=pltpu.P...]
  transfers between devices with their start and end apart: 6 -> 4, of which waited for: 5 -> 3; matrix products, arithmetic and copies ran while one was open for 0% -> 1% of each run, Pallas kernels for 23% -> 22%
where the time goes in v4:
time: 126 us; the launch traced here: 125 us
  blocking collectives  54.7 us (43%)
  Pallas kernels  42.5 us (34%)
  starting transfers between devices  17.1 us (14%)
  local copies, waits for them, and re-layouts  4.91 us (4%)
  waiting for transfers between devices  3.2 us (3%)
  other arithmetic  2.77 us (2%)
    all_to_all x2, blocking collectives, sent_to_all(): return lax.all_to_all(copies, axis, split_axis=0, concat_axis=0, tiled=True)  36 us
    all_to_all x1, blocking collectives, body(): arrived = lax.all_to_all(pair_sum, 'z', 0, 0, tiled=True)  18.6 us
    pallas_call x2, Pallas kernels, predict(): pl.pallas_call(functools.partial(predict_kernel, width), grid_spec=pltpu....  12.6 us
    pallas_call x1, Pallas kernels, prepare(): pl.pallas_call(functools.partial(prepare_kernel, last), grid_spec=pltpu.P...  11.1 us
    pallas_call x1, Pallas kernels, local_solve(): pl.pallas_call(local_kernel, grid=(count,), in_specs=[pl.BlockSpec((label...  8.52 us
    all_to_all x1, starting transfers between devices, body(): arrived = lax.all_to_all(sent, 'samp', 0, 0, tiled=True)  6.8 us
    all_to_all x1, starting transfers between devices, body(): messages = lax.all_to_all(messages, ('z', 'c'), 0, 0, tiled=True)  6.42 us
    unnamed x17, local copies, waits for them, and re-layouts  4.44 us
  transfers between devices with their start and end apart: 4, of which 3 were waited for; matrix products, arithmetic and copies ran while one was open for 1% of the time, Pallas kernels for 22%

profile of v4, /device:TPU:1, one launch (start us, length us, event | category | flops | bytes accessed | tf_op | source)
XLA Modules:
  0.0 125.4 jit_solution(9927458543649808476)
XLA Ops:
  0.0 0.0 copy-start
  0.0 1.0 copy-done
  1.0 6.6 %predict.2 = (bf16[1024,4096]{1,0:T(8,128)(2,1)S(1)}, f32[1024,128]{1,0:T(8,128)S(1)}, bf16[72,4096]{1,0:T(8,128)(2,1)S(1)}, bf16[4096,128]{1,0:T(8,128)(2,1)S(1)}) custom-call(s32[1]{0:T(128)} %bitcast.3.half, bf16[64,2048]{1,0:T(8,128)(2,1)} %bitcast.24, bf16[64,4096]{1,0:T(8,128)(2,1)} %bitcast.23, bf16[4096,128]{1,0:T(8,128)(2,1)} %coeffs.1), custom_call_target="tpu_custom_call" | custom-call | flops 1610612736 | bytes 8388608 | tf_op jit(solution)/shard_map/predict/pallas_call | solution.py:85
  7.7 3.3 %collective-permute-start = (f32[1024,128]{1,0:T(8,128)S(1)}, f32[1024,128]{1,0:T(8,128)S(1)}, u32[]{:S(2)}, u32[]{:S(2)}) collective-permute-start(f32[1024,128]{1,0:T(8,128)S(1)} %get-tuple-element.31), channel_id=1, source_target_pairs={{0,1},{1,0},{2,3},{3,2},{4,5},{5,4},{6,7},{7,6},{8,9},{9,8},{10,11... | collective-permute-start | bytes 1572872 | tf_op jit(solution)/shard_map/ppermute | solution.py:385
  11.0 5.9 %predict.3 = (bf16[1024,4096]{1,0:T(8,128)(2,1)S(1)}, f32[1024,128]{1,0:T(8,128)S(1)}) custom-call(s32[1]{0:T(128)} %bitcast.1.half, bf16[64,2048]{1,0:T(8,128)(2,1)} %bitcast.25, bf16[72,4096]{1,0:T(8,128)(2,1)S(1)} %get-tuple-element.28.centers, bf16[4096,128]{1,0:T(8,128)(2,1)S(1)} %get-tuple-element.29.coeffs), custom_call_target="tpu_custom_call" | custom-call | flops 1610612736 | bytes 8388608 | tf_op jit(solution)/shard_map/predict/pallas_call | solution.py:85
  16.9 0.0 collective-permute-done
  16.9 0.1 add_convert_fusion
  17.0 18.6 %all_to_all.25 = f16[8,128,128]{2,1,0:T(8,128)(2,1)S(1)} all-to-all(f16[8,128,128]{2,1,0:T(8,128)(2,1)S(1)} %bitcast.19), channel_id=1, replica_groups=mesh['samp'=16,'z'=8,'c'=2] {'z'}, dimensions={0} | all-to-all | bytes 524288 | tf_op jit(solution)/shard_map/all_to_all | solution.py:407
  35.8 14.6 %all_to_all.26 = bf16[8,128,128]{2,1,0:T(8,128)(2,1)S(1)} all-to-all(bf16[8,128,128]{2,1,0:T(8,128)(2,1)S(1)} %broadcast_in_dim.9), channel_id=1, replica_groups=mesh['samp'=16,'z'=8,'c'=2] {'z'}, dimensions={0} | all-to-all | bytes 524288 | tf_op jit(solution)/shard_map/all_to_all | solution.py:381
  50.4 0.6 collective-permute-start.1
  51.0 1.2 collective-permute-done.1.resid_b
  52.2 3.2 %gradient.1 = f32[128,4096]{1,0:T(8,128)S(1)} custom-call(bf16[1024,128]{1,0:T(8,128)(2,1)S(1)} %bitcast.18, bf16[1024,128]{1,0:T(8,128)(2,1)S(1)} %collective-permute-done.1.resid_b, bf16[1024,4096]{1,0:T(8,128)(2,1)S(1)} %get-tuple-element.33.rows_a, bf16[1024,4096]{1,0:T(8,128)(2,1)S(1)} %get-tuple-element.34.rows_b), custom_call_target="tpu_custom_call" | custom-call | flops 2147483648 | bytes 16777216 | tf_op jit(solution)/shard_map/gradient/pallas_call | solution.py:126
  55.3 0.0 copy-start.7
  55.3 1.1 convert_bitcast_fusion
  56.4 6.8 %all-to-all-start.2 = ((f16[16,8,4096]{2,1,0:T(8,128)(2,1)}), f16[16,8,4096]{2,1,0:T(8,128)(2,1)}, u32[]{:S(2)}, u32[]{:S(2)}) async-start(f16[16,8,4096]{2,1,0:T(8,128)(2,1)} %convert_bitcast_fusion), calls=%async_computation.2 | async-start | bytes 2097152 | tf_op jit(solution)/shard_map/all_to_all | solution.py:417
  63.2 0.0 copy-done.7
  63.3 0.4 constant_dynamic-slice_fusion
  63.6 0.3 copy.11
  63.9 11.1 %prepare.1 = (f32[64,4096]{1,0:T(8,128)}, f32[8,64,64]{2,1,0:T(8,128)}, f32[64,4096]{1,0:T(8,128)}, f32[64,4096]{1,0:T(8,128)}, f32[64,64]{1,0:T(8,128)}) custom-call(s32[8]{0:T(128)} %ranks, f32[8,512,512]{2,1,0:T(8,128)} %inverse.3, bf16[8,64,512]{2,1,0:T(8,128)(2,1)} %bitcast.20, bf16[8,64,512]{2,1,0:T(8,128)(2,1)} %bitcast.21, f32[8,1,64]{2,1,0:T(1,128)} %bitcast.22), custom_call_target="tpu_custom_call" | custom-call | flops 1073741824 | bytes 12582912 | tf_op jit(solution)/shard_map/prepare/pallas_call | solution.py:177
  75.1 0.0 copy-start.1
  75.1 1.2 copy-done.1
  76.3 0.0 copy-start.3
  76.3 0.9 copy-done.3
  77.3 0.0 copy-start.4
  77.3 0.0 copy-start.6
  77.3 1.4 %prefix.1.side = f32[64,4096]{1,0:T(8,128)S(1)} custom-call(f32[8,64,64]{2,1,0:T(8,128)S(1)} %copy-done.3, f32[64,4096]{1,0:T(8,128)S(1)} %copy-done.1), custom_call_target="tpu_custom_call" | custom-call | flops 100663296 | bytes 2097152 | tf_op jit(solution)/shard_map/prefix/pallas_call | solution.py:228
  78.7 0.3 all-to-all-done.2
  78.9 1.4 %convert_reduce_fusion = f32[8,4096]{1,0:T(8,128)S(1)} fusion(f16[16,8,4096]{2,1,0:T(8,128)(2,1)} %all-to-all-done.2), kind=kLoop, calls=%fused_computation | loop fusion | flops 1015808 | bytes 1179648 | tf_op jit(solution)/shard_map/reduce_sum | solution.py:430
  80.4 0.0 copy-done.4
  80.4 0.0 copy-done.6
  80.4 0.0 copy-start.2
  80.4 1.3 %offset.1 = bf16[16,48,128]{2,1,0:T(8,128)(2,1)} custom-call(f32[8,4096]{1,0:T(8,128)S(1)} %bitcast_add_fusion.grad, f32[64,4096]{1,0:T(8,128)S(1)} %copy-done.4, f32[64,64]{1,0:T(8,128)S(1)} %copy-done.6), custom_call_target="tpu_custom_call" | custom-call | tf_op jit(solution)/shard_map/offset/pallas_call | solution.py:255
  81.7 6.4 %all-to-all-start.3 = ((bf16[16,48,128]{2,1,0:T(8,128)(2,1)}), bf16[16,48,128]{2,1,0:T(8,128)(2,1)S(1)}, u32[]{:S(2)}, u32[]{:S(2)}) async-start(bf16[16,48,128]{2,1,0:T(8,128)(2,1)} %offset.1), calls=%async_computation.3 | async-start | bytes 393216 | tf_op jit(solution)/shard_map/all_to_all | solution.py:433
  88.1 0.0 copy-done.2
  88.1 8.5 %local_solve.1.solved = f32[8,4096]{1,0:T(8,128)} custom-call(f32[8,4096]{1,0:T(8,128)} %copy-done.2, f32[8,512,512]{2,1,0:T(8,128)} %inverse.3, f32[64,4096]{1,0:T(8,128)} %get-tuple-element.45.proj, f32[8,64,64]{2,1,0:T(8,128)} %get-tuple-element.46.step, f32[64,4096]{1,0:T(8,128)} %get-tuple-element.47.side), custom_call_target="tpu_custom_call" | custom-call | flops 100663296 | bytes 8388608 | tf_op jit(solution)/shard_map/local_solve/pallas_call | solution.py:286
  96.6 1.7 %all-to-all-done.3.messages = bf16[16,48,128]{2,1,0:T(8,128)(2,1)S(1)} async-done(((bf16[16,48,128]{2,1,0:T(8,128)(2,1)}), bf16[16,48,128]{2,1,0:T(8,128)(2,1)S(1)}, u32[]{:S(2)}, u32[]{:S(2)}) %all-to-all-start.3) | async-done | bytes 196640 | tf_op jit(solution)/shard_map/all_to_all | solution.py:433
  98.4 0.0 copy-start.5
  98.4 0.9 copy-done.5
  99.3 1.8 %finish.1 = f32[8,4224]{1,0:T(8,128)S(1)} custom-call(s32[1]{0:T(128)} %bitcast.place, bf16[16,48,128]{2,1,0:T(8,128)(2,1)S(1)} %all-to-all-done.3.messages, f32[8,4096]{1,0:T(8,128)S(1)} %copy-done.5, f32[64,4096]{1,0:T(8,128)S(1)} %prefix.1.side), custom_call_target="tpu_custom_call" | custom-call | tf_op jit(solution)/shard_map/finish/pallas_call | solution.py:344
  101.1 0.1 broadcast_in_dim.11
  101.2 21.4 %all_to_all.27 = f16[16,8,4224]{2,1,0:T(8,128)(2,1)S(1)} all-to-all(f16[16,8,4224]{2,1,0:T(8,128)(2,1)S(1)} %broadcast_in_dim.11), channel_id=1, replica_groups=mesh['samp'=16,'z'=8,'c'=2] {'samp'}, dimensions={0} | all-to-all | bytes 2162688 | tf_op jit(solution)/shard_map/all_to_all | solution.py:381
  122.6 0.1 bitcast_convert_fusion.powers.scaled
  122.8 2.7 %unscaled.1 = f32[4096,128]{1,0:T(8,128)} custom-call(f32[128,4224]{1,0:T(8,128)S(1)} %bitcast_convert_fusion.powers.scaled, f32[128,4224]{1,0:T(8,128)S(1)} %bitcast_convert_fusion.powers.scaled), custom_call_target="tpu_custom_call" | custom-call | tf_op jit(solution)/shard_map/unscaled/pallas_call | solution.py:365
  (6 shorter events, 0.1 us)
Async XLA Ops:
  0.0 1.0 copy-start
  7.7 9.2 %collective-permute-start = (f32[1024,128]{1,0:T(8,128)S(1)}, f32[1024,128]{1,0:T(8,128)S(1)}, u32[]{:S(2)}, u32[]{:S(2)}) collective-permute-start(f32[1024,128]{1,0:T(8,128)S(1)} %get-tuple-element.31), channel_id=1, source_target_pairs={{0,1},{1,0},{2,3},{3,2},{4,5},{5,4},{6,7},{7,6},{8,9},{9,8},{10,11... | collective-permute-start | bytes 1572872 | tf_op jit(solution)/shard_map/ppermute | solution.py:385
  50.4 1.8 %collective-permute-start.1 = (bf16[1024,128]{1,0:T(8,128)(2,1)S(1)}, bf16[1024,128]{1,0:T(8,128)(2,1)S(1)}, u32[]{:S(2)}, u32[]{:S(2)}) collective-permute-start(bf16[1024,128]{1,0:T(8,128)(2,1)S(1)} %bitcast.17), channel_id=1, source_target_pairs={{0,1},{1,0},{2,3},{3,2},{4,5},{5,4},{6,7},{7,6},{8,9},{9,8},{10,11... | collective-permute-start | bytes 786440 | tf_op jit(solution)/shard_map/ppermute | solution.py:385
  55.3 7.9 %copy-start.7 = (bf16[4096,128]{1,0:T(8,128)(2,1)S(1)}, bf16[4096,128]{1,0:T(8,128)(2,1)}, u32[]{:S(2)}) copy-start(bf16[4096,128]{1,0:T(8,128)(2,1)} %coeffs.1) | copy-start | bytes 3145732
  56.4 22.5 %all-to-all-start.2 = ((f16[16,8,4096]{2,1,0:T(8,128)(2,1)}), f16[16,8,4096]{2,1,0:T(8,128)(2,1)}, u32[]{:S(2)}, u32[]{:S(2)}) async-start(f16[16,8,4096]{2,1,0:T(8,128)(2,1)} %convert_bitcast_fusion), calls=%async_computation.2 | async-start | bytes 2097152 | tf_op jit(solution)/shard_map/all_to_all | solution.py:417
  75.1 1.2 copy-start.1
  76.3 0.9 copy-start.3
  77.3 3.1 %copy-start.4 = (f32[64,4096]{1,0:T(8,128)S(1)}, f32[64,4096]{1,0:T(8,128)}, u32[]{:S(2)}) copy-start(f32[64,4096]{1,0:T(8,128)} %get-tuple-element.43.suffix_proj) | copy-start | bytes 3145732
  77.3 3.1 %copy-start.6 = (f32[64,64]{1,0:T(8,128)S(1)}, f32[64,64]{1,0:T(8,128)}, u32[]{:S(2)}) copy-start(f32[64,64]{1,0:T(8,128)} %get-tuple-element.44.transfer) | copy-start | bytes 49156
  80.4 7.7 %copy-start.2 = (f32[8,4096]{1,0:T(8,128)}, f32[8,4096]{1,0:T(8,128)S(1)}, u32[]{:S(2)}) copy-start(f32[8,4096]{1,0:T(8,128)S(1)} %bitcast_add_fusion.grad) | copy-start | bytes 393220
  81.7 16.7 %all-to-all-start.3 = ((bf16[16,48,128]{2,1,0:T(8,128)(2,1)}), bf16[16,48,128]{2,1,0:T(8,128)(2,1)S(1)}, u32[]{:S(2)}, u32[]{:S(2)}) async-start(bf16[16,48,128]{2,1,0:T(8,128)(2,1)} %offset.1), calls=%async_computation.3 | async-start | bytes 393216 | tf_op jit(solution)/shard_map/all_to_all | solution.py:433
  98.4 0.9 copy-start.5

commit v5 on v4

--- a/solution.py
+++ b/solution.py
@@ -75,7 +75,7 @@
 vmem = pl.BlockSpec(memory_space=pltpu.VMEM)
 
 
-def predict(half, points_t, centers, coeffs, first, rows=512, width=256):
+def predict(half, points_t, centers, coeffs, first, rows=1024, width=256):
     n, m, labels = points_t.shape[1] // 2, centers.shape[1], coeffs.shape[1]
     steps = n // rows
     whole = lambda i, half: (0, 0)
@@ -105,47 +105,72 @@
     )(half.reshape(1), points_t, centers, coeffs)
 
 
-def gradient_kernel(resid_a, resid_b, rows_a, rows_b, out, turned_a, turned_b):
+def residual_kernel(share_at, pred, targets, out):
+    resid = (jax.nn.sigmoid(pred[...]) - targets[...].astype(f32)).astype(bf16)
+    for e in range(out.shape[0]):
+        out[e] = resid
+
+
+def residual_copies(share_at, pred, targets, copies):
+    n, labels = pred.shape
+    return pl.pallas_call(
+        residual_kernel,
+        grid_spec=pltpu.PrefetchScalarGridSpec(
+            num_scalar_prefetch=1,
+            grid=(1,),
+            in_specs=[
+                pl.BlockSpec((n, labels), lambda i, share_at: (0, 0)),
+                pl.BlockSpec((n, labels), lambda i, share_at: (share_at[0], 0)),
+            ],
+            out_specs=pl.BlockSpec((copies, n, labels), lambda i, share_at: (0, 0, 0)),
+        ),
+        out_shape=jax.ShapeDtypeStruct((copies, n, labels), bf16),
+        compiler_params=pltpu.CompilerParams(vmem_limit_bytes=8 << 20),
+        name="residual",
+    )(share_at.reshape(1), pred, targets)
+
+
+def gradient_kernel(resid, rows, *refs):
+    *earlier, out, turned = refs
     i = pl.program_id(0)
 
     @pl.when(i == 0)
     def _():
-        turned_a[...] = resid_a[...].astype(f32).T.astype(bf16)
-        turned_b[...] = resid_b[...].astype(f32).T.astype(bf16)
+        turned[...] = resid[...].astype(f32).T.astype(bf16)
 
     cols = out.shape[1] // pl.num_programs(0)
     here = pl.ds(pl.multiple_of(i * cols, cols), cols)
-    out[:, here] = dot(turned_a[...], rows_a[:, here], 1, 0) + dot(
-        turned_b[...], rows_b[:, here], 1, 0
-    )
-
-
-def gradient_t(resid_a, resid_b, stored_a, stored_b, cols=1024):
-    n, labels = resid_a.shape
-    m = stored_a.shape[1]
+    part = dot(turned[...], rows[:, here], 1, 0)
+    out[:, here] = earlier[0][:, here] + part if earlier else part
+
+
+def gradient_t(resid, stored, *earlier, cols=2048):
+    n, labels = resid.shape
+    m = stored.shape[1]
     return pl.pallas_call(
         gradient_kernel,
         grid=(m // cols,),
-        in_specs=[vmem, vmem, vmem, vmem],
+        in_specs=[vmem] * (2 + len(earlier)),
         out_specs=vmem,
         out_shape=pltpu.VMEM((labels, m), f32),
-        scratch_shapes=[pltpu.VMEM((labels, n), bf16)] * 2,
+        scratch_shapes=[pltpu.VMEM((labels, n), bf16)],
         compiler_params=pltpu.CompilerParams(vmem_limit_bytes=16 << 20),
         cost_estimate=pl.CostEstimate(
-            flops=4 * n * m * labels, bytes_accessed=4 * n * m, transcendentals=0
+            flops=2 * n * m * labels, bytes_accessed=2 * n * m, transcendentals=0
         ),
         name="gradient",
-    )(resid_a, resid_b, stored_a, stored_b)
-
-
-def prepare_kernel(last, ranks, inverse, left_t, right_t, rates, *refs):
-    proj, step, side, suffix_proj, transfer, acc = refs[-6:]
+    )(resid, stored, *earlier)
+
+
+def prepare_kernel(
+    last, ranks, inverse, left_t, right_t, rates, proj, step, side, suffix_proj, transfer, acc
+):
     i = pl.program_id(0)
     eye = lax.broadcasted_iota(jnp.int32, (R, R), 0) == lax.broadcasted_iota(jnp.int32, (R, R), 1)
 
     @pl.when(i == 0)
     def _():
-        acc[...] = eye.astype(f32) if len(refs) == 6 else refs[0][...]
+        acc[...] = eye.astype(f32)
 
     kept = lax.broadcasted_iota(jnp.int32, (R, B), 0) < ranks[last - i]
     left = jnp.where(kept, left_t[0].astype(f32), 0.0).astype(bf16)
@@ -165,33 +190,29 @@
     transfer[...] = suffix
 
 
-def prepare(block_ranks, diag_inv, left_t, right_t, rates, earlier=None):
+def prepare(block_ranks, diag_inv, left_t, right_t, rates):
     count = diag_inv.shape[0]
-    steps = count
     last = count - 1
     back = lambda i, ranks: (last - i, 0, 0)
     wide = lambda i, ranks: (0, last - i)
-    square = pl.BlockSpec((R, R), lambda i, ranks: (0, 0))
     wide_shape = jax.ShapeDtypeStruct((R, count * B), f32)
-    kept = () if earlier is None else (earlier[4], *earlier[:4])
     return pl.pallas_call(
         functools.partial(prepare_kernel, last),
         grid_spec=pltpu.PrefetchScalarGridSpec(
             num_scalar_prefetch=1,
-            grid=(steps,),
+            grid=(count,),
             in_specs=[
                 pl.BlockSpec((1, B, B), back),
                 pl.BlockSpec((1, R, B), back),
                 pl.BlockSpec((1, R, B), back),
                 pl.BlockSpec((1, 1, R), back),
-            ]
-            + ([square] + [pl.BlockSpec(memory_space=pl.ANY)] * 4 if kept else []),
+            ],
             out_specs=[
                 pl.BlockSpec((R, B), wide),
                 pl.BlockSpec((1, R, R), back),
                 pl.BlockSpec((R, B), wide),
                 pl.BlockSpec((R, B), wide),
-                square,
+                pl.BlockSpec((R, R), lambda i, ranks: (0, 0)),
             ],
             scratch_shapes=[pltpu.VMEM((R, R), f32)],
         ),
@@ -202,13 +223,12 @@
             wide_shape,
             jax.ShapeDtypeStruct((R, R), f32),
         ],
-        input_output_aliases={6: 0, 7: 1, 8: 2, 9: 3} if kept else {},
         cost_estimate=pl.CostEstimate(
-            flops=8 * steps * R * B * B, bytes_accessed=6 * steps * B * B, transcendentals=0
-        ),
-        compiler_params=pltpu.CompilerParams(vmem_limit_bytes=58 << 20),
+            flops=8 * count * R * B * B, bytes_accessed=6 * count * B * B, transcendentals=0
+        ),
+        compiler_params=pltpu.CompilerParams(vmem_limit_bytes=24 << 20),
         name="prepare",
-    )(block_ranks, diag_inv, left_t, right_t, rates[:, None, :], *kept)
+    )(block_ranks, diag_inv, left_t, right_t, rates[:, None, :])
 
 
 def prefix_kernel(step, side, out):
@@ -255,7 +275,7 @@
     return pl.pallas_call(
         offset_kernel,
         out_shape=jax.ShapeDtypeStruct((count, R // 2 + 16, 2 * R), bf16),
-        compiler_params=pltpu.CompilerParams(vmem_limit_bytes=40 << 20),
+        compiler_params=pltpu.CompilerParams(vmem_limit_bytes=58 << 20),
         name="offset",
     )(grad, suffix_proj, transfer)
 
@@ -299,7 +319,7 @@
         cost_estimate=pl.CostEstimate(
             flops=6 * count * labels * B * B, bytes_accessed=4 * count * B * B, transcendentals=0
         ),
-        compiler_params=pltpu.CompilerParams(vmem_limit_bytes=56 << 20),
+        compiler_params=pltpu.CompilerParams(vmem_limit_bytes=24 << 20),
         name="local_solve",
     )(grad, diag_inv, proj, step, side)
 
@@ -393,10 +413,8 @@
     place = chip * 2 + core
     share = n // (2 * chips)
 
-    first = core * (n // 2) + chip * share
-    own_targets = lax.dynamic_slice_in_dim(targets, first, share, 0)
-    points, own_targets = lax.optimization_barrier((points, own_targets))
     in_hbm = lambda array: pltpu.with_memory_space_constraint(array, pltpu.HBM)
+    points, share_at, place = lax.optimization_barrier((points, core * chips + chip, place))
     diag_inv, points_t, centers_t = in_hbm(diag_inv), in_hbm(points.T), in_hbm(centers.T)
     stored_b, pred_b, extended, coeffs_v = predict(
         1 - core, points_t, centers_t, in_hbm(coeffs), True
@@ -406,11 +424,12 @@
     pair_sum = (pred_a + from_partner).astype(wire).reshape(chips, share, labels)
     arrived = lax.all_to_all(pair_sum, "z", 0, 0, tiled=True)
     pred_own = arrived.astype(f32).sum(axis=0)
-    resid = (jax.nn.sigmoid(pred_own) - own_targets.astype(f32)).astype(bf16)
-    resid_a = sent_to_all(resid, "z").reshape(n // 2, labels)
+    resid = residual_copies(share_at, pred_own, in_hbm(targets), chips)
+    resid_a = lax.all_to_all(resid, "z", 0, 0, tiled=True).reshape(n // 2, labels)
     resid_b = to_partner(resid_a)
 
-    partial = gradient_t(resid_a, resid_b, stored_a, stored_b)
+    partial = gradient_t(resid_a, stored_a)
+    partial = gradient_t(resid_b, stored_b, partial)
     own = labels // samp
     sent = partial.astype(wire).reshape(samp, own, m)
     sent, block_ranks = lax.optimization_barrier((sent, block_ranks))

time: 126 us -> 126 us (level)
    all_to_all x2 -> x1, blocking collectives: 36 us -> 20.5 us  [sent_to_all(): return lax.all_to_all(copies, axis, split_axis=0, concat_axis=0, tiled=True)]
    all_to_all x0 -> x1, blocking collectives: none -> 14.6 us  [body(): lax.all_to_all(resid, 'z', 0, 0, tiled=True).reshape(n // 2, labels)]
    all_to_all x1, waiting for transfers between devices: 0.29 us -> 2.44 us  [body(): arrived = lax.all_to_all(sent, 'samp', 0, 0, tiled=True)]
    pallas_call x1 -> x3, Pallas kernels: 3.15 us -> 4.03 us  [the longest x2 3.24 us: gradient_t(): pl.pallas_call(gradient_kernel, grid=(m // cols,), in_specs=[vmem] * (2 +...]
  transfers between devices with their start and end apart: 4 -> 4, of which waited for: 3 -> 2; matrix products, arithmetic and copies ran while one was open for 1% -> 1% of each run, Pallas kernels for 22% -> 21%
where the time goes in v5:
time: 126 us; the launch traced here: 125 us
  blocking collectives  53.8 us (43%)
  Pallas kernels  43.1 us (34%)
  starting transfers between devices  16.5 us (13%)
  waiting for transfers between devices  4.36 us (3%)
  local copies, waits for them, and re-layouts  3.71 us (3%)
  other arithmetic  3.39 us (3%)
    all_to_all x1, blocking collectives, sent_to_all(): return lax.all_to_all(copies, axis, split_axis=0, concat_axis=0, tiled=True)  20.5 us
    all_to_all x1, blocking collectives, body(): arrived = lax.all_to_all(pair_sum, 'z', 0, 0, tiled=True)  18.6 us
    all_to_all x1, blocking collectives, body(): lax.all_to_all(resid, 'z', 0, 0, tiled=True).reshape(n // 2, labels)  14.6 us
    pallas_call x2, Pallas kernels, predict(): pl.pallas_call(functools.partial(predict_kernel, width), grid_spec=pltpu....  11.9 us
    pallas_call x1, Pallas kernels, prepare(): pl.pallas_call(functools.partial(prepare_kernel, last), grid_spec=pltpu.P...  10.3 us
    pallas_call x1, Pallas kernels, local_solve(): pl.pallas_call(local_kernel, grid=(count,), in_specs=[pl.BlockSpec((label...  7.55 us
    all_to_all x1, starting transfers between devices, body(): arrived = lax.all_to_all(sent, 'samp', 0, 0, tiled=True)  6.81 us
    all_to_all x1, starting transfers between devices, body(): messages = lax.all_to_all(messages, ('z', 'c'), 0, 0, tiled=True)  5.79 us
  transfers between devices with their start and end apart: 4, of which 2 were waited for; matrix products, arithmetic and copies ran while one was open for 1% of the time, Pallas kernels for 21%

profile of v5, /device:TPU:1, one launch (start us, length us, event | category | flops | bytes accessed | tf_op | source)
XLA Modules:
  0.0 125.0 jit_solution(17639584583757369385)
XLA Ops:
  0.0 6.3 %predict.2 = (bf16[1024,4096]{1,0:T(8,128)(2,1)S(1)}, f32[1024,128]{1,0:T(8,128)S(1)}, bf16[72,4096]{1,0:T(8,128)(2,1)S(1)}, bf16[4096,128]{1,0:T(8,128)(2,1)S(1)}) custom-call(s32[1]{0:T(128)} %bitcast.4.half, bf16[64,2048]{1,0:T(8,128)(2,1)} %bitcast.25, bf16[64,4096]{1,0:T(8,128)(2,1)} %bitcast.24, bf16[4096,128]{1,0:T(8,128)(2,1)} %coeffs.1), custom_call_target="tpu_custom_call" | custom-call | flops 1610612736 | bytes 8388608 | tf_op jit(solution)/shard_map/predict/pallas_call | solution.py:85
  6.3 3.3 %collective-permute-start = (f32[1024,128]{1,0:T(8,128)S(1)}, f32[1024,128]{1,0:T(8,128)S(1)}, u32[]{:S(2)}, u32[]{:S(2)}) collective-permute-start(f32[1024,128]{1,0:T(8,128)S(1)} %get-tuple-element.34), channel_id=1, source_target_pairs={{0,1},{1,0},{2,3},{3,2},{4,5},{5,4},{6,7},{7,6},{8,9},{9,8},{10,11... | collective-permute-start | bytes 1572872 | tf_op jit(solution)/shard_map/ppermute | solution.py:405
  9.6 5.6 %predict.3 = (bf16[1024,4096]{1,0:T(8,128)(2,1)S(1)}, f32[1024,128]{1,0:T(8,128)S(1)}) custom-call(s32[1]{0:T(128)} %bitcast.2.half, bf16[64,2048]{1,0:T(8,128)(2,1)} %bitcast.26, bf16[72,4096]{1,0:T(8,128)(2,1)S(1)} %get-tuple-element.31.centers, bf16[4096,128]{1,0:T(8,128)(2,1)S(1)} %get-tuple-element.32.coeffs), custom_call_target="tpu_custom_call" | custom-call | flops 1610612736 | bytes 8388608 | tf_op jit(solution)/shard_map/predict/pallas_call | solution.py:85
  15.2 0.0 collective-permute-done
  15.2 0.1 add_convert_fusion
  15.3 18.6 %all_to_all.25 = f16[8,128,128]{2,1,0:T(8,128)(2,1)S(1)} all-to-all(f16[8,128,128]{2,1,0:T(8,128)(2,1)S(1)} %bitcast.23), channel_id=1, replica_groups=mesh['samp'=16,'z'=8,'c'=2] {'z'}, dimensions={0} | all-to-all | bytes 524288 | tf_op jit(solution)/shard_map/all_to_all | solution.py:425
  34.0 0.8 residual.1
  34.8 14.6 %all_to_all.26 = bf16[8,128,128]{2,1,0:T(8,128)(2,1)S(1)} all-to-all(bf16[8,128,128]{2,1,0:T(8,128)(2,1)S(1)} %residual.1), channel_id=1, replica_groups=mesh['samp'=16,'z'=8,'c'=2] {'z'}, dimensions={0} | all-to-all | bytes 524288 | tf_op jit(solution)/shard_map/all_to_all | solution.py:428
  49.4 0.6 collective-permute-start.1
  50.0 1.6 %gradient.2.refs_0_ = f32[128,4096]{1,0:T(8,128)S(1)} custom-call(bf16[1024,128]{1,0:T(8,128)(2,1)S(1)} %bitcast.19, bf16[1024,4096]{1,0:T(8,128)(2,1)S(1)} %get-tuple-element.36.rows), custom_call_target="tpu_custom_call" | custom-call | flops 1073741824 | bytes 8388608 | tf_op jit(solution)/shard_map/gradient/pallas_call | solution.py:150
  51.6 0.0 collective-permute-done.1.resid
  51.6 1.6 %gradient.3 = f32[128,4096]{1,0:T(8,128)S(1)} custom-call(bf16[1024,128]{1,0:T(8,128)(2,1)S(1)} %collective-permute-done.1.resid, bf16[1024,4096]{1,0:T(8,128)(2,1)S(1)} %get-tuple-element.35.rows, f32[128,4096]{1,0:T(8,128)S(1)} %gradient.2.refs_0_), custom_call_target="tpu_custom_call" | custom-call | flops 1073741824 | bytes 8388608 | tf_op jit(solution)/shard_map/gradient/pallas_call | solution.py:150
  53.3 0.0 copy-start.7
  53.3 1.1 convert_bitcast_fusion
  54.4 6.8 %all-to-all-start.2 = ((f16[16,8,4096]{2,1,0:T(8,128)(2,1)}), f16[16,8,4096]{2,1,0:T(8,128)(2,1)}, u32[]{:S(2)}, u32[]{:S(2)}) async-start(f16[16,8,4096]{2,1,0:T(8,128)(2,1)} %convert_bitcast_fusion), calls=%async_computation.2 | async-start | bytes 2097152 | tf_op jit(solution)/shard_map/all_to_all | solution.py:436
  61.2 0.0 copy-start.2
  61.2 0.0 copy-start.3
  61.2 0.0 copy-start.5
  61.2 0.0 copy-start.6
  61.3 0.0 copy-done.7
  61.3 0.4 constant_dynamic-slice_fusion
  61.6 0.3 copy.11
  61.9 0.3 copy-done.2
  62.2 0.2 copy-done.3
  62.4 0.0 copy-done.5
  62.4 0.0 copy-done.6
  62.4 10.3 %prepare.1 = (f32[64,4096]{1,0:T(8,128)S(1)}, f32[8,64,64]{2,1,0:T(8,128)S(1)}, f32[64,4096]{1,0:T(8,128)S(1)}, f32[64,4096]{1,0:T(8,128)S(1)}, f32[64,64]{1,0:T(8,128)S(1)}) custom-call(s32[8]{0:T(128)S(1)} %copy-done.6, f32[8,512,512]{2,1,0:T(8,128)} %inverse.3, bf16[8,64,512]{2,1,0:T(8,128)(2,1)S(1)} %bitcast.20, bf16[8,64,512]{2,1,0:T(8,128)(2,1)S(1)} %bitcast.21, ...), custom_call_target="tpu_custom_call" | custom-call | flops 1073741824 | bytes 12582912 | tf_op jit(solution)/shard_map/prepare/pallas_call | solution.py:199
  72.7 0.0 copy-start.1
  72.7 1.0 copy-done.1
  73.7 0.0 copy-start.4
  73.7 0.6 copy-done.4
  74.3 1.4 %prefix.1.side = f32[64,4096]{1,0:T(8,128)S(1)} custom-call(f32[8,64,64]{2,1,0:T(8,128)S(1)} %get-tuple-element.48.step, f32[64,4096]{1,0:T(8,128)S(1)} %get-tuple-element.49.side), custom_call_target="tpu_custom_call" | custom-call | flops 100663296 | bytes 2097152 | tf_op jit(solution)/shard_map/prefix/pallas_call | solution.py:248
  75.7 2.4 %all-to-all-done.2 = f16[16,8,4096]{2,1,0:T(8,128)(2,1)} async-done(((f16[16,8,4096]{2,1,0:T(8,128)(2,1)}), f16[16,8,4096]{2,1,0:T(8,128)(2,1)}, u32[]{:S(2)}, u32[]{:S(2)}) %all-to-all-start.2) | async-done | bytes 1048608 | tf_op jit(solution)/shard_map/all_to_all | solution.py:436
  78.1 1.4 %convert_reduce_fusion = f32[8,4096]{1,0:T(8,128)S(1)} fusion(f16[16,8,4096]{2,1,0:T(8,128)(2,1)} %all-to-all-done.2), kind=kLoop, calls=%fused_computation | loop fusion | flops 1015808 | bytes 1179648 | tf_op jit(solution)/shard_map/reduce_sum | solution.py:449
  79.5 0.7 bitcast_add_fusion.grad
  80.2 2.5 %offset.1 = bf16[16,48,128]{2,1,0:T(8,128)(2,1)} custom-call(f32[8,4096]{1,0:T(8,128)} %bitcast_add_fusion.grad, f32[64,4096]{1,0:T(8,128)} %copy-done.1, f32[64,64]{1,0:T(8,128)} %copy-done.4), custom_call_target="tpu_custom_call" | custom-call | tf_op jit(solution)/shard_map/offset/pallas_call | solution.py:275
  82.7 5.8 %all-to-all-start.3 = ((bf16[16,48,128]{2,1,0:T(8,128)(2,1)}), bf16[16,48,128]{2,1,0:T(8,128)(2,1)}, u32[]{:S(2)}, u32[]{:S(2)}) async-start(bf16[16,48,128]{2,1,0:T(8,128)(2,1)} %offset.1), calls=%async_computation.3 | async-start | bytes 393216 | tf_op jit(solution)/shard_map/all_to_all | solution.py:452
  88.5 0.0 copy-start
  88.5 0.9 copy-done
  89.4 7.6 %local_solve.1.solved = f32[8,4096]{1,0:T(8,128)S(1)} custom-call(f32[8,4096]{1,0:T(8,128)S(1)} %copy-done, f32[8,512,512]{2,1,0:T(8,128)} %inverse.3, f32[64,4096]{1,0:T(8,128)S(1)} %get-tuple-element.47.proj, f32[8,64,64]{2,1,0:T(8,128)S(1)} %get-tuple-element.48.step, f32[64,4096]{1,0:T(8,128)S(1)} %get-tuple-element.49.side), custom_call_target="tpu_custom_call" | custom-call | flops 100663296 | bytes 8388608 | tf_op jit(solution)/shard_map/local_solve/pallas_call | solution.py:306
  96.9 1.9 %all-to-all-done.3.messages = bf16[16,48,128]{2,1,0:T(8,128)(2,1)} async-done(((bf16[16,48,128]{2,1,0:T(8,128)(2,1)}), bf16[16,48,128]{2,1,0:T(8,128)(2,1)}, u32[]{:S(2)}, u32[]{:S(2)}) %all-to-all-start.3) | async-done | bytes 196640 | tf_op jit(solution)/shard_map/all_to_all | solution.py:452
  98.8 2.8 %finish.1 = f32[8,4224]{1,0:T(8,128)S(1)} custom-call(s32[1]{0:T(128)} %bitcast.place, bf16[16,48,128]{2,1,0:T(8,128)(2,1)} %all-to-all-done.3.messages, f32[8,4096]{1,0:T(8,128)S(1)} %local_solve.1.solved, f32[64,4096]{1,0:T(8,128)S(1)} %prefix.1.side), custom_call_target="tpu_custom_call" | custom-call | tf_op jit(solution)/shard_map/finish/pallas_call | solution.py:364
  101.6 0.1 broadcast_in_dim.7
  101.7 20.5 %all_to_all.27 = f16[16,8,4224]{2,1,0:T(8,128)(2,1)S(1)} all-to-all(f16[16,8,4224]{2,1,0:T(8,128)(2,1)S(1)} %broadcast_in_dim.7), channel_id=1, replica_groups=mesh['samp'=16,'z'=8,'c'=2] {'samp'}, dimensions={0} | all-to-all | bytes 2162688 | tf_op jit(solution)/shard_map/all_to_all | solution.py:401
  122.2 0.1 bitcast_convert_fusion.powers.scaled
  122.4 2.7 %unscaled.1 = f32[4096,128]{1,0:T(8,128)} custom-call(f32[128,4224]{1,0:T(8,128)S(1)} %bitcast_convert_fusion.powers.scaled, f32[128,4224]{1,0:T(8,128)S(1)} %bitcast_convert_fusion.powers.scaled), custom_call_target="tpu_custom_call" | custom-call | tf_op jit(solution)/shard_map/unscaled/pallas_call | solution.py:385
  (2 shorter events, 0.0 us)
Async XLA Ops:
  6.3 8.9 %collective-permute-start = (f32[1024,128]{1,0:T(8,128)S(1)}, f32[1024,128]{1,0:T(8,128)S(1)}, u32[]{:S(2)}, u32[]{:S(2)}) collective-permute-start(f32[1024,128]{1,0:T(8,128)S(1)} %get-tuple-element.34), channel_id=1, source_target_pairs={{0,1},{1,0},{2,3},{3,2},{4,5},{5,4},{6,7},{7,6},{8,9},{9,8},{10,11... | collective-permute-start | bytes 1572872 | tf_op jit(solution)/shard_map/ppermute | solution.py:405
  49.4 2.2 %collective-permute-start.1 = (bf16[1024,128]{1,0:T(8,128)(2,1)S(1)}, bf16[1024,128]{1,0:T(8,128)(2,1)S(1)}, u32[]{:S(2)}, u32[]{:S(2)}) collective-permute-start(bf16[1024,128]{1,0:T(8,128)(2,1)S(1)} %bitcast.18), channel_id=1, source_target_pairs={{0,1},{1,0},{2,3},{3,2},{4,5},{5,4},{6,7},{7,6},{8,9},{9,8},{10,11... | collective-permute-start | bytes 786440 | tf_op jit(solution)/shard_map/ppermute | solution.py:405
  53.3 8.0 %copy-start.7 = (bf16[4096,128]{1,0:T(8,128)(2,1)S(1)}, bf16[4096,128]{1,0:T(8,128)(2,1)}, u32[]{:S(2)}) copy-start(bf16[4096,128]{1,0:T(8,128)(2,1)} %coeffs.1) | copy-start | bytes 3145732
  54.4 23.7 %all-to-all-start.2 = ((f16[16,8,4096]{2,1,0:T(8,128)(2,1)}), f16[16,8,4096]{2,1,0:T(8,128)(2,1)}, u32[]{:S(2)}, u32[]{:S(2)}) async-start(f16[16,8,4096]{2,1,0:T(8,128)(2,1)} %convert_bitcast_fusion), calls=%async_computation.2 | async-start | bytes 2097152 | tf_op jit(solution)/shard_map/all_to_all | solution.py:436
  61.2 1.0 copy-start.2
  61.2 1.2 copy-start.3
  61.2 1.2 copy-start.5
  61.2 1.2 copy-start.6
  72.7 1.0 copy-start.1
  73.7 0.6 copy-start.4
  82.7 16.2 %all-to-all-start.3 = ((bf16[16,48,128]{2,1,0:T(8,128)(2,1)}), bf16[16,48,128]{2,1,0:T(8,128)(2,1)}, u32[]{:S(2)}, u32[]{:S(2)}) async-start(bf16[16,48,128]{2,1,0:T(8,128)(2,1)} %offset.1), calls=%async_computation.3 | async-start | bytes 393216 | tf_op jit(solution)/shard_map/all_to_all | solution.py:452
  88.5 0.9 copy-start

commit v6 on v5

--- a/solution.py
+++ b/solution.py
@@ -50,23 +50,22 @@
 
 
 def predict_kernel(width, half, points_t, centers, coeffs, stored, pred, *kept):
-    i = pl.program_id(0)
-    rows = pred.shape[0]
+    arriving = None
     if kept:
-        centers_t, (centers, coeffs_v) = centers, kept
-
-        @pl.when(i == 0)
-        def _():
-            centers[...] = with_norms(centers_t[...].astype(f32), False).astype(bf16)
-            coeffs_v[...] = coeffs[...]
+        centers_t, (centers, coeffs_v, arrived) = centers, kept
+        arriving = pltpu.make_async_copy(coeffs, coeffs_v, arrived)
+        arriving.start()
+        centers[...] = with_norms(centers_t[...].astype(f32), False).astype(bf16)
+        coeffs = coeffs_v
 
     x = with_norms(points_t[...].astype(f32), True).T.astype(bf16)
-    here = pl.ds(pl.multiple_of(i * rows, rows), rows)
     total = None
     for at in range(0, centers.shape[1], width):
         scaled = dot(x, centers[:, at : at + width], 1, 0) * (2 * LOG2E / D)
         k = jnp.exp2(scaled).astype(bf16)
-        stored[here, at : at + width] = k
+        stored[:, at : at + width] = k
+        if arriving is not None and at == 0:
+            arriving.wait()
         part = dot(k, coeffs[at : at + width, :], 1, 0)
         total = part if total is None else total + part
     pred[...] = total
@@ -75,9 +74,8 @@
 vmem = pl.BlockSpec(memory_space=pltpu.VMEM)
 
 
-def predict(half, points_t, centers, coeffs, first, rows=1024, width=256):
+def predict(half, points_t, centers, coeffs, first, width=256):
     n, m, labels = points_t.shape[1] // 2, centers.shape[1], coeffs.shape[1]
-    steps = n // rows
     whole = lambda i, half: (0, 0)
     outs = [pltpu.VMEM((n, m), bf16), jax.ShapeDtypeStruct((n, labels), f32)]
     if first:
@@ -86,15 +84,16 @@
         functools.partial(predict_kernel, width),
         grid_spec=pltpu.PrefetchScalarGridSpec(
             num_scalar_prefetch=1,
-            grid=(steps,),
-            in_specs=[pl.BlockSpec((D, rows), lambda i, half: (0, half[0] * steps + i))]
+            grid=(1,),
+            in_specs=[pl.BlockSpec((D, n), lambda i, half: (0, half[0]))]
             + (
-                [pl.BlockSpec((D, m), whole), pl.BlockSpec((m, labels), whole)]
+                [pl.BlockSpec((D, m), whole), pl.BlockSpec(memory_space=pl.ANY)]
                 if first
                 else [vmem, vmem]
             ),
-            out_specs=[vmem, pl.BlockSpec((rows, labels), lambda i, half: (i, 0))]
+            out_specs=[vmem, pl.BlockSpec((n, labels), lambda i, half: (0, 0))]
             + ([vmem, vmem] if first else []),
+            scratch_shapes=[pltpu.SemaphoreType.DMA] if first else [],
         ),
         out_shape=outs,
         compiler_params=pltpu.CompilerParams(vmem_limit_bytes=20 << 20),
@@ -274,8 +273,8 @@
 def offset_messages(grad, suffix_proj, transfer, count):
     return pl.pallas_call(
         offset_kernel,
-        out_shape=jax.ShapeDtypeStruct((count, R // 2 + 16, 2 * R), bf16),
-        compiler_params=pltpu.CompilerParams(vmem_limit_bytes=58 << 20),
+        out_shape=pltpu.HBM((count, R // 2 + 16, 2 * R), bf16),
+        compiler_params=pltpu.CompilerParams(vmem_limit_bytes=40 << 20),
         name="offset",
     )(grad, suffix_proj, transfer)
 
@@ -319,7 +318,7 @@
         cost_estimate=pl.CostEstimate(
             flops=6 * count * labels * B * B, bytes_accessed=4 * count * B * B, transcendentals=0
         ),
-        compiler_params=pltpu.CompilerParams(vmem_limit_bytes=24 << 20),
+        compiler_params=pltpu.CompilerParams(vmem_limit_bytes=40 << 20),
         name="local_solve",
     )(grad, diag_inv, proj, step, side)
 

time: 126 us -> 125 us (level)
  Pallas kernels: 43.1 us -> 41.7 us
    unnamed x17 -> x19, local copies, waits for them, and re-layouts: 3.27 us -> 3.93 us
where the time goes in v6:
time: 125 us; the launch traced here: 124 us
  blocking collectives  53.8 us (43%)
  Pallas kernels  41.7 us (33%)
  starting transfers between devices  15.9 us (13%)
  local copies, waits for them, and re-layouts  4.37 us (3%)
  waiting for transfers between devices  4.28 us (3%)
  other arithmetic  3.58 us (3%)
    all_to_all x1, blocking collectives, sent_to_all(): return lax.all_to_all(copies, axis, split_axis=0, concat_axis=0, tiled=True)  20.5 us
    all_to_all x1, blocking collectives, body(): arrived = lax.all_to_all(pair_sum, 'z', 0, 0, tiled=True)  18.6 us
    all_to_all x1, blocking collectives, body(): lax.all_to_all(resid, 'z', 0, 0, tiled=True).reshape(n // 2, labels)  14.6 us
    pallas_call x2, Pallas kernels, predict(): pl.pallas_call(functools.partial(predict_kernel, width), grid_spec=pltpu....  12.6 us
    pallas_call x1, Pallas kernels, prepare(): pl.pallas_call(functools.partial(prepare_kernel, last), grid_spec=pltpu.P...  10.3 us
    pallas_call x1, Pallas kernels, local_solve(): pl.pallas_call(local_kernel, grid=(count,), in_specs=[pl.BlockSpec((label...  7.55 us
    all_to_all x1, starting transfers between devices, body(): arrived = lax.all_to_all(sent, 'samp', 0, 0, tiled=True)  6.8 us
    all_to_all x1, starting transfers between devices, body(): messages = lax.all_to_all(messages, ('z', 'c'), 0, 0, tiled=True)  5.26 us
  transfers between devices with their start and end apart: 4, of which 2 were waited for; matrix products, arithmetic and copies ran while one was open for 1% of the time, Pallas kernels for 21%

profile of v6, /device:TPU:1, one launch (start us, length us, event | category | flops | bytes accessed | tf_op | source)
XLA Modules:
  0.0 123.8 jit_solution(15367749704652690279)
XLA Ops:
  0.0 7.0 %predict.2 = (bf16[1024,4096]{1,0:T(8,128)(2,1)S(1)}, f32[1024,128]{1,0:T(8,128)S(1)}, bf16[72,4096]{1,0:T(8,128)(2,1)S(1)}, bf16[4096,128]{1,0:T(8,128)(2,1)S(1)}) custom-call(s32[1]{0:T(128)} %bitcast.4.half, bf16[64,2048]{1,0:T(8,128)(2,1)} %bitcast.25, bf16[64,4096]{1,0:T(8,128)(2,1)} %bitcast.24, bf16[4096,128]{1,0:T(8,128)(2,1)} %coeffs.1), custom_call_target="tpu_custom_call" | custom-call | flops 1610612736 | bytes 8388608 | tf_op jit(solution)/shard_map/predict/pallas_call | solution.py:83
  7.0 3.3 %collective-permute-start = (f32[1024,128]{1,0:T(8,128)S(1)}, f32[1024,128]{1,0:T(8,128)S(1)}, u32[]{:S(2)}, u32[]{:S(2)}) collective-permute-start(f32[1024,128]{1,0:T(8,128)S(1)} %get-tuple-element.34), channel_id=1, source_target_pairs={{0,1},{1,0},{2,3},{3,2},{4,5},{5,4},{6,7},{7,6},{8,9},{9,8},{10,11... | collective-permute-start | bytes 1572872 | tf_op jit(solution)/shard_map/ppermute | solution.py:404
  10.3 5.6 %predict.3 = (bf16[1024,4096]{1,0:T(8,128)(2,1)S(1)}, f32[1024,128]{1,0:T(8,128)S(1)}) custom-call(s32[1]{0:T(128)} %bitcast.2.half, bf16[64,2048]{1,0:T(8,128)(2,1)} %bitcast.26, bf16[72,4096]{1,0:T(8,128)(2,1)S(1)} %get-tuple-element.31.centers, bf16[4096,128]{1,0:T(8,128)(2,1)S(1)} %get-tuple-element.32.coeffs), custom_call_target="tpu_custom_call" | custom-call | flops 1610612736 | bytes 8388608 | tf_op jit(solution)/shard_map/predict/pallas_call | solution.py:83
  15.9 0.0 collective-permute-done
  15.9 0.1 add_convert_fusion
  16.0 18.6 %all_to_all.25 = f16[8,128,128]{2,1,0:T(8,128)(2,1)S(1)} all-to-all(f16[8,128,128]{2,1,0:T(8,128)(2,1)S(1)} %bitcast.23), channel_id=1, replica_groups=mesh['samp'=16,'z'=8,'c'=2] {'z'}, dimensions={0} | all-to-all | bytes 524288 | tf_op jit(solution)/shard_map/all_to_all | solution.py:424
  34.7 0.8 residual.1
  35.5 14.6 %all_to_all.26 = bf16[8,128,128]{2,1,0:T(8,128)(2,1)S(1)} all-to-all(bf16[8,128,128]{2,1,0:T(8,128)(2,1)S(1)} %residual.1), channel_id=1, replica_groups=mesh['samp'=16,'z'=8,'c'=2] {'z'}, dimensions={0} | all-to-all | bytes 524288 | tf_op jit(solution)/shard_map/all_to_all | solution.py:427
  50.1 0.6 collective-permute-start.1
  50.7 1.6 %gradient.2.refs_0_ = f32[128,4096]{1,0:T(8,128)S(1)} custom-call(bf16[1024,128]{1,0:T(8,128)(2,1)S(1)} %bitcast.19, bf16[1024,4096]{1,0:T(8,128)(2,1)S(1)} %get-tuple-element.36.rows), custom_call_target="tpu_custom_call" | custom-call | flops 1073741824 | bytes 8388608 | tf_op jit(solution)/shard_map/gradient/pallas_call | solution.py:149
  52.3 0.0 collective-permute-done.1.resid
  52.3 1.6 %gradient.3 = f32[128,4096]{1,0:T(8,128)S(1)} custom-call(bf16[1024,128]{1,0:T(8,128)(2,1)S(1)} %collective-permute-done.1.resid, bf16[1024,4096]{1,0:T(8,128)(2,1)S(1)} %get-tuple-element.35.rows, f32[128,4096]{1,0:T(8,128)S(1)} %gradient.2.refs_0_), custom_call_target="tpu_custom_call" | custom-call | flops 1073741824 | bytes 8388608 | tf_op jit(solution)/shard_map/gradient/pallas_call | solution.py:149
  54.0 0.0 copy-start.8
  54.0 1.1 convert_bitcast_fusion
  55.1 6.8 %all-to-all-start.2 = ((f16[16,8,4096]{2,1,0:T(8,128)(2,1)}), f16[16,8,4096]{2,1,0:T(8,128)(2,1)}, u32[]{:S(2)}, u32[]{:S(2)}) async-start(f16[16,8,4096]{2,1,0:T(8,128)(2,1)} %convert_bitcast_fusion), calls=%async_computation.2 | async-start | bytes 2097152 | tf_op jit(solution)/shard_map/all_to_all | solution.py:435
  61.9 0.0 copy-start.2
  61.9 0.0 copy-start.3
  61.9 0.0 copy-start.6
  61.9 0.0 copy-start.7
  61.9 0.0 copy-done.8
  61.9 0.4 constant_dynamic-slice_fusion
  62.3 1.0 copy.11
  63.3 0.0 copy-done.2
  63.3 0.0 copy-done.3
  63.3 0.0 copy-done.6
  63.3 0.0 copy-done.7
  63.3 10.3 %prepare.1 = (f32[64,4096]{1,0:T(8,128)S(1)}, f32[8,64,64]{2,1,0:T(8,128)S(1)}, f32[64,4096]{1,0:T(8,128)S(1)}, f32[64,4096]{1,0:T(8,128)S(1)}, f32[64,64]{1,0:T(8,128)S(1)}) custom-call(s32[8]{0:T(128)S(1)} %copy-done.7, f32[8,512,512]{2,1,0:T(8,128)} %inverse.3, bf16[8,64,512]{2,1,0:T(8,128)(2,1)S(1)} %bitcast.20, bf16[8,64,512]{2,1,0:T(8,128)(2,1)S(1)} %bitcast.21, ...), custom_call_target="tpu_custom_call" | custom-call | flops 1073741824 | bytes 12582912 | tf_op jit(solution)/shard_map/prepare/pallas_call | solution.py:198
  73.6 0.0 copy-start
  73.6 1.0 copy-done
  74.6 0.0 copy-start.4
  74.6 1.4 %prefix.1.side = f32[64,4096]{1,0:T(8,128)S(1)} custom-call(f32[8,64,64]{2,1,0:T(8,128)S(1)} %get-tuple-element.48.step, f32[64,4096]{1,0:T(8,128)S(1)} %get-tuple-element.49.side), custom_call_target="tpu_custom_call" | custom-call | flops 100663296 | bytes 2097152 | tf_op jit(solution)/shard_map/prefix/pallas_call | solution.py:247
  76.0 2.8 %all-to-all-done.2 = f16[16,8,4096]{2,1,0:T(8,128)(2,1)} async-done(((f16[16,8,4096]{2,1,0:T(8,128)(2,1)}), f16[16,8,4096]{2,1,0:T(8,128)(2,1)}, u32[]{:S(2)}, u32[]{:S(2)}) %all-to-all-start.2) | async-done | bytes 1048608 | tf_op jit(solution)/shard_map/all_to_all | solution.py:435
  78.7 0.0 copy-done.4
  78.7 1.4 %convert_reduce_fusion = f32[8,4096]{1,0:T(8,128)S(1)} fusion(f16[16,8,4096]{2,1,0:T(8,128)(2,1)} %all-to-all-done.2), kind=kLoop, calls=%fused_computation | loop fusion | flops 1015808 | bytes 1179648 | tf_op jit(solution)/shard_map/reduce_sum | solution.py:448
  80.1 0.9 bitcast_add_fusion.grad
  81.0 0.0 copy-start.5
  81.0 0.7 copy-done.5
  81.8 1.3 %offset.1 = bf16[16,48,128]{2,1,0:T(8,128)(2,1)} custom-call(f32[8,4096]{1,0:T(8,128)S(1)} %bitcast_add_fusion.grad, f32[64,4096]{1,0:T(8,128)S(1)} %get-tuple-element.45.suffix_proj, f32[64,64]{1,0:T(8,128)S(1)} %copy-done.5), custom_call_target="tpu_custom_call" | custom-call | tf_op jit(solution)/shard_map/offset/pallas_call | solution.py:274
  83.0 5.3 %all-to-all-start.3 = ((bf16[16,48,128]{2,1,0:T(8,128)(2,1)}), bf16[16,48,128]{2,1,0:T(8,128)(2,1)S(1)}, u32[]{:S(2)}, u32[]{:S(2)}) async-start(bf16[16,48,128]{2,1,0:T(8,128)(2,1)} %offset.1), calls=%async_computation.3 | async-start | bytes 393216 | tf_op jit(solution)/shard_map/all_to_all | solution.py:451
  88.3 0.0 copy-start.1
  88.3 1.2 copy-done.1
  89.5 7.6 %local_solve.1.solved = f32[8,4096]{1,0:T(8,128)S(1)} custom-call(f32[8,4096]{1,0:T(8,128)S(1)} %bitcast_add_fusion.grad, f32[8,512,512]{2,1,0:T(8,128)} %inverse.3, f32[64,4096]{1,0:T(8,128)S(1)} %copy-done.1, f32[8,64,64]{2,1,0:T(8,128)S(1)} %get-tuple-element.48.step, f32[64,4096]{1,0:T(8,128)S(1)} %get-tuple-element.49.side), custom_call_target="tpu_custom_call" | custom-call | flops 100663296 | bytes 8388608 | tf_op jit(solution)/shard_map/local_solve/pallas_call | solution.py:305
  97.1 1.5 %all-to-all-done.3.messages = bf16[16,48,128]{2,1,0:T(8,128)(2,1)S(1)} async-done(((bf16[16,48,128]{2,1,0:T(8,128)(2,1)}), bf16[16,48,128]{2,1,0:T(8,128)(2,1)S(1)}, u32[]{:S(2)}, u32[]{:S(2)}) %all-to-all-start.3) | async-done | bytes 196640 | tf_op jit(solution)/shard_map/all_to_all | solution.py:451
  98.6 1.8 %finish.1 = f32[8,4224]{1,0:T(8,128)S(1)} custom-call(s32[1]{0:T(128)} %bitcast.place, bf16[16,48,128]{2,1,0:T(8,128)(2,1)S(1)} %all-to-all-done.3.messages, f32[8,4096]{1,0:T(8,128)S(1)} %local_solve.1.solved, f32[64,4096]{1,0:T(8,128)S(1)} %prefix.1.side), custom_call_target="tpu_custom_call" | custom-call | tf_op jit(solution)/shard_map/finish/pallas_call | solution.py:363
  100.4 0.1 broadcast_in_dim.7
  100.5 20.5 %all_to_all.27 = f16[16,8,4224]{2,1,0:T(8,128)(2,1)S(1)} all-to-all(f16[16,8,4224]{2,1,0:T(8,128)(2,1)S(1)} %broadcast_in_dim.7), channel_id=1, replica_groups=mesh['samp'=16,'z'=8,'c'=2] {'samp'}, dimensions={0} | all-to-all | bytes 2162688 | tf_op jit(solution)/shard_map/all_to_all | solution.py:400
  121.0 0.1 bitcast_convert_fusion.powers.scaled
  121.2 2.7 %unscaled.1 = f32[4096,128]{1,0:T(8,128)} custom-call(f32[128,4224]{1,0:T(8,128)S(1)} %bitcast_convert_fusion.powers.scaled, f32[128,4224]{1,0:T(8,128)S(1)} %bitcast_convert_fusion.powers.scaled), custom_call_target="tpu_custom_call" | custom-call | tf_op jit(solution)/shard_map/unscaled/pallas_call | solution.py:384
  (2 shorter events, 0.0 us)
Async XLA Ops:
  7.0 8.9 %collective-permute-start = (f32[1024,128]{1,0:T(8,128)S(1)}, f32[1024,128]{1,0:T(8,128)S(1)}, u32[]{:S(2)}, u32[]{:S(2)}) collective-permute-start(f32[1024,128]{1,0:T(8,128)S(1)} %get-tuple-element.34), channel_id=1, source_target_pairs={{0,1},{1,0},{2,3},{3,2},{4,5},{5,4},{6,7},{7,6},{8,9},{9,8},{10,11... | collective-permute-start | bytes 1572872 | tf_op jit(solution)/shard_map/ppermute | solution.py:404
  50.1 2.2 %collective-permute-start.1 = (bf16[1024,128]{1,0:T(8,128)(2,1)S(1)}, bf16[1024,128]{1,0:T(8,128)(2,1)S(1)}, u32[]{:S(2)}, u32[]{:S(2)}) collective-permute-start(bf16[1024,128]{1,0:T(8,128)(2,1)S(1)} %bitcast.18), channel_id=1, source_target_pairs={{0,1},{1,0},{2,3},{3,2},{4,5},{5,4},{6,7},{7,6},{8,9},{9,8},{10,11... | collective-permute-start | bytes 786440 | tf_op jit(solution)/shard_map/ppermute | solution.py:404
  54.0 8.0 %copy-start.8 = (bf16[4096,128]{1,0:T(8,128)(2,1)S(1)}, bf16[4096,128]{1,0:T(8,128)(2,1)}, u32[]{:S(2)}) copy-start(bf16[4096,128]{1,0:T(8,128)(2,1)} %coeffs.1) | copy-start | bytes 3145732
  55.1 23.7 %all-to-all-start.2 = ((f16[16,8,4096]{2,1,0:T(8,128)(2,1)}), f16[16,8,4096]{2,1,0:T(8,128)(2,1)}, u32[]{:S(2)}, u32[]{:S(2)}) async-start(f16[16,8,4096]{2,1,0:T(8,128)(2,1)} %convert_bitcast_fusion), calls=%async_computation.2 | async-start | bytes 2097152 | tf_op jit(solution)/shard_map/all_to_all | solution.py:435
  61.9 1.4 %copy-start.2 = (bf16[8,512,64]{1,2,0:T(8,128)(2,1)S(1)}, bf16[8,512,64]{1,2,0:T(8,128)(2,1)}, u32[]{:S(2)}) copy-start(bf16[8,512,64]{1,2,0:T(8,128)(2,1)} %param.14) | copy-start | bytes 1572868
  61.9 1.4 %copy-start.3 = (bf16[8,512,64]{1,2,0:T(8,128)(2,1)S(1)}, bf16[8,512,64]{1,2,0:T(8,128)(2,1)}, u32[]{:S(2)}) copy-start(bf16[8,512,64]{1,2,0:T(8,128)(2,1)} %param.15) | copy-start | bytes 1572868
  61.9 1.4 %copy-start.6 = (f32[8,64]{1,0:T(8,128)S(1)}, f32[8,64]{1,0:T(8,128)}, u32[]{:S(2)}) copy-start(f32[8,64]{1,0:T(8,128)} %param.16) | copy-start | bytes 6148
  61.9 1.4 %copy-start.7 = (s32[8]{0:T(128)S(1)}, s32[8]{0:T(128)}, u32[]{:S(2)}) copy-start(s32[8]{0:T(128)} %ranks) | copy-start | bytes 100
  73.6 1.0 copy-start
  74.6 4.2 %copy-start.4 = (f32[64,64]{1,0:T(8,128)}, f32[64,64]{1,0:T(8,128)S(1)}, u32[]{:S(2)}) copy-start(f32[64,64]{1,0:T(8,128)S(1)} %get-tuple-element.46.transfer) | copy-start | bytes 49156
  81.0 0.8 copy-start.5
  83.0 15.5 %all-to-all-start.3 = ((bf16[16,48,128]{2,1,0:T(8,128)(2,1)}), bf16[16,48,128]{2,1,0:T(8,128)(2,1)S(1)}, u32[]{:S(2)}, u32[]{:S(2)}) async-start(bf16[16,48,128]{2,1,0:T(8,128)(2,1)} %offset.1), calls=%async_computation.3 | async-start | bytes 393216 | tf_op jit(solution)/shard_map/all_to_all | solution.py:451
  88.3 1.2 copy-start.1

commit v7 on v6

--- a/solution.py
+++ b/solution.py
@@ -50,13 +50,10 @@
 
 
 def predict_kernel(width, half, points_t, centers, coeffs, stored, pred, *kept):
-    arriving = None
     if kept:
-        centers_t, (centers, coeffs_v, arrived) = centers, kept
-        arriving = pltpu.make_async_copy(coeffs, coeffs_v, arrived)
-        arriving.start()
+        centers_t, (centers, coeffs_v) = centers, kept
         centers[...] = with_norms(centers_t[...].astype(f32), False).astype(bf16)
-        coeffs = coeffs_v
+        coeffs_v[...] = coeffs[...]
 
     x = with_norms(points_t[...].astype(f32), True).T.astype(bf16)
     total = None
@@ -64,8 +61,6 @@
         scaled = dot(x, centers[:, at : at + width], 1, 0) * (2 * LOG2E / D)
         k = jnp.exp2(scaled).astype(bf16)
         stored[:, at : at + width] = k
-        if arriving is not None and at == 0:
-            arriving.wait()
         part = dot(k, coeffs[at : at + width, :], 1, 0)
         total = part if total is None else total + part
     pred[...] = total
@@ -87,13 +82,12 @@
             grid=(1,),
             in_specs=[pl.BlockSpec((D, n), lambda i, half: (0, half[0]))]
             + (
-                [pl.BlockSpec((D, m), whole), pl.BlockSpec(memory_space=pl.ANY)]
+                [pl.BlockSpec((D, m), whole), pl.BlockSpec((m, labels), whole)]
                 if first
                 else [vmem, vmem]
             ),
             out_specs=[vmem, pl.BlockSpec((n, labels), lambda i, half: (0, 0))]
             + ([vmem, vmem] if first else []),
-            scratch_shapes=[pltpu.SemaphoreType.DMA] if first else [],
         ),
         out_shape=outs,
         compiler_params=pltpu.CompilerParams(vmem_limit_bytes=20 << 20),
@@ -447,7 +441,7 @@
     scaling = 1.0 / math.sqrt(n * samp)
     grad = arrived.astype(f32).sum(axis=0) * scaling + ridge_weight * own_coeffs.astype(f32)
 
-    messages = offset_messages(grad, suffix_proj, transfer, 2 * chips)
+    messages = offset_messages(grad, suffix_proj, in_hbm(transfer), 2 * chips)
     messages = lax.all_to_all(messages, ("z", "c"), 0, 0, tiled=True)
     solved = local_solve(grad, diag_inv, proj, step, side)
     direction = finish(place, messages, solved, side_prefix)

time: 125 us -> 124 us (level)
    unnamed x19 -> x17, local copies, waits for them, and re-layouts: 3.93 us -> 3.17 us
  transfers between devices with their start and end apart: 4 -> 4, of which waited for: 2 -> 2; matrix products, arithmetic and copies ran while one was open for 1% -> 1% of each run, Pallas kernels for 21% -> 22%
where the time goes in v7:
time: 124 us; the launch traced here: 123 us
  blocking collectives  53.8 us (43%)
  Pallas kernels  41.7 us (34%)
  starting transfers between devices  15.9 us (13%)
  waiting for transfers between devices  4.35 us (4%)
  local copies, waits for them, and re-layouts  3.61 us (3%)
  other arithmetic  3.58 us (3%)
    all_to_all x1, blocking collectives, sent_to_all(): return lax.all_to_all(copies, axis, split_axis=0, concat_axis=0, tiled=True)  20.5 us
    all_to_all x1, blocking collectives, body(): arrived = lax.all_to_all(pair_sum, 'z', 0, 0, tiled=True)  18.6 us
    all_to_all x1, blocking collectives, body(): lax.all_to_all(resid, 'z', 0, 0, tiled=True).reshape(n // 2, labels)  14.6 us
    pallas_call x2, Pallas kernels, predict(): pl.pallas_call(functools.partial(predict_kernel, width), grid_spec=pltpu....  11.9 us
    pallas_call x1, Pallas kernels, prepare(): pl.pallas_call(functools.partial(prepare_kernel, last), grid_spec=pltpu.P...  10.3 us
    pallas_call x1, Pallas kernels, local_solve(): pl.pallas_call(local_kernel, grid=(count,), in_specs=[pl.BlockSpec((label...  7.55 us
    all_to_all x1, starting transfers between devices, body(): arrived = lax.all_to_all(sent, 'samp', 0, 0, tiled=True)  6.82 us
    all_to_all x1, starting transfers between devices, body(): messages = lax.all_to_all(messages, ('z', 'c'), 0, 0, tiled=True)  5.2 us
  transfers between devices with their start and end apart: 4, of which 2 were waited for; matrix products, arithmetic and copies ran while one was open for 1% of the time, Pallas kernels for 22%

profile of v7, /device:TPU:1, one launch (start us, length us, event | category | flops | bytes accessed | tf_op | source)
XLA Modules:
  0.0 123.1 jit_solution(13001169153936823641)
XLA Ops:
  0.0 6.3 %predict.2 = (bf16[1024,4096]{1,0:T(8,128)(2,1)S(1)}, f32[1024,128]{1,0:T(8,128)S(1)}, bf16[72,4096]{1,0:T(8,128)(2,1)S(1)}, bf16[4096,128]{1,0:T(8,128)(2,1)S(1)}) custom-call(s32[1]{0:T(128)} %bitcast.4.half, bf16[64,2048]{1,0:T(8,128)(2,1)} %bitcast.25, bf16[64,4096]{1,0:T(8,128)(2,1)} %bitcast.24, bf16[4096,128]{1,0:T(8,128)(2,1)} %coeffs.1), custom_call_target="tpu_custom_call" | custom-call | flops 1610612736 | bytes 8388608 | tf_op jit(solution)/shard_map/predict/pallas_call | solution.py:78
  6.3 3.3 %collective-permute-start = (f32[1024,128]{1,0:T(8,128)S(1)}, f32[1024,128]{1,0:T(8,128)S(1)}, u32[]{:S(2)}, u32[]{:S(2)}) collective-permute-start(f32[1024,128]{1,0:T(8,128)S(1)} %get-tuple-element.34), channel_id=1, source_target_pairs={{0,1},{1,0},{2,3},{3,2},{4,5},{5,4},{6,7},{7,6},{8,9},{9,8},{10,11... | collective-permute-start | bytes 1572872 | tf_op jit(solution)/shard_map/ppermute | solution.py:398
  9.6 5.6 %predict.3 = (bf16[1024,4096]{1,0:T(8,128)(2,1)S(1)}, f32[1024,128]{1,0:T(8,128)S(1)}) custom-call(s32[1]{0:T(128)} %bitcast.2.half, bf16[64,2048]{1,0:T(8,128)(2,1)} %bitcast.26, bf16[72,4096]{1,0:T(8,128)(2,1)S(1)} %get-tuple-element.31.centers, bf16[4096,128]{1,0:T(8,128)(2,1)S(1)} %get-tuple-element.32.coeffs), custom_call_target="tpu_custom_call" | custom-call | flops 1610612736 | bytes 8388608 | tf_op jit(solution)/shard_map/predict/pallas_call | solution.py:78
  15.2 0.0 collective-permute-done
  15.2 0.1 add_convert_fusion
  15.3 18.6 %all_to_all.25 = f16[8,128,128]{2,1,0:T(8,128)(2,1)S(1)} all-to-all(f16[8,128,128]{2,1,0:T(8,128)(2,1)S(1)} %bitcast.23), channel_id=1, replica_groups=mesh['samp'=16,'z'=8,'c'=2] {'z'}, dimensions={0} | all-to-all | bytes 524288 | tf_op jit(solution)/shard_map/all_to_all | solution.py:418
  34.0 0.8 residual.1
  34.8 14.6 %all_to_all.26 = bf16[8,128,128]{2,1,0:T(8,128)(2,1)S(1)} all-to-all(bf16[8,128,128]{2,1,0:T(8,128)(2,1)S(1)} %residual.1), channel_id=1, replica_groups=mesh['samp'=16,'z'=8,'c'=2] {'z'}, dimensions={0} | all-to-all | bytes 524288 | tf_op jit(solution)/shard_map/all_to_all | solution.py:421
  49.4 0.6 collective-permute-start.1
  50.0 1.6 %gradient.2.refs_0_ = f32[128,4096]{1,0:T(8,128)S(1)} custom-call(bf16[1024,128]{1,0:T(8,128)(2,1)S(1)} %bitcast.19, bf16[1024,4096]{1,0:T(8,128)(2,1)S(1)} %get-tuple-element.36.rows), custom_call_target="tpu_custom_call" | custom-call | flops 1073741824 | bytes 8388608 | tf_op jit(solution)/shard_map/gradient/pallas_call | solution.py:143
  51.6 0.0 collective-permute-done.1.resid
  51.6 1.6 %gradient.3 = f32[128,4096]{1,0:T(8,128)S(1)} custom-call(bf16[1024,128]{1,0:T(8,128)(2,1)S(1)} %collective-permute-done.1.resid, bf16[1024,4096]{1,0:T(8,128)(2,1)S(1)} %get-tuple-element.35.rows, f32[128,4096]{1,0:T(8,128)S(1)} %gradient.2.refs_0_), custom_call_target="tpu_custom_call" | custom-call | flops 1073741824 | bytes 8388608 | tf_op jit(solution)/shard_map/gradient/pallas_call | solution.py:143
  53.3 0.0 copy-start.7
  53.3 1.1 convert_bitcast_fusion
  54.4 6.8 %all-to-all-start.2 = ((f16[16,8,4096]{2,1,0:T(8,128)(2,1)}), f16[16,8,4096]{2,1,0:T(8,128)(2,1)}, u32[]{:S(2)}, u32[]{:S(2)}) async-start(f16[16,8,4096]{2,1,0:T(8,128)(2,1)} %convert_bitcast_fusion), calls=%async_computation.2 | async-start | bytes 2097152 | tf_op jit(solution)/shard_map/all_to_all | solution.py:429
  61.2 0.0 copy-start.2
  61.2 0.0 copy-start.3
  61.2 0.0 copy-start.5
  61.2 0.0 copy-start.6
  61.2 0.0 copy-done.7
  61.3 0.4 constant_dynamic-slice_fusion
  61.6 1.0 copy.11
  62.6 0.0 copy-done.2
  62.6 0.0 copy-done.3
  62.6 0.0 copy-done.5
  62.6 0.0 copy-done.6
  62.6 10.3 %prepare.1 = (f32[64,4096]{1,0:T(8,128)S(1)}, f32[8,64,64]{2,1,0:T(8,128)S(1)}, f32[64,4096]{1,0:T(8,128)S(1)}, f32[64,4096]{1,0:T(8,128)S(1)}, f32[64,64]{1,0:T(8,128)S(1)}) custom-call(s32[8]{0:T(128)S(1)} %copy-done.6, f32[8,512,512]{2,1,0:T(8,128)} %inverse.3, bf16[8,64,512]{2,1,0:T(8,128)(2,1)S(1)} %bitcast.20, bf16[8,64,512]{2,1,0:T(8,128)(2,1)S(1)} %bitcast.21, ...), custom_call_target="tpu_custom_call" | custom-call | flops 1073741824 | bytes 12582912 | tf_op jit(solution)/shard_map/prepare/pallas_call | solution.py:192
  72.9 0.0 copy-start
  72.9 1.0 copy-done
  73.9 0.0 copy-start.4
  73.9 1.4 %prefix.1.side = f32[64,4096]{1,0:T(8,128)S(1)} custom-call(f32[8,64,64]{2,1,0:T(8,128)S(1)} %get-tuple-element.48.step, f32[64,4096]{1,0:T(8,128)S(1)} %get-tuple-element.49.side), custom_call_target="tpu_custom_call" | custom-call | flops 100663296 | bytes 2097152 | tf_op jit(solution)/shard_map/prefix/pallas_call | solution.py:241
  75.3 2.9 %all-to-all-done.2 = f16[16,8,4096]{2,1,0:T(8,128)(2,1)} async-done(((f16[16,8,4096]{2,1,0:T(8,128)(2,1)}), f16[16,8,4096]{2,1,0:T(8,128)(2,1)}, u32[]{:S(2)}, u32[]{:S(2)}) %all-to-all-start.2) | async-done | bytes 1048608 | tf_op jit(solution)/shard_map/all_to_all | solution.py:429
  78.1 0.0 copy-done.4
  78.1 1.4 %convert_reduce_fusion = f32[8,4096]{1,0:T(8,128)S(1)} fusion(f16[16,8,4096]{2,1,0:T(8,128)(2,1)} %all-to-all-done.2), kind=kLoop, calls=%fused_computation | loop fusion | flops 1015808 | bytes 1179648 | tf_op jit(solution)/shard_map/reduce_sum | solution.py:442
  79.5 0.9 bitcast_add_fusion.grad
  80.4 2.0 %offset.1 = bf16[16,48,128]{2,1,0:T(8,128)(2,1)} custom-call(f32[8,4096]{1,0:T(8,128)S(1)} %bitcast_add_fusion.grad, f32[64,4096]{1,0:T(8,128)S(1)} %get-tuple-element.45.suffix_proj, f32[64,64]{1,0:T(8,128)} %copy-done.4), custom_call_target="tpu_custom_call" | custom-call | tf_op jit(solution)/shard_map/offset/pallas_call | solution.py:268
  82.4 5.2 %all-to-all-start.3 = ((bf16[16,48,128]{2,1,0:T(8,128)(2,1)}), bf16[16,48,128]{2,1,0:T(8,128)(2,1)S(1)}, u32[]{:S(2)}, u32[]{:S(2)}) async-start(bf16[16,48,128]{2,1,0:T(8,128)(2,1)} %offset.1), calls=%async_computation.3 | async-start | bytes 393216 | tf_op jit(solution)/shard_map/all_to_all | solution.py:445
  87.6 0.0 copy-start.1
  87.6 1.2 copy-done.1
  88.8 7.6 %local_solve.1.solved = f32[8,4096]{1,0:T(8,128)S(1)} custom-call(f32[8,4096]{1,0:T(8,128)S(1)} %bitcast_add_fusion.grad, f32[8,512,512]{2,1,0:T(8,128)} %inverse.3, f32[64,4096]{1,0:T(8,128)S(1)} %copy-done.1, f32[8,64,64]{2,1,0:T(8,128)S(1)} %get-tuple-element.48.step, f32[64,4096]{1,0:T(8,128)S(1)} %get-tuple-element.49.side), custom_call_target="tpu_custom_call" | custom-call | flops 100663296 | bytes 8388608 | tf_op jit(solution)/shard_map/local_solve/pallas_call | solution.py:299
  96.4 1.5 %all-to-all-done.3.messages = bf16[16,48,128]{2,1,0:T(8,128)(2,1)S(1)} async-done(((bf16[16,48,128]{2,1,0:T(8,128)(2,1)}), bf16[16,48,128]{2,1,0:T(8,128)(2,1)S(1)}, u32[]{:S(2)}, u32[]{:S(2)}) %all-to-all-start.3) | async-done | bytes 196640 | tf_op jit(solution)/shard_map/all_to_all | solution.py:445
  97.9 1.8 %finish.1 = f32[8,4224]{1,0:T(8,128)S(1)} custom-call(s32[1]{0:T(128)} %bitcast.place, bf16[16,48,128]{2,1,0:T(8,128)(2,1)S(1)} %all-to-all-done.3.messages, f32[8,4096]{1,0:T(8,128)S(1)} %local_solve.1.solved, f32[64,4096]{1,0:T(8,128)S(1)} %prefix.1.side), custom_call_target="tpu_custom_call" | custom-call | tf_op jit(solution)/shard_map/finish/pallas_call | solution.py:357
  99.7 0.1 broadcast_in_dim.7
  99.8 20.5 %all_to_all.27 = f16[16,8,4224]{2,1,0:T(8,128)(2,1)S(1)} all-to-all(f16[16,8,4224]{2,1,0:T(8,128)(2,1)S(1)} %broadcast_in_dim.7), channel_id=1, replica_groups=mesh['samp'=16,'z'=8,'c'=2] {'samp'}, dimensions={0} | all-to-all | bytes 2162688 | tf_op jit(solution)/shard_map/all_to_all | solution.py:394
  120.3 0.1 bitcast_convert_fusion.powers.scaled
  120.5 2.7 %unscaled.1 = f32[4096,128]{1,0:T(8,128)} custom-call(f32[128,4224]{1,0:T(8,128)S(1)} %bitcast_convert_fusion.powers.scaled, f32[128,4224]{1,0:T(8,128)S(1)} %bitcast_convert_fusion.powers.scaled), custom_call_target="tpu_custom_call" | custom-call | tf_op jit(solution)/shard_map/unscaled/pallas_call | solution.py:378
  (2 shorter events, 0.0 us)
Async XLA Ops:
  6.3 8.9 %collective-permute-start = (f32[1024,128]{1,0:T(8,128)S(1)}, f32[1024,128]{1,0:T(8,128)S(1)}, u32[]{:S(2)}, u32[]{:S(2)}) collective-permute-start(f32[1024,128]{1,0:T(8,128)S(1)} %get-tuple-element.34), channel_id=1, source_target_pairs={{0,1},{1,0},{2,3},{3,2},{4,5},{5,4},{6,7},{7,6},{8,9},{9,8},{10,11... | collective-permute-start | bytes 1572872 | tf_op jit(solution)/shard_map/ppermute | solution.py:398
  49.4 2.2 %collective-permute-start.1 = (bf16[1024,128]{1,0:T(8,128)(2,1)S(1)}, bf16[1024,128]{1,0:T(8,128)(2,1)S(1)}, u32[]{:S(2)}, u32[]{:S(2)}) collective-permute-start(bf16[1024,128]{1,0:T(8,128)(2,1)S(1)} %bitcast.18), channel_id=1, source_target_pairs={{0,1},{1,0},{2,3},{3,2},{4,5},{5,4},{6,7},{7,6},{8,9},{9,8},{10,11... | collective-permute-start | bytes 786440 | tf_op jit(solution)/shard_map/ppermute | solution.py:398
  53.3 8.0 %copy-start.7 = (bf16[4096,128]{1,0:T(8,128)(2,1)S(1)}, bf16[4096,128]{1,0:T(8,128)(2,1)}, u32[]{:S(2)}) copy-start(bf16[4096,128]{1,0:T(8,128)(2,1)} %coeffs.1) | copy-start | bytes 3145732
  54.4 23.8 %all-to-all-start.2 = ((f16[16,8,4096]{2,1,0:T(8,128)(2,1)}), f16[16,8,4096]{2,1,0:T(8,128)(2,1)}, u32[]{:S(2)}, u32[]{:S(2)}) async-start(f16[16,8,4096]{2,1,0:T(8,128)(2,1)} %convert_bitcast_fusion), calls=%async_computation.2 | async-start | bytes 2097152 | tf_op jit(solution)/shard_map/all_to_all | solution.py:429
  61.2 1.4 %copy-start.2 = (bf16[8,512,64]{1,2,0:T(8,128)(2,1)S(1)}, bf16[8,512,64]{1,2,0:T(8,128)(2,1)}, u32[]{:S(2)}) copy-start(bf16[8,512,64]{1,2,0:T(8,128)(2,1)} %param.14) | copy-start | bytes 1572868
  61.2 1.4 %copy-start.3 = (bf16[8,512,64]{1,2,0:T(8,128)(2,1)S(1)}, bf16[8,512,64]{1,2,0:T(8,128)(2,1)}, u32[]{:S(2)}) copy-start(bf16[8,512,64]{1,2,0:T(8,128)(2,1)} %param.15) | copy-start | bytes 1572868
  61.2 1.4 %copy-start.5 = (f32[8,64]{1,0:T(8,128)S(1)}, f32[8,64]{1,0:T(8,128)}, u32[]{:S(2)}) copy-start(f32[8,64]{1,0:T(8,128)} %param.16) | copy-start | bytes 6148
  61.2 1.3 %copy-start.6 = (s32[8]{0:T(128)S(1)}, s32[8]{0:T(128)}, u32[]{:S(2)}) copy-start(s32[8]{0:T(128)} %ranks) | copy-start | bytes 100
  72.9 1.0 copy-start
  73.9 4.3 %copy-start.4 = (f32[64,64]{1,0:T(8,128)}, f32[64,64]{1,0:T(8,128)S(1)}, u32[]{:S(2)}) copy-start(f32[64,64]{1,0:T(8,128)S(1)} %get-tuple-element.46.transfer) | copy-start | bytes 49156
  82.4 15.5 %all-to-all-start.3 = ((bf16[16,48,128]{2,1,0:T(8,128)(2,1)}), bf16[16,48,128]{2,1,0:T(8,128)(2,1)S(1)}, u32[]{:S(2)}, u32[]{:S(2)}) async-start(bf16[16,48,128]{2,1,0:T(8,128)(2,1)} %offset.1), calls=%async_computation.3 | async-start | bytes 393216 | tf_op jit(solution)/shard_map/all_to_all | solution.py:445
  87.6 1.2 copy-start.1
